TPU v7x, 256 devices: a whole 4x4x8 slice. The times are simulated.
256 devices in a mesh: row: 32 (over x, y, core), col: 8 (over z).
Axes of the slice: x: 4, y: 4, z: 8, core: 2. Of those that a mesh axis runs over, the one named last changes fastest.
Arguments:
- tile_values: bfloat16 [24576, 256, 256], P(('row', 'col')), may hold values from -0.375 to 0.375
- tile_coords: int32 [24576, 2], P(('row', 'col')), may hold values from 0 to 15, as said below
- live_counts: int32 [256], P(('row', 'col')), may hold values from 24 to 96, as said below
Outputs:
- range_basis: float32 [131072, 192], P(('row', 'col'))
- projected: float32 [8, 4096, 192], P('col', 'row')
Inputs may be any that keep to these rules, and one draw needn't show every extreme that they name: `tile_coords`: for each device, column 0 is below 16, column 1 is below 16, and the 96 positions of its slots are distinct. `live_counts`: some device has all 96 slots live.
All inputs are finite; a program needn't handle non-finite values.
Results may differ from a plain program's by a relative error of at most 0.0003.
Values sent between devices are 32-bit elements; how exact they have to be, the bound alone decides.
No kernel may reach another device: no remote copies, remote signals or barrier semaphores. Data moves between devices by JAX's collectives and lax.ppermute only.
A program may use at most 128 MiB of HBM per device.

v0:
```python
import functools
import math

import jax
import jax.numpy as jnp
from jax import lax
from jax.experimental import pallas as pl
from jax.experimental.pallas import tpu as pltpu
from jax.sharding import Mesh
from jax.sharding import PartitionSpec as P

TB = 256
K = 192
RT = 16
CT = 16
NT = 96
NZ = 8
KH = K // 2
CH = RT * TB // NZ
SLOTS = 8
UNROLL = 4
STEPS = NT // SLOTS
HIGHEST = lax.Precision.HIGHEST


def dot_nt(a, b, precision=None):
    return lax.dot_general(
        a, b, (((1,), (1,)), ((), ())), precision=precision, preferred_element_type=jnp.float32
    )


def dot_nn(a, b, precision=None):
    return lax.dot_general(
        a, b, (((1,), (0,)), ((), ())), precision=precision, preferred_element_type=jnp.float32
    )


SMEM_SPEC = pl.BlockSpec(memory_space=pltpu.SMEM)
VMEM_SPEC = pl.BlockSpec(memory_space=pltpu.VMEM)
HBM_SPEC = pl.BlockSpec(memory_space=pltpu.HBM)


def sketch_body(meta_ref, live_ref, pos_ref, tiles_ref, *refs):
    outs = refs[: 2 * NZ]
    omega_ref, acc_ref, buf_ref, sems = refs[2 * NZ :]
    steps = (live_ref[0] + SLOTS - 1) >> 3

    def copy(step):
        return pltpu.make_async_copy(
            tiles_ref.at[pl.ds(step * SLOTS, SLOTS)],
            buf_ref.at[pl.ds(step * SLOTS, SLOTS)],
            sems.at[step],
        )

    def fetch(step, carry):
        copy(step).start()
        return carry

    lax.fori_loop(0, steps, fetch, 0)
    k_ids = lax.broadcasted_iota(jnp.int32, (K, TB), 0)
    g_ids = lax.broadcasted_iota(jnp.int32, (K, TB), 1)
    base = g_ids * K + k_ids
    z = pos_ref[0]

    def fill(j, carry):
        h = base + (z * CT + j) * (TB * K)
        h = h * 747796405 + 1442695040
        h = h ^ (h >> 15)
        h = h * 1103515245 + 12345
        h = h ^ (h >> 13)
        omega_ref[j] = (1 - 2 * ((h >> 9) & 1)).astype(jnp.float32).astype(jnp.bfloat16)
        acc_ref[j] = jnp.zeros((K, TB), jnp.float32)
        return carry

    lax.fori_loop(0, CT, fill, 0)

    def work(step, carry):
        copy(step).wait()
        for t in range(SLOTS):
            slot = step * SLOTS + t
            code = meta_ref[slot]
            acc_ref[code >> 4] += dot_nt(omega_ref[code & 15], buf_ref[slot])
        return carry

    lax.fori_loop(0, steps, work, 0)
    for d in range(NZ):
        for half in range(2):
            for e in range(2):
                outs[half * NZ + d][:, e * TB : (e + 1) * TB] = acc_ref[
                    2 * d + e, half * KH : (half + 1) * KH, :
                ]


def sketch_call(meta, live, pos, tiles):
    return pl.pallas_call(
        sketch_body,
        name="sketch",
        in_specs=[SMEM_SPEC, SMEM_SPEC, SMEM_SPEC, HBM_SPEC],
        out_specs=[VMEM_SPEC] * (2 * NZ),
        scratch_shapes=[
            pltpu.VMEM((CT, K, TB), jnp.bfloat16),
            pltpu.VMEM((RT + 1, K, TB), jnp.float32),
            pltpu.VMEM((NT, TB, TB), jnp.bfloat16),
            pltpu.SemaphoreType.DMA((STEPS,)),
        ],
        out_shape=[jax.ShapeDtypeStruct((KH, CH), jnp.float32)] * (2 * NZ),
        compiler_params=pltpu.CompilerParams(vmem_limit_bytes=24 << 20),
    )(meta, live, pos, tiles)


NEAR = (0, 1, 2, 6, 7)
FAR = (3, 4, 5)


def split_body(*refs, n, last):
    chunks = refs[: 2 * n]
    split_ref, gram_ref, sum_ref = refs[-3:]

    for c in range(n):
        for half in range(2):
            chunk = chunks[half * n + c]

            def part(g, carry):
                rows = pl.ds(pl.multiple_of(g * 32, 32), 32)
                at = pl.multiple_of(half * KH + g * 32, 32)
                full = chunk[rows, :]
                high = full.astype(jnp.bfloat16)
                low = (full - high.astype(jnp.float32)).astype(jnp.bfloat16)
                for e in range(2):
                    cols = slice(e * TB, (e + 1) * TB)
                    split_ref[2 * c + e, pl.ds(at, 32), :] = high[:, cols]
                    split_ref[2 * c + e, pl.ds(K + at, 32), :] = low[:, cols]
                return carry

            lax.fori_loop(0, KH // 32, part, 0)
    sum_ref[...] = jnp.zeros((2 * K, K), jnp.float32)

    def square(i, carry):
        sum_ref[...] += dot_nt(split_ref[i], split_ref[i, :K, :])
        return carry

    lax.fori_loop(0, 2 * n, square, 0)
    cross = sum_ref[K:, :]
    gram = sum_ref[:K, :] + (cross + cross.T)
    if last:
        gram = refs[2 * n][...] + gram
        for row, col, (i, j) in PACKED:
            gram_ref[row : row + NB, col : col + NB] = gram[i : i + NB, j : j + NB]
    else:
        gram_ref[...] = gram


NB = 64
PACKED = (
    (0, 0, (0, 0)),
    (0, NB, (NB, 0)),
    (NB, 0, (2 * NB, 0)),
    (NB, NB, (NB, NB)),
    (2 * NB, 0, (2 * NB, 2 * NB)),
    (2 * NB, NB, (2 * NB, NB)),
)


def split_call(chunks, carried=()):
    n = len(chunks) // 2
    return pl.pallas_call(
        functools.partial(split_body, n=n, last=bool(carried)),
        name="split_far" if carried else "split_near",
        in_specs=[VMEM_SPEC] * (len(chunks) + len(carried)),
        out_specs=[VMEM_SPEC] * 2,
        scratch_shapes=[pltpu.VMEM((2 * K, K), jnp.float32)],
        out_shape=[
            jax.ShapeDtypeStruct((2 * n, 2 * K, TB), jnp.bfloat16),
            jax.ShapeDtypeStruct((K, 2 * NB) if carried else (K, K), jnp.float32),
        ],
        compiler_params=pltpu.CompilerParams(vmem_limit_bytes=8 << 20),
    )(*chunks, *carried)


def adjoint_body(order_ref, meta_ref, count_ref, pos_ref, tiles_ref, split_ref, *refs, dists, last):
    if last:
        acc_in, keep_ref, give_ref = refs[:3]
    else:
        acc_out = refs[0]
    acc_ref, buf_ref, sems = refs[-3:]
    first = count_ref[0] if last else 0
    total = count_ref[1] if last else count_ref[0]
    steps = (total + UNROLL - 1) >> 2
    core = pos_ref[1]

    def copy(step, t):
        rank = step * UNROLL + t
        slot = order_ref[jnp.minimum(first + rank, NT - 1)]
        return pltpu.make_async_copy(tiles_ref.at[slot], buf_ref.at[rank], sems.at[step])

    def fetch(step, carry):
        for t in range(UNROLL):
            copy(step, t).start()
        return carry

    lax.fori_loop(0, steps, fetch, 0)

    def clear(j, carry):
        acc_ref[j] = acc_in[j] if last else jnp.zeros((K, TB), jnp.float32)
        return carry

    lax.fori_loop(0, CT, clear, 0)

    def work(step, carry):
        for t in range(UNROLL):
            copy(step, t).wait()
        for t in range(UNROLL):
            rank = step * UNROLL + t
            code = meta_ref[order_ref[jnp.minimum(first + rank, NT - 1)]]
            i = place_of((code >> 4) & 15, dists)
            j = jnp.where(rank < total, code & 15, CT)
            part = dot_nn(split_ref[i], buf_ref[rank])
            acc_ref[j] += part[:K] + part[K:]
        return carry

    lax.fori_loop(0, steps, work, 0)
    if last:
        mine = pl.multiple_of(core * 128, 128)
        other = pl.multiple_of((1 - core) * 128, 128)

        def place(q, carry):
            one = q >> 2
            two = q & 3
            swap = core == 1
            own = chip_of(pos_ref, jnp.where(swap, two, one), jnp.where(swap, one, two))
            far = chip_of(pos_ref, jnp.where(swap, one, two), jnp.where(swap, two, one))
            keep_ref[q] = acc_ref[own, :, pl.ds(mine, 128)]
            give_ref[q] = acc_ref[far, :, pl.ds(other, 128)]
            return carry

        lax.fori_loop(0, CT, place, 0)
    else:

        def save(j, carry):
            acc_out[j] = acc_ref[j]
            return carry

        lax.fori_loop(0, CT, save, 0)


def place_of(i, dists):
    if dists == FAR:
        return jnp.clip(i - 2 * FAR[0], 0, 2 * len(FAR) - 1)
    return jnp.clip(jnp.where(i >= 12, i - 6, i), 0, 2 * len(NEAR) - 1)


def chip_of(pos_ref, dx, dy):
    return ((pos_ref[2] + dx) & 3) * 4 + ((pos_ref[3] + dy) & 3)


def adjoint_call(order, meta, count, pos, tiles, split, dists, carried=()):
    last = bool(carried)
    part = (CT, K, 128)
    outs = [part, part] if last else [(CT, K, TB)]
    return pl.pallas_call(
        functools.partial(adjoint_body, dists=dists, last=last),
        name="adjoint_far" if last else "adjoint_near",
        in_specs=[SMEM_SPEC] * 4 + [HBM_SPEC] + [VMEM_SPEC] * (1 + len(carried)),
        out_specs=[VMEM_SPEC] * len(outs),
        scratch_shapes=[
            pltpu.VMEM((CT + 1, K, TB), jnp.float32),
            pltpu.VMEM((NT, TB, TB), jnp.bfloat16),
            pltpu.SemaphoreType.DMA((NT // UNROLL,)),
        ],
        out_shape=[jax.ShapeDtypeStruct(o, jnp.float32) for o in outs],
        compiler_params=pltpu.CompilerParams(vmem_limit_bytes=24 << 20),
    )(order, meta, count, pos, tiles, split, *carried)


def inverse_factor(block, rows_ref):
    eye = (
        lax.broadcasted_iota(jnp.int32, (NB, NB), 0) == lax.broadcasted_iota(jnp.int32, (NB, NB), 1)
    ).astype(jnp.float32)
    work = jnp.concatenate([eye, block], axis=1)
    first = 0
    for k in range(0, NB, 2):
        o = k - first
        rows = NB - first
        a = jnp.broadcast_to(work[:, NB + k : NB + k + 1], (rows, 2 * NB))
        b = jnp.broadcast_to(work[:, NB + k + 1 : NB + k + 2], (rows, 2 * NB))
        p = a[o : o + 1]
        q = a[o + 1 : o + 2]
        r = b[o + 1 : o + 2]
        r0 = work[o : o + 1]
        r1 = work[o + 1 : o + 2]
        inv = 1.0 / (p * r - q * q)
        u0 = (r * r0 - q * r1) * inv
        u1 = (p * r1 - q * r0) * inv
        rows_ref[k : k + 1, :] = r0 * lax.rsqrt(p)
        ratio = q / p
        rows_ref[k + 1 : k + 2, :] = (r1 - ratio * r0) * lax.rsqrt(r - ratio * q)
        if k + 2 == NB:
            break
        skip = (k + 2) // 8 * 8 - first
        if skip:
            work, a, b = work[skip:], a[skip:], b[skip:]
            first += skip
        if (k + 2) % 8:
            below = lax.broadcasted_iota(jnp.int32, a.shape, 0) >= k + 2 - first
            a = jnp.where(below, a, 0.0)
            b = jnp.where(below, b, 0.0)
        work = work - (a * u0 + b * u1)
    return rows_ref[:, :NB]


def factor_body(packed_ref, out_ref, gram_ref, rows_ref, panel_ref, *, scale):
    n = NB
    for row, col, (i, j) in PACKED:
        block = packed_ref[row : row + n, col : col + n]
        gram_ref[i : i + n, j : j + n] = block
        if i == 2 * n and j == n:
            gram_ref[j : j + n, i : i + n] = block.T
    rows_ref[3, :, :n] = gram_ref[:n, :n]
    out_ref[...] = jnp.zeros((K, K), jnp.float32)

    def block(b, carry):
        w = inverse_factor(rows_ref[3, :, :n], rows_ref.at[b])

        @pl.when(b == 0)
        def _():
            panel = dot_nt(gram_ref[n:, :n], w, HIGHEST)
            panel_ref[...] = panel
            trail = gram_ref[n:, n:] - dot_nt(panel, panel, HIGHEST)
            gram_ref[n:, n:] = trail
            rows_ref[3] = trail[:n]

        @pl.when(b == 1)
        def _():
            l21 = dot_nt(gram_ref[2 * n :, n : 2 * n], w, HIGHEST)
            gram_ref[2 * n :, :n] = l21
            rows_ref[3, :, :n] = gram_ref[2 * n :, 2 * n :] - dot_nt(l21, l21, HIGHEST)

        return carry

    lax.fori_loop(0, 3, block, 0)
    w0, w1, w2 = (rows_ref[b, :, :n] for b in range(3))
    panel = panel_ref[...]
    l21 = gram_ref[2 * n :, :n]
    x10 = -dot_nn(w1, dot_nn(panel[:n], w0, HIGHEST), HIGHEST)
    x21 = -dot_nn(w2, dot_nn(l21, w1, HIGHEST), HIGHEST)
    x20 = -dot_nn(w2, dot_nn(panel[n:], w0, HIGHEST) + dot_nn(l21, x10, HIGHEST), HIGHEST)
    out_ref[:n, :n] = w0 * scale
    out_ref[n : 2 * n, :n] = x10 * scale
    out_ref[n : 2 * n, n : 2 * n] = w1 * scale
    out_ref[2 * n :, :n] = x20 * scale
    out_ref[2 * n :, n : 2 * n] = x21 * scale
    out_ref[2 * n :, 2 * n :] = w2 * scale


def factor_call(packed, scale):
    return pl.pallas_call(
        functools.partial(factor_body, scale=scale),
        name="factor",
        in_specs=[VMEM_SPEC],
        out_specs=VMEM_SPEC,
        scratch_shapes=[
            pltpu.VMEM((K, K), jnp.float32),
            pltpu.VMEM((4, NB, 2 * NB), jnp.float32),
            pltpu.VMEM((2 * NB, NB), jnp.float32),
        ],
        out_shape=jax.ShapeDtypeStruct((K, K), jnp.float32),
        compiler_params=pltpu.CompilerParams(vmem_limit_bytes=4 << 20),
    )(packed)


def apply_body(factor_ref, *refs):
    out_ref = refs[-1]
    both = jnp.concatenate([r[...] for r in refs[:-1]], axis=0)
    out_ref[...] = dot_nn(factor_ref[...], both, HIGHEST)


def apply_call(factor, parts):
    return pl.pallas_call(
        apply_body,
        in_specs=[VMEM_SPEC] * (1 + len(parts)),
        out_specs=VMEM_SPEC,
        out_shape=jax.ShapeDtypeStruct((K, parts[0].shape[1]), jnp.float32),
        compiler_params=pltpu.CompilerParams(vmem_limit_bytes=4 << 20),
    )(factor, *parts)


def shift(x, axis, size, by):
    return lax.ppermute(x, axis, [(i, (i + by) % size) for i in range(size)])


def reduce_z(parts):
    chains = []
    for half, part in enumerate(parts):
        up, down = (4, 3) if half == 0 else (3, 4)
        chains.append([part[up], part[NZ - down], up, down])
    for _ in range(4):
        for chain, part in zip(chains, parts):
            if chain[2]:
                chain[0] = shift(chain[0], "z", NZ, 1)
                chain[2] -= 1
                if chain[2]:
                    chain[0] = chain[0] + part[chain[2]]
            if chain[3]:
                chain[1] = shift(chain[1], "z", NZ, -1)
                chain[3] -= 1
                if chain[3]:
                    chain[1] = chain[1] + part[NZ - chain[3]]
    return [chain[0] + chain[1] + part[0] for chain, part in zip(chains, parts)]


def gather_z(own):
    found = [[mine] + [None] * (NZ - 1) for mine in own]
    for step in range(1, 5):
        for half, got in enumerate(found):
            if step <= (4 if half == 0 else 3):
                got[NZ - step] = shift(got[(NZ - step + 1) % NZ], "z", NZ, 1)
            if step <= (3 if half == 0 else 4):
                got[step] = shift(got[step - 1], "z", NZ, -1)
    return found


def shift_xy(x, by, stage):
    pairs = []
    for i in range(32):
        px, py, core = i // 8, i // 2 % 4, i % 2
        if core == stage:
            px = (px + by) % 4
        else:
            py = (py + by) % 4
        pairs.append((i, (px * 4 + py) * 2 + core))
    return lax.ppermute(x, ("x", "y", "core"), pairs)


def exchange(blocks, stage):
    total = blocks[0]
    for d in (2, 1, 3):
        total = total + shift_xy(blocks[d], d, stage)
    return total


def per_device(tiles, tile_coords, live_counts):
    x, y, core, z = (lax.axis_index(name).astype(jnp.int32) for name in ("x", "y", "core", "z"))
    pos = jnp.stack([z, core, x, y])
    slots = jnp.arange(NT, dtype=jnp.int32)
    live = slots < live_counts[0]
    relative = (tile_coords[:, 0] - 2 * z) & (RT - 1)
    meta = jnp.where(live, relative, RT) * CT + tile_coords[:, 1]
    parts = sketch_call(meta, live_counts, pos, tiles)
    far = (relative >= 2 * FAR[0]) & (relative < 2 * FAR[-1] + 2)
    key = jnp.where(live, far.astype(jnp.int32), 2) * NT + slots
    rank = jnp.sum((key[:, None] > key[None, :]).astype(jnp.int32), axis=1)
    order = jnp.sum(jnp.where(rank[:, None] == slots[None, :], slots[:, None], 0), axis=0)
    count = jnp.stack([jnp.sum(live & ~far), jnp.sum(live & far)]).astype(jnp.int32)
    own = reduce_z([parts[:NZ], parts[NZ:]])
    found = gather_z(own)
    near = [got[d] for got in found for d in NEAR]
    near_split, near_gram = split_call(near)
    carried = adjoint_call(order, meta, count, pos, tiles, near_split, NEAR)
    rest = [got[d] for got in found for d in FAR]
    far_split, gram = split_call(rest, (near_gram,))
    gram = gram + shift(gram, "core", 2, 1)
    keep, give = adjoint_call(order, meta, count, pos, tiles, far_split, FAR, carried)
    gram = exchange([gram] * 4, 0)
    blocks = (keep + shift(give, "core", 2, 1)).reshape(4, 4, K, 128)
    gram = exchange([gram] * 4, 1)
    blocks = exchange([blocks[d] for d in range(4)], 0)
    block = exchange([blocks[d] for d in range(4)], 1)
    scale = math.sqrt(RT * TB * 32)
    factor = factor_call(gram, scale)
    range_basis = apply_call(factor, own)
    projected = apply_call(factor, [block])
    return range_basis.T, projected.T[None]


def solution(mesh):
    split = Mesh(mesh.devices.reshape(4, 4, 2, NZ), ("x", "y", "core", "z"))
    row = ("x", "y", "core")
    both = (*row, "z")
    in_specs = (P(both, None, None), P(both, None), P(both))
    out_specs = (P(both, None), P("z", row, None))
    return jax.shard_map(
        per_device, mesh=split, in_specs=in_specs, out_specs=out_specs, check_vma=False
    )
```

profile of v0, /device:TPU:2, one launch (start us, length us, event | category | flops | bytes accessed | tf_op | source)
XLA Modules:
  0.0 166.3 jit_solution(11764054690841908924)
XLA Ops:
  1.3 1.5 fusion.5
  2.8 4.6 %copy-done = bf16[96,256,256]{2,1,0:T(8,128)(2,1)S(1)} copy-done((bf16[96,256,256]{2,1,0:T(8,128)(2,1)S(1)}, bf16[96,256,256]{2,1,0:T(8,128)(2,1)}, u32[]{:S(2)}) %copy-start) | copy-done | bytes 12582936
  7.4 9.1 %sketch.1 = (f32[96,512]{1,0:T(8,128)S(1)}, f32[96,512]{1,0:T(8,128)S(1)}, f32[96,512]{1,0:T(8,128)S(1)}, f32[96,512]{1,0:T(8,128)S(1)}, f32[96,512]{1,0:T(8,128...) custom-call(s32[96]{0:T(128)S(1)} %get-tuple-element.55.meta_ref, ...), custom_call_target="tpu_custom_call" | custom-call | tf_op jit(solution)/shard_map/sketch/pallas_call | solution.py:95
  16.5 4.7 %collective-permute-start.17 = (f32[96,512]{1,0:T(8,128)S(1)}, f32[96,512]{1,0:T(8,128)S(1)}, u32[]{:S(2)}, u32[]{:S(2)}) collective-permute-start(f32[96,512]{1,0:T(8,128)S(1)} %get-tuple-element.35), channel_id=1, source_target_pairs={{0,7},{1,0},{2,1},{3,2},{4,3},{5,4},{6,5},{7,6},{8,15},{9,8},{10,9... | collective-permute-start | bytes 589832 | tf_op jit(solution)/shard_map/ppermute | solution.py:388
  21.3 3.2 %collective-permute-done.17 = f32[96,512]{1,0:T(8,128)S(1)} collective-permute-done((f32[96,512]{1,0:T(8,128)S(1)}, f32[96,512]{1,0:T(8,128)S(1)}, u32[]{:S(2)}, u32[]{:S(2)}) %collective-permute-start.17) | collective-permute-done | bytes 196640 | tf_op jit(solution)/shard_map/ppermute | solution.py:388
  24.5 3.8 %collective-permute-start.18 = (f32[96,512]{1,0:T(8,128)S(1)}, f32[96,512]{1,0:T(8,128)S(1)}, u32[]{:S(2)}, u32[]{:S(2)}) collective-permute-start(f32[96,512]{1,0:T(8,128)S(1)} %add.107), channel_id=1, source_target_pairs={{0,7},{1,0},{2,1},{3,2},{4,3},{5,4},{6,5},{7,6},{8,15},{9,8},{10,9... | collective-permute-start | bytes 589832 | tf_op jit(solution)/shard_map/ppermute | solution.py:388
  28.3 0.6 collective-permute-start.4
  28.9 1.3 collective-permute-done
  30.3 0.2 collective-permute-start.1
  30.4 1.9 %collective-permute-done.14 = f32[96,512]{1,0:T(8,128)S(1)} collective-permute-done((f32[96,512]{1,0:T(8,128)S(1)}, f32[96,512]{1,0:T(8,128)S(1)}, u32[]{:S(2)}, u32[]{:S(2)}) %collective-permute-start.14) | collective-permute-done | bytes 196640 | tf_op jit(solution)/shard_map/ppermute | solution.py:388
  32.4 0.1 collective-permute-start.15
  32.4 1.1 collective-permute-done.18
  33.6 3.8 %collective-permute-start.19 = (f32[96,512]{1,0:T(8,128)S(1)}, f32[96,512]{1,0:T(8,128)S(1)}, u32[]{:S(2)}, u32[]{:S(2)}) collective-permute-start(f32[96,512]{1,0:T(8,128)S(1)} %add.108), channel_id=1, source_target_pairs={{0,7},{1,0},{2,1},{3,2},{4,3},{5,4},{6,5},{7,6},{8,15},{9,8},{10,9... | collective-permute-start | bytes 589832 | tf_op jit(solution)/shard_map/ppermute | solution.py:388
  37.4 3.8 %collective-permute-start.5 = (f32[96,512]{1,0:T(8,128)S(1)}, f32[96,512]{1,0:T(8,128)S(1)}, u32[]{:S(2)}, u32[]{:S(2)}) collective-permute-start(f32[96,512]{1,0:T(8,128)S(1)} %add.101), channel_id=1, source_target_pairs={{0,7},{1,0},{2,1},{3,2},{4,3},{5,4},{6,5},{7,6},{8,15},{9,8},{10,9... | collective-permute-start | bytes 589832 | tf_op jit(solution)/shard_map/ppermute | solution.py:388
  41.2 0.1 collective-permute-start.2
  41.3 0.2 collective-permute-done.15
  41.5 0.1 collective-permute-start.16
  41.6 1.0 collective-permute-done.19
  42.7 3.7 %collective-permute-start.20 = (f32[96,512]{1,0:T(8,128)S(1)}, f32[96,512]{1,0:T(8,128)S(1)}, u32[]{:S(2)}, u32[]{:S(2)}) collective-permute-start(f32[96,512]{1,0:T(8,128)S(1)} %add.109), channel_id=1, source_target_pairs={{0,7},{1,0},{2,1},{3,2},{4,3},{5,4},{6,5},{7,6},{8,15},{9,8},{10,9... | collective-permute-start | bytes 589832 | tf_op jit(solution)/shard_map/ppermute | solution.py:388
  46.4 0.2 collective-permute-done.5
  46.6 3.8 %collective-permute-start.6 = (f32[96,512]{1,0:T(8,128)S(1)}, f32[96,512]{1,0:T(8,128)S(1)}, u32[]{:S(2)}, u32[]{:S(2)}) collective-permute-start(f32[96,512]{1,0:T(8,128)S(1)} %add.102), channel_id=1, source_target_pairs={{0,7},{1,0},{2,1},{3,2},{4,3},{5,4},{6,5},{7,6},{8,15},{9,8},{10,9... | collective-permute-start | bytes 589832 | tf_op jit(solution)/shard_map/ppermute | solution.py:388
  50.4 0.1 collective-permute-start.3
  50.5 0.8 collective-permute-done.20
  51.3 3.9 %collective-permute-start.21 = (f32[96,512]{1,0:T(8,128)S(1)}, f32[96,512]{1,0:T(8,128)S(1)}, u32[]{:S(2)}, u32[]{:S(2)}) collective-permute-start(f32[96,512]{1,0:T(8,128)S(1)} %add_add_fusion.refs_5_.refs_1_), channel_id=1, source_target_pairs={{0,7},{1,0},{2,1},{3,2},{4,3},{5,4},{6,5},{7,6},{8,15},{9,8},{10,9... | collective-permute-start | bytes 589832 | tf_op jit(solution)/shard_map/ppermute | solution.py:388
  55.3 3.2 %collective-permute-done.3 = f32[96,512]{1,0:T(8,128)S(1)} collective-permute-done((f32[96,512]{1,0:T(8,128)S(1)}, f32[96,512]{1,0:T(8,128)S(1)}, u32[]{:S(2)}, u32[]{:S(2)}) %collective-permute-start.3) | collective-permute-done | bytes 196640 | tf_op jit(solution)/shard_map/ppermute | solution.py:388
  58.5 0.1 collective-permute-start.10
  58.6 0.1 collective-permute-start.25
  58.7 3.2 %collective-permute-start.7 = (f32[96,512]{1,0:T(8,128)S(1)}, f32[96,512]{1,0:T(8,128)S(1)}, u32[]{:S(2)}, u32[]{:S(2)}) collective-permute-start(f32[96,512]{1,0:T(8,128)S(1)} %add_add_fusion.1.refs_0_), channel_id=1, source_target_pairs={{0,7},{1,0},{2,1},{3,2},{4,3},{5,4},{6,5},{7,6},{8,15},{9,8},{10,9... | collective-permute-start | bytes 589832 | tf_op jit(solution)/shard_map/ppermute | solution.py:388
  62.0 2.3 %collective-permute-start.22 = (f32[96,512]{1,0:T(8,128)S(1)}, f32[96,512]{1,0:T(8,128)S(1)}, u32[]{:S(2)}, u32[]{:S(2)}) collective-permute-start(f32[96,512]{1,0:T(8,128)S(1)} %collective-permute-done.21.refs_6_), channel_id=1, source_target_pairs={{0,7},{1,0},{2,1},{3,2},{4,3},{5,4},{6,5},{7,6},{8,15},{9,8},{10,9... | collective-permute-start | bytes 589832 | tf_op jit(solution)/shard_map/ppermute | solution.py:388
  64.2 3.4 %collective-permute-done.10.refs_4_ = f32[96,512]{1,0:T(8,128)S(1)} collective-permute-done((f32[96,512]{1,0:T(8,128)S(1)}, f32[96,512]{1,0:T(8,128)S(1)}, u32[]{:S(2)}, u32[]{:S(2)}) %collective-permute-start.10) | collective-permute-done | bytes 196640 | tf_op jit(solution)/shard_map/ppermute | solution.py:388
  67.6 4.2 %collective-permute-done.25.refs_9_ = f32[96,512]{1,0:T(8,128)S(1)} collective-permute-done((f32[96,512]{1,0:T(8,128)S(1)}, f32[96,512]{1,0:T(8,128)S(1)}, u32[]{:S(2)}, u32[]{:S(2)}) %collective-permute-start.25) | collective-permute-done | bytes 196640 | tf_op jit(solution)/shard_map/ppermute | solution.py:388
  71.8 3.2 %collective-permute-start.8 = (f32[96,512]{1,0:T(8,128)S(1)}, f32[96,512]{1,0:T(8,128)S(1)}, u32[]{:S(2)}, u32[]{:S(2)}) collective-permute-start(f32[96,512]{1,0:T(8,128)S(1)} %collective-permute-done.7.refs_1_), channel_id=1, source_target_pairs={{0,7},{1,0},{2,1},{3,2},{4,3},{5,4},{6,5},{7,6},{8,15},{9,8},{10,9... | collective-permute-start | bytes 589832 | tf_op jit(solution)/shard_map/ppermute | solution.py:388
  75.2 1.2 collective-permute-done.11.refs_3_
  76.3 0.8 collective-permute-start.12
  77.1 0.2 convert_reduce_fusion
  77.3 3.5 %collective-permute-done.26.refs_8_ = f32[96,512]{1,0:T(8,128)S(1)} collective-permute-done((f32[96,512]{1,0:T(8,128)S(1)}, f32[96,512]{1,0:T(8,128)S(1)}, u32[]{:S(2)}, u32[]{:S(2)}) %collective-permute-start.26) | collective-permute-done | bytes 196640 | tf_op jit(solution)/shard_map/ppermute | solution.py:388
  80.8 3.2 %collective-permute-start.9 = (f32[96,512]{1,0:T(8,128)S(1)}, f32[96,512]{1,0:T(8,128)S(1)}, u32[]{:S(2)}, u32[]{:S(2)}) collective-permute-start(f32[96,512]{1,0:T(8,128)S(1)} %collective-permute-done.8.refs_2_), channel_id=1, source_target_pairs={{0,7},{1,0},{2,1},{3,2},{4,3},{5,4},{6,5},{7,6},{8,15},{9,8},{10,9... | collective-permute-start | bytes 589832 | tf_op jit(solution)/shard_map/ppermute | solution.py:388
  84.1 2.4 %collective-permute-start.24 = (f32[96,512]{1,0:T(8,128)S(1)}, f32[96,512]{1,0:T(8,128)S(1)}, u32[]{:S(2)}, u32[]{:S(2)}) collective-permute-start(f32[96,512]{1,0:T(8,128)S(1)} %collective-permute-done.23.refs_3_), channel_id=1, source_target_pairs={{0,7},{1,0},{2,1},{3,2},{4,3},{5,4},{6,5},{7,6},{8,15},{9,8},{10,9... | collective-permute-start | bytes 589832 | tf_op jit(solution)/shard_map/ppermute | solution.py:388
  86.5 1.3 pad_add_fusion.1.count_ref
  87.8 0.1 select_reduce_fusion.order_ref
  87.9 2.9 %split_near.1 = (bf16[10,384,256]{2,1,0:T(8,128)(2,1)S(1)}, f32[192,192]{1,0:T(8,128)S(1)}) custom-call(f32[96,512]{1,0:T(8,128)S(1)} %add_add_fusion.1.refs_0_, f32[96,512]{1,0:T(8,128)S(1)} %collective-permute-done.7.refs_1_, f32[96,512]{1,0:T(8,128)S(1)} %collective-permute-done.8.refs_2_, f32[96,512]{1,0:T(8,128)S(1)} %collective-permute-done.11.refs_3_, ...), custom_call_target="tpu_custom_call" | custom-call | tf_op jit(solution)/shard_map/split_near/pallas_call | solution.py:166
  90.8 15.5 %adjoint_near.1.refs_0_ = f32[16,192,256]{2,1,0:T(8,128)S(1)} custom-call(s32[96]{0:T(128)S(1)} %select_reduce_fusion.order_ref, s32[96]{0:T(128)S(1)} %get-tuple-element.55.meta_ref, s32[2]{0:T(128)S(1)} %pad_add_fusion.1.count_ref, s32[4]{0:T(128)S(1)} %pad_add_fusion.pos_ref, bf16[96,256,256]{2,1,0:T(8,128)(2,1)S(1)} %copy-done, ...), custom_call_target="tpu_custom_call" | custom-call | tf_op jit(solution)/shard_map/adjoint_near/pallas_call | solution.py:260
  106.3 1.9 %split_far.1 = (bf16[6,384,256]{2,1,0:T(8,128)(2,1)S(1)}, f32[192,128]{1,0:T(8,128)S(1)}) custom-call(f32[96,512]{1,0:T(8,128)S(1)} %collective-permute-done.9.refs_0_, f32[96,512]{1,0:T(8,128)S(1)} %collective-permute-done.13.refs_1_, f32[96,512]{1,0:T(8,128)S(1)} %collective-permute-done.12.refs_2_, f32[96,512]{1,0:T(8,128)S(1)} %collective-permute-done.23.refs_3_, ...), custom_call_target="tpu_custom_call" | custom-call | tf_op jit(solution)/shard_map/split_far/pallas_call | solution.py:166
  108.2 11.3 %adjoint_far.1 = (f32[16,192,128]{2,1,0:T(8,128)S(1)}, f32[16,192,128]{2,1,0:T(8,128)S(1)}) custom-call(s32[96]{0:T(128)S(1)} %select_reduce_fusion.order_ref, s32[96]{0:T(128)S(1)} %get-tuple-element.55.meta_ref, s32[2]{0:T(128)S(1)} %pad_add_fusion.1.count_ref, s32[4]{0:T(128)S(1)} %pad_add_fusion.pos_ref, bf16[96,256,256]{2,1,0:T(8,128)(2,1)S(1)} %copy-done, ...), custom_call_target="tpu_custom_call" | custom-call | tf_op jit(solution)/shard_map/adjoint_far/pallas_call | solution.py:260
  119.5 0.3 collective-permute-start.35
  119.8 0.5 collective-permute-start.28
  120.3 3.0 %collective-permute-done.28 = f32[192,128]{1,0:T(8,128)S(1)} collective-permute-done((f32[192,128]{1,0:T(8,128)S(1)}, f32[192,128]{1,0:T(8,128)S(1)}, u32[]{:S(2)}, u32[]{:S(2)}) %collective-permute-start.28) | collective-permute-done | bytes 98336 | tf_op jit(solution)/shard_map/ppermute | solution.py:388
  123.4 5.4 %collective-permute-start.29 = (f32[192,128]{1,0:T(8,128)S(1)}, f32[192,128]{1,0:T(8,128)S(1)}, u32[]{:S(2)}, u32[]{:S(2)}) collective-permute-start(f32[192,128]{1,0:T(8,128)S(1)} %add.112), channel_id=1, source_target_pairs={{0,128},{8,40},{16,144},{24,56},{32,160},{40,8},{48,176},{56,24},{... | collective-permute-start | bytes 294920 | tf_op jit(solution)/shard_map/ppermute | solution.py:431
  128.8 0.2 add.121
  129.1 0.1 collective-permute-start.36
  129.3 2.0 %collective-permute-start.38 = (f32[4,192,128]{2,1,0:T(8,128)S(1)}, f32[4,192,128]{2,1,0:T(8,128)S(1)}, u32[]{:S(2)}, u32[]{:S(2)}) collective-permute-start(f32[4,192,128]{2,1,0:T(8,128)S(1)} %get-tuple-element.50), channel_id=1, source_target_pairs={{0,192},{8,56},{16,208},{24,8},{32,224},{40,24},{48,240},{56,40},{... | collective-permute-start | bytes 1179656 | tf_op jit(solution)/shard_map/ppermute | solution.py:431
  131.3 2.0 %collective-permute-start.30 = (f32[192,128]{1,0:T(8,128)S(1)}, f32[192,128]{1,0:T(8,128)S(1)}, u32[]{:S(2)}, u32[]{:S(2)}) collective-permute-start(f32[192,128]{1,0:T(8,128)S(1)} %add.112), channel_id=1, source_target_pairs={{0,64},{8,24},{16,80},{24,40},{32,96},{40,56},{48,112},{56,8},{64,... | collective-permute-start | bytes 294920 | tf_op jit(solution)/shard_map/ppermute | solution.py:431
  133.3 0.6 collective-permute-start.31
  133.9 5.0 %collective-permute-done.30 = f32[192,128]{1,0:T(8,128)S(1)} collective-permute-done((f32[192,128]{1,0:T(8,128)S(1)}, f32[192,128]{1,0:T(8,128)S(1)}, u32[]{:S(2)}, u32[]{:S(2)}) %collective-permute-start.30) | collective-permute-done | bytes 98336 | tf_op jit(solution)/shard_map/ppermute | solution.py:431
  138.9 4.8 %collective-permute-done.31 = f32[192,128]{1,0:T(8,128)S(1)} collective-permute-done((f32[192,128]{1,0:T(8,128)S(1)}, f32[192,128]{1,0:T(8,128)S(1)}, u32[]{:S(2)}, u32[]{:S(2)}) %collective-permute-start.31) | collective-permute-done | bytes 98336 | tf_op jit(solution)/shard_map/ppermute | solution.py:431
  143.8 2.0 %collective-permute-start.32 = (f32[192,128]{1,0:T(8,128)S(1)}, f32[192,128]{1,0:T(8,128)S(1)}, u32[]{:S(2)}, u32[]{:S(2)}) collective-permute-start(f32[192,128]{1,0:T(8,128)S(1)} %add_add_fusion.3), channel_id=1, source_target_pairs={{0,32},{8,136},{16,48},{24,152},{32,0},{40,168},{48,16},{56,184},{... | collective-permute-start | bytes 294920 | tf_op jit(solution)/shard_map/ppermute | solution.py:431
  145.7 3.2 %collective-permute-start.34 = (f32[192,128]{1,0:T(8,128)S(1)}, f32[192,128]{1,0:T(8,128)S(1)}, u32[]{:S(2)}, u32[]{:S(2)}) collective-permute-start(f32[192,128]{1,0:T(8,128)S(1)} %add_add_fusion.3), channel_id=1, source_target_pairs={{0,48},{8,200},{16,0},{24,216},{32,16},{40,232},{48,32},{56,248},{... | collective-permute-start | bytes 294920 | tf_op jit(solution)/shard_map/ppermute | solution.py:431
  149.0 0.1 fusion.1
  149.1 0.5 collective-permute-start.39
  149.6 0.4 collective-permute-start.40
  150.1 2.8 %collective-permute-start.41 = (f32[192,128]{1,0:T(8,128)S(1)}, f32[192,128]{1,0:T(8,128)S(1)}, u32[]{:S(2)}, u32[]{:S(2)}) collective-permute-start(f32[192,128]{1,0:T(8,128)S(1)} %get-tuple-element.53), channel_id=1, source_target_pairs={{0,48},{8,200},{16,0},{24,216},{32,16},{40,232},{48,32},{56,248},{... | collective-permute-start | bytes 294920 | tf_op jit(solution)/shard_map/ppermute | solution.py:431
  152.9 11.1 %factor.1.factor_ref = f32[192,192]{1,0:T(8,128)S(1)} custom-call(f32[192,128]{1,0:T(8,128)S(1)} %add_add_fusion.2.packed_ref), custom_call_target="tpu_custom_call" | custom-call | tf_op jit(solution)/shard_map/factor/pallas_call | solution.py:356
  164.0 1.2 shard_map.50
  165.3 1.0 shard_map.51
  (59 shorter events, 0.9 us)
Async XLA Ops:
  2.8 4.6 %copy-start = (bf16[96,256,256]{2,1,0:T(8,128)(2,1)S(1)}, bf16[96,256,256]{2,1,0:T(8,128)(2,1)}, u32[]{:S(2)}) copy-start(bf16[96,256,256]{2,1,0:T(8,128)(2,1)} %tiles_ref.5) | copy-start | bytes 37748740
  16.5 7.9 %collective-permute-start.17 = (f32[96,512]{1,0:T(8,128)S(1)}, f32[96,512]{1,0:T(8,128)S(1)}, u32[]{:S(2)}, u32[]{:S(2)}) collective-permute-start(f32[96,512]{1,0:T(8,128)S(1)} %get-tuple-element.35), channel_id=1, source_target_pairs={{0,7},{1,0},{2,1},{3,2},{4,3},{5,4},{6,5},{7,6},{8,15},{9,8},{10,9... | collective-permute-start | bytes 589832 | tf_op jit(solution)/shard_map/ppermute | solution.py:388
  21.3 8.9 %collective-permute-start = (f32[96,512]{1,0:T(8,128)S(1)}, f32[96,512]{1,0:T(8,128)S(1)}, u32[]{:S(2)}, u32[]{:S(2)}) collective-permute-start(f32[96,512]{1,0:T(8,128)S(1)} %get-tuple-element.24), channel_id=1, source_target_pairs={{0,1},{1,2},{2,3},{3,4},{4,5},{5,6},{6,7},{7,0},{8,9},{9,10},{10,1... | collective-permute-start | bytes 589832 | tf_op jit(solution)/shard_map/ppermute | solution.py:388
  21.3 11.0 %collective-permute-start.14 = (f32[96,512]{1,0:T(8,128)S(1)}, f32[96,512]{1,0:T(8,128)S(1)}, u32[]{:S(2)}, u32[]{:S(2)}) collective-permute-start(f32[96,512]{1,0:T(8,128)S(1)} %get-tuple-element.32), channel_id=1, source_target_pairs={{0,1},{1,2},{2,3},{3,4},{4,5},{5,6},{6,7},{7,0},{8,9},{9,10},{10,1... | collective-permute-start | bytes 589832 | tf_op jit(solution)/shard_map/ppermute | solution.py:388
  24.5 9.0 %collective-permute-start.18 = (f32[96,512]{1,0:T(8,128)S(1)}, f32[96,512]{1,0:T(8,128)S(1)}, u32[]{:S(2)}, u32[]{:S(2)}) collective-permute-start(f32[96,512]{1,0:T(8,128)S(1)} %add.107), channel_id=1, source_target_pairs={{0,7},{1,0},{2,1},{3,2},{4,3},{5,4},{6,5},{7,6},{8,15},{9,8},{10,9... | collective-permute-start | bytes 589832 | tf_op jit(solution)/shard_map/ppermute | solution.py:388
  28.3 9.1 %collective-permute-start.4 = (f32[96,512]{1,0:T(8,128)S(1)}, f32[96,512]{1,0:T(8,128)S(1)}, u32[]{:S(2)}, u32[]{:S(2)}) collective-permute-start(f32[96,512]{1,0:T(8,128)S(1)} %get-tuple-element.28), channel_id=1, source_target_pairs={{0,7},{1,0},{2,1},{3,2},{4,3},{5,4},{6,5},{7,6},{8,15},{9,8},{10,9... | collective-permute-start | bytes 589832 | tf_op jit(solution)/shard_map/ppermute | solution.py:388
  30.3 10.9 %collective-permute-start.1 = (f32[96,512]{1,0:T(8,128)S(1)}, f32[96,512]{1,0:T(8,128)S(1)}, u32[]{:S(2)}, u32[]{:S(2)}) collective-permute-start(f32[96,512]{1,0:T(8,128)S(1)} %add.98), channel_id=1, source_target_pairs={{0,1},{1,2},{2,3},{3,4},{4,5},{5,6},{6,7},{7,0},{8,9},{9,10},{10,1... | collective-permute-start | bytes 589832 | tf_op jit(solution)/shard_map/ppermute | solution.py:388
  32.4 9.1 %collective-permute-start.15 = (f32[96,512]{1,0:T(8,128)S(1)}, f32[96,512]{1,0:T(8,128)S(1)}, u32[]{:S(2)}, u32[]{:S(2)}) collective-permute-start(f32[96,512]{1,0:T(8,128)S(1)} %add.105), channel_id=1, source_target_pairs={{0,1},{1,2},{2,3},{3,4},{4,5},{5,6},{6,7},{7,0},{8,9},{9,10},{10,1... | collective-permute-start | bytes 589832 | tf_op jit(solution)/shard_map/ppermute | solution.py:388
  33.6 9.0 %collective-permute-start.19 = (f32[96,512]{1,0:T(8,128)S(1)}, f32[96,512]{1,0:T(8,128)S(1)}, u32[]{:S(2)}, u32[]{:S(2)}) collective-permute-start(f32[96,512]{1,0:T(8,128)S(1)} %add.108), channel_id=1, source_target_pairs={{0,7},{1,0},{2,1},{3,2},{4,3},{5,4},{6,5},{7,6},{8,15},{9,8},{10,9... | collective-permute-start | bytes 589832 | tf_op jit(solution)/shard_map/ppermute | solution.py:388
  37.4 9.2 %collective-permute-start.5 = (f32[96,512]{1,0:T(8,128)S(1)}, f32[96,512]{1,0:T(8,128)S(1)}, u32[]{:S(2)}, u32[]{:S(2)}) collective-permute-start(f32[96,512]{1,0:T(8,128)S(1)} %add.101), channel_id=1, source_target_pairs={{0,7},{1,0},{2,1},{3,2},{4,3},{5,4},{6,5},{7,6},{8,15},{9,8},{10,9... | collective-permute-start | bytes 589832 | tf_op jit(solution)/shard_map/ppermute | solution.py:388
  41.2 9.2 %collective-permute-start.2 = (f32[96,512]{1,0:T(8,128)S(1)}, f32[96,512]{1,0:T(8,128)S(1)}, u32[]{:S(2)}, u32[]{:S(2)}) collective-permute-start(f32[96,512]{1,0:T(8,128)S(1)} %add.99), channel_id=1, source_target_pairs={{0,1},{1,2},{2,3},{3,4},{4,5},{5,6},{6,7},{7,0},{8,9},{9,10},{10,1... | collective-permute-start | bytes 589832 | tf_op jit(solution)/shard_map/ppermute | solution.py:388
  41.5 9.0 %collective-permute-start.16 = (f32[96,512]{1,0:T(8,128)S(1)}, f32[96,512]{1,0:T(8,128)S(1)}, u32[]{:S(2)}, u32[]{:S(2)}) collective-permute-start(f32[96,512]{1,0:T(8,128)S(1)} %add.106), channel_id=1, source_target_pairs={{0,1},{1,2},{2,3},{3,4},{4,5},{5,6},{6,7},{7,0},{8,9},{9,10},{10,1... | collective-permute-start | bytes 589832 | tf_op jit(solution)/shard_map/ppermute | solution.py:388
  42.6 25.0 %copy-start.1 = (s32[96,2]{0,1:T(2,128)S(1)}, s32[96,2]{0,1:T(2,128)}, u32[]{:S(2)}) copy-start(s32[96,2]{0,1:T(2,128)} %param.4) | copy-start | bytes 2308
  42.7 8.6 %collective-permute-start.20 = (f32[96,512]{1,0:T(8,128)S(1)}, f32[96,512]{1,0:T(8,128)S(1)}, u32[]{:S(2)}, u32[]{:S(2)}) collective-permute-start(f32[96,512]{1,0:T(8,128)S(1)} %add.109), channel_id=1, source_target_pairs={{0,7},{1,0},{2,1},{3,2},{4,3},{5,4},{6,5},{7,6},{8,15},{9,8},{10,9... | collective-permute-start | bytes 589832 | tf_op jit(solution)/shard_map/ppermute | solution.py:388
  46.6 8.7 %collective-permute-start.6 = (f32[96,512]{1,0:T(8,128)S(1)}, f32[96,512]{1,0:T(8,128)S(1)}, u32[]{:S(2)}, u32[]{:S(2)}) collective-permute-start(f32[96,512]{1,0:T(8,128)S(1)} %add.102), channel_id=1, source_target_pairs={{0,7},{1,0},{2,1},{3,2},{4,3},{5,4},{6,5},{7,6},{8,15},{9,8},{10,9... | collective-permute-start | bytes 589832 | tf_op jit(solution)/shard_map/ppermute | solution.py:388
  50.4 8.1 %collective-permute-start.3 = (f32[96,512]{1,0:T(8,128)S(1)}, f32[96,512]{1,0:T(8,128)S(1)}, u32[]{:S(2)}, u32[]{:S(2)}) collective-permute-start(f32[96,512]{1,0:T(8,128)S(1)} %add.100), channel_id=1, source_target_pairs={{0,1},{1,2},{2,3},{3,4},{4,5},{5,6},{6,7},{7,0},{8,9},{9,10},{10,1... | collective-permute-start | bytes 589832 | tf_op jit(solution)/shard_map/ppermute | solution.py:388
  51.3 10.7 %collective-permute-start.21 = (f32[96,512]{1,0:T(8,128)S(1)}, f32[96,512]{1,0:T(8,128)S(1)}, u32[]{:S(2)}, u32[]{:S(2)}) collective-permute-start(f32[96,512]{1,0:T(8,128)S(1)} %add_add_fusion.refs_5_.refs_1_), channel_id=1, source_target_pairs={{0,7},{1,0},{2,1},{3,2},{4,3},{5,4},{6,5},{7,6},{8,15},{9,8},{10,9... | collective-permute-start | bytes 589832 | tf_op jit(solution)/shard_map/ppermute | solution.py:388
  58.5 9.1 %collective-permute-start.10 = (f32[96,512]{1,0:T(8,128)S(1)}, f32[96,512]{1,0:T(8,128)S(1)}, u32[]{:S(2)}, u32[]{:S(2)}) collective-permute-start(f32[96,512]{1,0:T(8,128)S(1)} %add_add_fusion.1.refs_0_), channel_id=1, source_target_pairs={{0,1},{1,2},{2,3},{3,4},{4,5},{5,6},{6,7},{7,0},{8,9},{9,10},{10,1... | collective-permute-start | bytes 589832 | tf_op jit(solution)/shard_map/ppermute | solution.py:388
  58.6 13.2 %collective-permute-start.25 = (f32[96,512]{1,0:T(8,128)S(1)}, f32[96,512]{1,0:T(8,128)S(1)}, u32[]{:S(2)}, u32[]{:S(2)}) collective-permute-start(f32[96,512]{1,0:T(8,128)S(1)} %add_add_fusion.refs_5_.refs_1_), channel_id=1, source_target_pairs={{0,1},{1,2},{2,3},{3,4},{4,5},{5,6},{6,7},{7,0},{8,9},{9,10},{10,1... | collective-permute-start | bytes 589832 | tf_op jit(solution)/shard_map/ppermute | solution.py:388
  58.7 13.1 %collective-permute-start.7 = (f32[96,512]{1,0:T(8,128)S(1)}, f32[96,512]{1,0:T(8,128)S(1)}, u32[]{:S(2)}, u32[]{:S(2)}) collective-permute-start(f32[96,512]{1,0:T(8,128)S(1)} %add_add_fusion.1.refs_0_), channel_id=1, source_target_pairs={{0,7},{1,0},{2,1},{3,2},{4,3},{5,4},{6,5},{7,6},{8,15},{9,8},{10,9... | collective-permute-start | bytes 589832 | tf_op jit(solution)/shard_map/ppermute | solution.py:388
  62.0 13.1 %collective-permute-start.22 = (f32[96,512]{1,0:T(8,128)S(1)}, f32[96,512]{1,0:T(8,128)S(1)}, u32[]{:S(2)}, u32[]{:S(2)}) collective-permute-start(f32[96,512]{1,0:T(8,128)S(1)} %collective-permute-done.21.refs_6_), channel_id=1, source_target_pairs={{0,7},{1,0},{2,1},{3,2},{4,3},{5,4},{6,5},{7,6},{8,15},{9,8},{10,9... | collective-permute-start | bytes 589832 | tf_op jit(solution)/shard_map/ppermute | solution.py:388
  67.6 8.7 %collective-permute-start.11 = (f32[96,512]{1,0:T(8,128)S(1)}, f32[96,512]{1,0:T(8,128)S(1)}, u32[]{:S(2)}, u32[]{:S(2)}) collective-permute-start(f32[96,512]{1,0:T(8,128)S(1)} %collective-permute-done.10.refs_4_), channel_id=1, source_target_pairs={{0,1},{1,2},{2,3},{3,4},{4,5},{5,6},{6,7},{7,0},{8,9},{9,10},{10,1... | collective-permute-start | bytes 589832 | tf_op jit(solution)/shard_map/ppermute | solution.py:388
  71.8 9.0 %collective-permute-start.26 = (f32[96,512]{1,0:T(8,128)S(1)}, f32[96,512]{1,0:T(8,128)S(1)}, u32[]{:S(2)}, u32[]{:S(2)}) collective-permute-start(f32[96,512]{1,0:T(8,128)S(1)} %collective-permute-done.25.refs_9_), channel_id=1, source_target_pairs={{0,1},{1,2},{2,3},{3,4},{4,5},{5,6},{6,7},{7,0},{8,9},{9,10},{10,1... | collective-permute-start | bytes 589832 | tf_op jit(solution)/shard_map/ppermute | solution.py:388
  71.8 9.0 %collective-permute-start.8 = (f32[96,512]{1,0:T(8,128)S(1)}, f32[96,512]{1,0:T(8,128)S(1)}, u32[]{:S(2)}, u32[]{:S(2)}) collective-permute-start(f32[96,512]{1,0:T(8,128)S(1)} %collective-permute-done.7.refs_1_), channel_id=1, source_target_pairs={{0,7},{1,0},{2,1},{3,2},{4,3},{5,4},{6,5},{7,6},{8,15},{9,8},{10,9... | collective-permute-start | bytes 589832 | tf_op jit(solution)/shard_map/ppermute | solution.py:388
  75.1 9.0 %collective-permute-start.23 = (f32[96,512]{1,0:T(8,128)S(1)}, f32[96,512]{1,0:T(8,128)S(1)}, u32[]{:S(2)}, u32[]{:S(2)}) collective-permute-start(f32[96,512]{1,0:T(8,128)S(1)} %collective-permute-done.22.refs_7_), channel_id=1, source_target_pairs={{0,7},{1,0},{2,1},{3,2},{4,3},{5,4},{6,5},{7,6},{8,15},{9,8},{10,9... | collective-permute-start | bytes 589832 | tf_op jit(solution)/shard_map/ppermute | solution.py:388
  76.3 10.2 %collective-permute-start.12 = (f32[96,512]{1,0:T(8,128)S(1)}, f32[96,512]{1,0:T(8,128)S(1)}, u32[]{:S(2)}, u32[]{:S(2)}) collective-permute-start(f32[96,512]{1,0:T(8,128)S(1)} %collective-permute-done.11.refs_3_), channel_id=1, source_target_pairs={{0,1},{1,2},{2,3},{3,4},{4,5},{5,6},{6,7},{7,0},{8,9},{9,10},{10,1... | collective-permute-start | bytes 589832 | tf_op jit(solution)/shard_map/ppermute | solution.py:388
  80.8 25.4 %collective-permute-start.27 = (f32[96,512]{1,0:T(8,128)S(1)}, f32[96,512]{1,0:T(8,128)S(1)}, u32[]{:S(2)}, u32[]{:S(2)}) collective-permute-start(f32[96,512]{1,0:T(8,128)S(1)} %collective-permute-done.26.refs_8_), channel_id=1, source_target_pairs={{0,1},{1,2},{2,3},{3,4},{4,5},{5,6},{6,7},{7,0},{8,9},{9,10},{10,1... | collective-permute-start | bytes 589832 | tf_op jit(solution)/shard_map/ppermute | solution.py:388
  80.8 25.4 %collective-permute-start.9 = (f32[96,512]{1,0:T(8,128)S(1)}, f32[96,512]{1,0:T(8,128)S(1)}, u32[]{:S(2)}, u32[]{:S(2)}) collective-permute-start(f32[96,512]{1,0:T(8,128)S(1)} %collective-permute-done.8.refs_2_), channel_id=1, source_target_pairs={{0,7},{1,0},{2,1},{3,2},{4,3},{5,4},{6,5},{7,6},{8,15},{9,8},{10,9... | collective-permute-start | bytes 589832 | tf_op jit(solution)/shard_map/ppermute | solution.py:388
  84.1 22.2 %collective-permute-start.24 = (f32[96,512]{1,0:T(8,128)S(1)}, f32[96,512]{1,0:T(8,128)S(1)}, u32[]{:S(2)}, u32[]{:S(2)}) collective-permute-start(f32[96,512]{1,0:T(8,128)S(1)} %collective-permute-done.23.refs_3_), channel_id=1, source_target_pairs={{0,7},{1,0},{2,1},{3,2},{4,3},{5,4},{6,5},{7,6},{8,15},{9,8},{10,9... | collective-permute-start | bytes 589832 | tf_op jit(solution)/shard_map/ppermute | solution.py:388
  86.5 19.8 %collective-permute-start.13 = (f32[96,512]{1,0:T(8,128)S(1)}, f32[96,512]{1,0:T(8,128)S(1)}, u32[]{:S(2)}, u32[]{:S(2)}) collective-permute-start(f32[96,512]{1,0:T(8,128)S(1)} %collective-permute-done.12.refs_2_), channel_id=1, source_target_pairs={{0,1},{1,2},{2,3},{3,4},{4,5},{5,6},{6,7},{7,0},{8,9},{9,10},{10,1... | collective-permute-start | bytes 589832 | tf_op jit(solution)/shard_map/ppermute | solution.py:388
  119.5 9.3 %collective-permute-start.35 = (f32[16,192,128]{2,1,0:T(8,128)S(1)}, f32[16,192,128]{2,1,0:T(8,128)S(1)}, u32[]{:S(2)}, u32[]{:S(2)}) collective-permute-start(f32[16,192,128]{2,1,0:T(8,128)S(1)} %get-tuple-element.45), channel_id=1, source_target_pairs={{0,8},{8,0},{1,9},{9,1},{2,10},{10,2},{3,11},{11,3},{4,12},{12,4},... | collective-permute-start | bytes 4718600 | tf_op jit(solution)/shard_map/ppermute | solution.py:388
  119.8 3.5 %collective-permute-start.28 = (f32[192,128]{1,0:T(8,128)S(1)}, f32[192,128]{1,0:T(8,128)S(1)}, u32[]{:S(2)}, u32[]{:S(2)}) collective-permute-start(f32[192,128]{1,0:T(8,128)S(1)} %get-tuple-element.41), channel_id=1, source_target_pairs={{0,8},{8,0},{1,9},{9,1},{2,10},{10,2},{3,11},{11,3},{4,12},{12,4},... | collective-permute-start | bytes 294920 | tf_op jit(solution)/shard_map/ppermute | solution.py:388
  123.4 9.9 %collective-permute-start.29 = (f32[192,128]{1,0:T(8,128)S(1)}, f32[192,128]{1,0:T(8,128)S(1)}, u32[]{:S(2)}, u32[]{:S(2)}) collective-permute-start(f32[192,128]{1,0:T(8,128)S(1)} %add.112), channel_id=1, source_target_pairs={{0,128},{8,40},{16,144},{24,56},{32,160},{40,8},{48,176},{56,24},{... | collective-permute-start | bytes 294920 | tf_op jit(solution)/shard_map/ppermute | solution.py:431
  129.1 16.6 %collective-permute-start.36 = (f32[4,192,128]{2,1,0:T(8,128)S(1)}, f32[4,192,128]{2,1,0:T(8,128)S(1)}, u32[]{:S(2)}, u32[]{:S(2)}) collective-permute-start(f32[4,192,128]{2,1,0:T(8,128)S(1)} %get-tuple-element.49), channel_id=1, source_target_pairs={{0,128},{8,40},{16,144},{24,56},{32,160},{40,8},{48,176},{56,24},{... | collective-permute-start | bytes 1179656 | tf_op jit(solution)/shard_map/ppermute | solution.py:431
  129.2 19.8 %collective-permute-start.37 = (f32[4,192,128]{2,1,0:T(8,128)S(1)}, f32[4,192,128]{2,1,0:T(8,128)S(1)}, u32[]{:S(2)}, u32[]{:S(2)}) collective-permute-start(f32[4,192,128]{2,1,0:T(8,128)S(1)} %get-tuple-element.51), channel_id=1, source_target_pairs={{0,64},{8,24},{16,80},{24,40},{32,96},{40,56},{48,112},{56,8},{64,... | collective-permute-start | bytes 1179656 | tf_op jit(solution)/shard_map/ppermute | solution.py:431
  129.3 19.7 %collective-permute-start.38 = (f32[4,192,128]{2,1,0:T(8,128)S(1)}, f32[4,192,128]{2,1,0:T(8,128)S(1)}, u32[]{:S(2)}, u32[]{:S(2)}) collective-permute-start(f32[4,192,128]{2,1,0:T(8,128)S(1)} %get-tuple-element.50), channel_id=1, source_target_pairs={{0,192},{8,56},{16,208},{24,8},{32,224},{40,24},{48,240},{56,40},{... | collective-permute-start | bytes 1179656 | tf_op jit(solution)/shard_map/ppermute | solution.py:431
  131.3 7.6 %collective-permute-start.30 = (f32[192,128]{1,0:T(8,128)S(1)}, f32[192,128]{1,0:T(8,128)S(1)}, u32[]{:S(2)}, u32[]{:S(2)}) collective-permute-start(f32[192,128]{1,0:T(8,128)S(1)} %add.112), channel_id=1, source_target_pairs={{0,64},{8,24},{16,80},{24,40},{32,96},{40,56},{48,112},{56,8},{64,... | collective-permute-start | bytes 294920 | tf_op jit(solution)/shard_map/ppermute | solution.py:431
  133.3 10.4 %collective-permute-start.31 = (f32[192,128]{1,0:T(8,128)S(1)}, f32[192,128]{1,0:T(8,128)S(1)}, u32[]{:S(2)}, u32[]{:S(2)}) collective-permute-start(f32[192,128]{1,0:T(8,128)S(1)} %add.112), channel_id=1, source_target_pairs={{0,192},{8,56},{16,208},{24,8},{32,224},{40,24},{48,240},{56,40},{... | collective-permute-start | bytes 294920 | tf_op jit(solution)/shard_map/ppermute | solution.py:431
  143.8 6.3 %collective-permute-start.32 = (f32[192,128]{1,0:T(8,128)S(1)}, f32[192,128]{1,0:T(8,128)S(1)}, u32[]{:S(2)}, u32[]{:S(2)}) collective-permute-start(f32[192,128]{1,0:T(8,128)S(1)} %add_add_fusion.3), channel_id=1, source_target_pairs={{0,32},{8,136},{16,48},{24,152},{32,0},{40,168},{48,16},{56,184},{... | collective-permute-start | bytes 294920 | tf_op jit(solution)/shard_map/ppermute | solution.py:431
  145.7 7.1 %collective-permute-start.33 = (f32[192,128]{1,0:T(8,128)S(1)}, f32[192,128]{1,0:T(8,128)S(1)}, u32[]{:S(2)}, u32[]{:S(2)}) collective-permute-start(f32[192,128]{1,0:T(8,128)S(1)} %add_add_fusion.3), channel_id=1, source_target_pairs={{0,16},{8,72},{16,32},{24,88},{32,48},{40,104},{48,0},{56,120},{64... | collective-permute-start | bytes 294920 | tf_op jit(solution)/shard_map/ppermute | solution.py:431
  145.7 7.1 %collective-permute-start.34 = (f32[192,128]{1,0:T(8,128)S(1)}, f32[192,128]{1,0:T(8,128)S(1)}, u32[]{:S(2)}, u32[]{:S(2)}) collective-permute-start(f32[192,128]{1,0:T(8,128)S(1)} %add_add_fusion.3), channel_id=1, source_target_pairs={{0,48},{8,200},{16,0},{24,216},{32,16},{40,232},{48,32},{56,248},{... | collective-permute-start | bytes 294920 | tf_op jit(solution)/shard_map/ppermute | solution.py:431
  149.1 16.1 %collective-permute-start.39 = (f32[192,128]{1,0:T(8,128)S(1)}, f32[192,128]{1,0:T(8,128)S(1)}, u32[]{:S(2)}, u32[]{:S(2)}) collective-permute-start(f32[192,128]{1,0:T(8,128)S(1)} %get-tuple-element.52), channel_id=1, source_target_pairs={{0,32},{8,136},{16,48},{24,152},{32,0},{40,168},{48,16},{56,184},{... | collective-permute-start | bytes 294920 | tf_op jit(solution)/shard_map/ppermute | solution.py:431
  149.6 15.6 %collective-permute-start.40 = (f32[192,128]{1,0:T(8,128)S(1)}, f32[192,128]{1,0:T(8,128)S(1)}, u32[]{:S(2)}, u32[]{:S(2)}) collective-permute-start(f32[192,128]{1,0:T(8,128)S(1)} %get-tuple-element.54), channel_id=1, source_target_pairs={{0,16},{8,72},{16,32},{24,88},{32,48},{40,104},{48,0},{56,120},{64... | collective-permute-start | bytes 294920 | tf_op jit(solution)/shard_map/ppermute | solution.py:431
  150.1 15.2 %collective-permute-start.41 = (f32[192,128]{1,0:T(8,128)S(1)}, f32[192,128]{1,0:T(8,128)S(1)}, u32[]{:S(2)}, u32[]{:S(2)}) collective-permute-start(f32[192,128]{1,0:T(8,128)S(1)} %get-tuple-element.53), channel_id=1, source_target_pairs={{0,48},{8,200},{16,0},{24,216},{32,16},{40,232},{48,32},{56,248},{... | collective-permute-start | bytes 294920 | tf_op jit(solution)/shard_map/ppermute | solution.py:431
where the time goes:
time: 168 us; the launch traced here: 166 us
  starting transfers between devices  64 us (38%)
  Pallas kernels  54 us (32%)
  waiting for transfers between devices  38.1 us (23%)
  local copies, waits for them, and re-layouts  4.68 us (3%)
  other arithmetic  3.88 us (2%)
    ppermute x30, starting transfers between devices, shift(): return lax.ppermute(x, axis, [(i, (i + by) % size) for i in range(size)])  44.9 us
    ppermute x30, waiting for transfers between devices, shift(): return lax.ppermute(x, axis, [(i, (i + by) % size) for i in range(size)])  28.3 us
    pallas_call x2, Pallas kernels, adjoint_call(): pl.pallas_call(functools.partial(adjoint_body, dists=dists, last=last), n...  26.8 us
    ppermute x12, starting transfers between devices, shift_xy(): return lax.ppermute(x, ('x', 'y', 'core'), pairs)  19.2 us
    pallas_call x1, Pallas kernels, factor_call(): pl.pallas_call(functools.partial(factor_body, scale=scale), name='factor'...  11.1 us
    ppermute x12, waiting for transfers between devices, shift_xy(): return lax.ppermute(x, ('x', 'y', 'core'), pairs)  9.86 us
    pallas_call x1, Pallas kernels, sketch_call(): pl.pallas_call(sketch_body, name='sketch', in_specs=[SMEM_SPEC, SMEM_SPEC...  9.15 us
    pallas_call x2, Pallas kernels, split_call(): pl.pallas_call(functools.partial(split_body, n=n, last=bool(carried)), na...  4.72 us
  transfers between devices with their start and end apart: 42, of which 16 were waited for; matrix products, arithmetic and copies ran while one was open for 1% of the time, Pallas kernels for 18%

commit v1 on v0

--- a/solution.py
+++ b/solution.py
@@ -40,7 +40,12 @@
 HBM_SPEC = pl.BlockSpec(memory_space=pltpu.HBM)
 
 
-def sketch_body(meta_ref, live_ref, pos_ref, tiles_ref, *refs):
+def place_on_mesh(index_ref):
+    index = index_ref[0]
+    return (index >> 6) & 3, (index >> 4) & 3, (index >> 3) & 1, index & 7
+
+
+def sketch_body(coords_ref, live_ref, index_ref, tiles_ref, *refs):
     outs = refs[: 2 * NZ]
     omega_ref, acc_ref, buf_ref, sems = refs[2 * NZ :]
     steps = (live_ref[0] + SLOTS - 1) >> 3
@@ -60,7 +65,7 @@
     k_ids = lax.broadcasted_iota(jnp.int32, (K, TB), 0)
     g_ids = lax.broadcasted_iota(jnp.int32, (K, TB), 1)
     base = g_ids * K + k_ids
-    z = pos_ref[0]
+    z = place_on_mesh(index_ref)[3]
 
     def fill(j, carry):
         h = base + (z * CT + j) * (TB * K)
@@ -78,8 +83,9 @@
         copy(step).wait()
         for t in range(SLOTS):
             slot = step * SLOTS + t
-            code = meta_ref[slot]
-            acc_ref[code >> 4] += dot_nt(omega_ref[code & 15], buf_ref[slot])
+            i = (coords_ref[0, slot] - 2 * z) & (RT - 1)
+            i = jnp.where(slot < live_ref[0], i, RT)
+            acc_ref[i] += dot_nt(omega_ref[coords_ref[1, slot]], buf_ref[slot])
         return carry
 
     lax.fori_loop(0, steps, work, 0)
@@ -91,7 +97,7 @@
                 ]
 
 
-def sketch_call(meta, live, pos, tiles):
+def sketch_call(coords, live, index, tiles):
     return pl.pallas_call(
         sketch_body,
         name="sketch",
@@ -105,7 +111,7 @@
         ],
         out_shape=[jax.ShapeDtypeStruct((KH, CH), jnp.float32)] * (2 * NZ),
         compiler_params=pltpu.CompilerParams(vmem_limit_bytes=24 << 20),
-    )(meta, live, pos, tiles)
+    )(coords, live, index, tiles)
 
 
 NEAR = (0, 1, 2, 6, 7)
@@ -177,7 +183,9 @@
     )(*chunks, *carried)
 
 
-def adjoint_body(order_ref, meta_ref, count_ref, pos_ref, tiles_ref, split_ref, *refs, dists, last):
+def adjoint_body(
+    order_ref, coords_ref, count_ref, index_ref, tiles_ref, split_ref, *refs, dists, last
+):
     if last:
         acc_in, keep_ref, give_ref = refs[:3]
     else:
@@ -186,7 +194,7 @@
     first = count_ref[0] if last else 0
     total = count_ref[1] if last else count_ref[0]
     steps = (total + UNROLL - 1) >> 2
-    core = pos_ref[1]
+    x, y, core, z = place_on_mesh(index_ref)
 
     def copy(step, t):
         rank = step * UNROLL + t
@@ -211,9 +219,9 @@
             copy(step, t).wait()
         for t in range(UNROLL):
             rank = step * UNROLL + t
-            code = meta_ref[order_ref[jnp.minimum(first + rank, NT - 1)]]
-            i = place_of((code >> 4) & 15, dists)
-            j = jnp.where(rank < total, code & 15, CT)
+            slot = order_ref[jnp.minimum(first + rank, NT - 1)]
+            i = place_of((coords_ref[0, slot] - 2 * z) & (RT - 1), dists)
+            j = jnp.where(rank < total, coords_ref[1, slot], CT)
             part = dot_nn(split_ref[i], buf_ref[rank])
             acc_ref[j] += part[:K] + part[K:]
         return carry
@@ -227,8 +235,8 @@
             one = q >> 2
             two = q & 3
             swap = core == 1
-            own = chip_of(pos_ref, jnp.where(swap, two, one), jnp.where(swap, one, two))
-            far = chip_of(pos_ref, jnp.where(swap, one, two), jnp.where(swap, two, one))
+            own = chip_of(x, y, jnp.where(swap, two, one), jnp.where(swap, one, two))
+            far = chip_of(x, y, jnp.where(swap, one, two), jnp.where(swap, two, one))
             keep_ref[q] = acc_ref[own, :, pl.ds(mine, 128)]
             give_ref[q] = acc_ref[far, :, pl.ds(other, 128)]
             return carry
@@ -249,11 +257,11 @@
     return jnp.clip(jnp.where(i >= 12, i - 6, i), 0, 2 * len(NEAR) - 1)
 
 
-def chip_of(pos_ref, dx, dy):
-    return ((pos_ref[2] + dx) & 3) * 4 + ((pos_ref[3] + dy) & 3)
-
-
-def adjoint_call(order, meta, count, pos, tiles, split, dists, carried=()):
+def chip_of(x, y, dx, dy):
+    return ((x + dx) & 3) * 4 + ((y + dy) & 3)
+
+
+def adjoint_call(order, coords, count, index, tiles, split, dists, carried=()):
     last = bool(carried)
     part = (CT, K, 128)
     outs = [part, part] if last else [(CT, K, TB)]
@@ -269,7 +277,7 @@
         ],
         out_shape=[jax.ShapeDtypeStruct(o, jnp.float32) for o in outs],
         compiler_params=pltpu.CompilerParams(vmem_limit_bytes=24 << 20),
-    )(order, meta, count, pos, tiles, split, *carried)
+    )(order, coords, count, index, tiles, split, *carried)
 
 
 def inverse_factor(block, rows_ref):
@@ -439,13 +447,13 @@
 
 
 def per_device(tiles, tile_coords, live_counts):
-    x, y, core, z = (lax.axis_index(name).astype(jnp.int32) for name in ("x", "y", "core", "z"))
-    pos = jnp.stack([z, core, x, y])
+    index = lax.axis_index(("x", "y", "core", "z")).astype(jnp.int32).reshape(1)
+    coords = tile_coords.T
+    tiles = pltpu.with_memory_space_constraint(tiles, pltpu.HBM)
+    parts = sketch_call(coords, live_counts, index, tiles)
     slots = jnp.arange(NT, dtype=jnp.int32)
     live = slots < live_counts[0]
-    relative = (tile_coords[:, 0] - 2 * z) & (RT - 1)
-    meta = jnp.where(live, relative, RT) * CT + tile_coords[:, 1]
-    parts = sketch_call(meta, live_counts, pos, tiles)
+    relative = (coords[0] - 2 * (index[0] & (NZ - 1))) & (RT - 1)
     far = (relative >= 2 * FAR[0]) & (relative < 2 * FAR[-1] + 2)
     key = jnp.where(live, far.astype(jnp.int32), 2) * NT + slots
     rank = jnp.sum((key[:, None] > key[None, :]).astype(jnp.int32), axis=1)
@@ -455,11 +463,11 @@
     found = gather_z(own)
     near = [got[d] for got in found for d in NEAR]
     near_split, near_gram = split_call(near)
-    carried = adjoint_call(order, meta, count, pos, tiles, near_split, NEAR)
+    carried = adjoint_call(order, coords, count, index, tiles, near_split, NEAR)
     rest = [got[d] for got in found for d in FAR]
     far_split, gram = split_call(rest, (near_gram,))
     gram = gram + shift(gram, "core", 2, 1)
-    keep, give = adjoint_call(order, meta, count, pos, tiles, far_split, FAR, carried)
+    keep, give = adjoint_call(order, coords, count, index, tiles, far_split, FAR, carried)
     gram = exchange([gram] * 4, 0)
     blocks = (keep + shift(give, "core", 2, 1)).reshape(4, 4, K, 128)
     gram = exchange([gram] * 4, 1)

time: 168 us -> 148 us (0.88)
  Pallas kernels: 54 us -> 39.4 us
  local copies, waits for them, and re-layouts: 4.68 us -> 0.78 us
  waiting for transfers between devices: 38.1 us -> 35.6 us
    pallas_call x2, Pallas kernels: 26.8 us -> 13.1 us  [adjoint_call(): pl.pallas_call(functools.partial(adjoint_body, dists=dists, last=last), n...]
    unnamed x4, local copies, waits for them, and re-layouts: 4.58 us -> 0.68 us
    ppermute x30, waiting for transfers between devices: 28.3 us -> 25.7 us  [shift(): return lax.ppermute(x, axis, [(i, (i + by) % size) for i in range(size)])]
  transfers between devices with their start and end apart: 42 -> 42, of which waited for: 16 -> 17; matrix products, arithmetic and copies ran while one was open for 1% -> 2% of each run, Pallas kernels for 18% -> 15%
where the time goes in v1:
time: 148 us; the launch traced here: 145 us
  starting transfers between devices  64.9 us (44%)
  Pallas kernels  39.4 us (27%)
  waiting for transfers between devices  35.6 us (24%)
  other arithmetic  3.07 us (2%)
  between operations  1.58 us (1%)
    ppermute x30, starting transfers between devices, shift(): return lax.ppermute(x, axis, [(i, (i + by) % size) for i in range(size)])  46 us
    ppermute x30, waiting for transfers between devices, shift(): return lax.ppermute(x, axis, [(i, (i + by) % size) for i in range(size)])  25.7 us
    ppermute x12, starting transfers between devices, shift_xy(): return lax.ppermute(x, ('x', 'y', 'core'), pairs)  18.9 us
    pallas_call x2, Pallas kernels, adjoint_call(): pl.pallas_call(functools.partial(adjoint_body, dists=dists, last=last), n...  13.1 us
    pallas_call x1, Pallas kernels, factor_call(): pl.pallas_call(functools.partial(factor_body, scale=scale), name='factor'...  11.1 us
    ppermute x12, waiting for transfers between devices, shift_xy(): return lax.ppermute(x, ('x', 'y', 'core'), pairs)  9.86 us
    pallas_call x1, Pallas kernels, sketch_call(): pl.pallas_call(sketch_body, name='sketch', in_specs=[SMEM_SPEC, SMEM_SPEC...  8.38 us
    pallas_call x2, Pallas kernels, split_call(): pl.pallas_call(functools.partial(split_body, n=n, last=bool(carried)), na...  4.71 us
  transfers between devices with their start and end apart: 42, of which 17 were waited for; matrix products, arithmetic and copies ran while one was open for 2% of the time, Pallas kernels for 15%

profile of v1, /device:TPU:2, one launch (start us, length us, event | category | flops | bytes accessed | tf_op | source)
XLA Modules:
  0.0 145.3 jit_solution(8708112314038507157)
XLA Ops:
  1.3 0.7 copy-done
  2.0 8.4 %sketch.1 = (f32[96,512]{1,0:T(8,128)S(1)}, f32[96,512]{1,0:T(8,128)S(1)}, f32[96,512]{1,0:T(8,128)S(1)}, f32[96,512]{1,0:T(8,128)S(1)}, f32[96,512]{1,0:T(8,128...) custom-call(s32[2,96]{1,0:T(2,128)S(1)} %bitcast.48, ...), custom_call_target="tpu_custom_call" | custom-call | tf_op jit(solution)/shard_map/sketch/pallas_call | solution.py:101
  10.4 4.9 %collective-permute-start.17 = (f32[96,512]{1,0:T(8,128)S(1)}, f32[96,512]{1,0:T(8,128)S(1)}, u32[]{:S(2)}, u32[]{:S(2)}) collective-permute-start(f32[96,512]{1,0:T(8,128)S(1)} %get-tuple-element.35), channel_id=1, source_target_pairs={{0,7},{1,0},{2,1},{3,2},{4,3},{5,4},{6,5},{7,6},{8,15},{9,8},{10,9... | collective-permute-start | bytes 589832 | tf_op jit(solution)/shard_map/ppermute | solution.py:396
  15.2 3.2 %collective-permute-done.17 = f32[96,512]{1,0:T(8,128)S(1)} collective-permute-done((f32[96,512]{1,0:T(8,128)S(1)}, f32[96,512]{1,0:T(8,128)S(1)}, u32[]{:S(2)}, u32[]{:S(2)}) %collective-permute-start.17) | collective-permute-done | bytes 196640 | tf_op jit(solution)/shard_map/ppermute | solution.py:396
  18.4 3.8 %collective-permute-start.18 = (f32[96,512]{1,0:T(8,128)S(1)}, f32[96,512]{1,0:T(8,128)S(1)}, u32[]{:S(2)}, u32[]{:S(2)}) collective-permute-start(f32[96,512]{1,0:T(8,128)S(1)} %add.115), channel_id=1, source_target_pairs={{0,7},{1,0},{2,1},{3,2},{4,3},{5,4},{6,5},{7,6},{8,15},{9,8},{10,9... | collective-permute-start | bytes 589832 | tf_op jit(solution)/shard_map/ppermute | solution.py:396
  22.2 1.0 collective-permute-start.4
  23.2 0.8 collective-permute-done
  24.0 0.3 collective-permute-start.1
  24.3 1.8 %collective-permute-done.14 = f32[96,512]{1,0:T(8,128)S(1)} collective-permute-done((f32[96,512]{1,0:T(8,128)S(1)}, f32[96,512]{1,0:T(8,128)S(1)}, u32[]{:S(2)}, u32[]{:S(2)}) %collective-permute-start.14) | collective-permute-done | bytes 196640 | tf_op jit(solution)/shard_map/ppermute | solution.py:396
  26.1 0.1 collective-permute-start.15
  26.2 1.3 collective-permute-done.18
  27.5 3.8 %collective-permute-start.19 = (f32[96,512]{1,0:T(8,128)S(1)}, f32[96,512]{1,0:T(8,128)S(1)}, u32[]{:S(2)}, u32[]{:S(2)}) collective-permute-start(f32[96,512]{1,0:T(8,128)S(1)} %add.116), channel_id=1, source_target_pairs={{0,7},{1,0},{2,1},{3,2},{4,3},{5,4},{6,5},{7,6},{8,15},{9,8},{10,9... | collective-permute-start | bytes 589832 | tf_op jit(solution)/shard_map/ppermute | solution.py:396
  31.4 3.8 %collective-permute-start.5 = (f32[96,512]{1,0:T(8,128)S(1)}, f32[96,512]{1,0:T(8,128)S(1)}, u32[]{:S(2)}, u32[]{:S(2)}) collective-permute-start(f32[96,512]{1,0:T(8,128)S(1)} %add.109), channel_id=1, source_target_pairs={{0,7},{1,0},{2,1},{3,2},{4,3},{5,4},{6,5},{7,6},{8,15},{9,8},{10,9... | collective-permute-start | bytes 589832 | tf_op jit(solution)/shard_map/ppermute | solution.py:396
  35.2 0.1 collective-permute-start.2
  35.3 0.2 collective-permute-done.15
  35.5 0.1 collective-permute-start.16
  35.6 0.8 collective-permute-done.19
  36.4 3.8 %collective-permute-start.20 = (f32[96,512]{1,0:T(8,128)S(1)}, f32[96,512]{1,0:T(8,128)S(1)}, u32[]{:S(2)}, u32[]{:S(2)}) collective-permute-start(f32[96,512]{1,0:T(8,128)S(1)} %add.117), channel_id=1, source_target_pairs={{0,7},{1,0},{2,1},{3,2},{4,3},{5,4},{6,5},{7,6},{8,15},{9,8},{10,9... | collective-permute-start | bytes 589832 | tf_op jit(solution)/shard_map/ppermute | solution.py:396
  40.2 3.5 %collective-permute-start.6 = (f32[96,512]{1,0:T(8,128)S(1)}, f32[96,512]{1,0:T(8,128)S(1)}, u32[]{:S(2)}, u32[]{:S(2)}) collective-permute-start(f32[96,512]{1,0:T(8,128)S(1)} %add.110), channel_id=1, source_target_pairs={{0,7},{1,0},{2,1},{3,2},{4,3},{5,4},{6,5},{7,6},{8,15},{9,8},{10,9... | collective-permute-start | bytes 589832 | tf_op jit(solution)/shard_map/ppermute | solution.py:396
  43.7 0.1 collective-permute-start.3
  43.8 0.6 collective-permute-done.16
  44.4 0.7 collective-permute-done.20
  45.1 3.9 %collective-permute-start.21 = (f32[96,512]{1,0:T(8,128)S(1)}, f32[96,512]{1,0:T(8,128)S(1)}, u32[]{:S(2)}, u32[]{:S(2)}) collective-permute-start(f32[96,512]{1,0:T(8,128)S(1)} %add_add_fusion.refs_5_.refs_1_), channel_id=1, source_target_pairs={{0,7},{1,0},{2,1},{3,2},{4,3},{5,4},{6,5},{7,6},{8,15},{9,8},{10,9... | collective-permute-start | bytes 589832 | tf_op jit(solution)/shard_map/ppermute | solution.py:396
  49.1 2.1 %collective-permute-done.3 = f32[96,512]{1,0:T(8,128)S(1)} collective-permute-done((f32[96,512]{1,0:T(8,128)S(1)}, f32[96,512]{1,0:T(8,128)S(1)}, u32[]{:S(2)}, u32[]{:S(2)}) %collective-permute-start.3) | collective-permute-done | bytes 196640 | tf_op jit(solution)/shard_map/ppermute | solution.py:396
  51.3 0.1 collective-permute-start.10
  51.4 0.7 fusion.11
  52.1 3.2 %collective-permute-start.7 = (f32[96,512]{1,0:T(8,128)S(1)}, f32[96,512]{1,0:T(8,128)S(1)}, u32[]{:S(2)}, u32[]{:S(2)}) collective-permute-start(f32[96,512]{1,0:T(8,128)S(1)} %add_add_fusion.1.refs_0_), channel_id=1, source_target_pairs={{0,7},{1,0},{2,1},{3,2},{4,3},{5,4},{6,5},{7,6},{8,15},{9,8},{10,9... | collective-permute-start | bytes 589832 | tf_op jit(solution)/shard_map/ppermute | solution.py:396
  55.3 2.8 %collective-permute-start.22 = (f32[96,512]{1,0:T(8,128)S(1)}, f32[96,512]{1,0:T(8,128)S(1)}, u32[]{:S(2)}, u32[]{:S(2)}) collective-permute-start(f32[96,512]{1,0:T(8,128)S(1)} %collective-permute-done.21.refs_6_), channel_id=1, source_target_pairs={{0,7},{1,0},{2,1},{3,2},{4,3},{5,4},{6,5},{7,6},{8,15},{9,8},{10,9... | collective-permute-start | bytes 589832 | tf_op jit(solution)/shard_map/ppermute | solution.py:396
  58.1 2.0 %collective-permute-done.10.refs_4_ = f32[96,512]{1,0:T(8,128)S(1)} collective-permute-done((f32[96,512]{1,0:T(8,128)S(1)}, f32[96,512]{1,0:T(8,128)S(1)}, u32[]{:S(2)}, u32[]{:S(2)}) %collective-permute-start.10) | collective-permute-done | bytes 196640 | tf_op jit(solution)/shard_map/ppermute | solution.py:396
  60.1 4.2 %collective-permute-done.25.refs_9_ = f32[96,512]{1,0:T(8,128)S(1)} collective-permute-done((f32[96,512]{1,0:T(8,128)S(1)}, f32[96,512]{1,0:T(8,128)S(1)}, u32[]{:S(2)}, u32[]{:S(2)}) %collective-permute-start.25) | collective-permute-done | bytes 196640 | tf_op jit(solution)/shard_map/ppermute | solution.py:396
  64.3 3.2 %collective-permute-start.8 = (f32[96,512]{1,0:T(8,128)S(1)}, f32[96,512]{1,0:T(8,128)S(1)}, u32[]{:S(2)}, u32[]{:S(2)}) collective-permute-start(f32[96,512]{1,0:T(8,128)S(1)} %collective-permute-done.7.refs_1_), channel_id=1, source_target_pairs={{0,7},{1,0},{2,1},{3,2},{4,3},{5,4},{6,5},{7,6},{8,15},{9,8},{10,9... | collective-permute-start | bytes 589832 | tf_op jit(solution)/shard_map/ppermute | solution.py:396
  67.5 0.1 collective-permute-start.23
  67.6 1.4 collective-permute-done.11.refs_3_
  69.0 0.5 collective-permute-start.12
  69.5 0.2 convert_reduce_fusion
  69.7 3.5 %collective-permute-done.26.refs_8_ = f32[96,512]{1,0:T(8,128)S(1)} collective-permute-done((f32[96,512]{1,0:T(8,128)S(1)}, f32[96,512]{1,0:T(8,128)S(1)}, u32[]{:S(2)}, u32[]{:S(2)}) %collective-permute-start.26) | collective-permute-done | bytes 196640 | tf_op jit(solution)/shard_map/ppermute | solution.py:396
  73.3 3.2 %collective-permute-start.9 = (f32[96,512]{1,0:T(8,128)S(1)}, f32[96,512]{1,0:T(8,128)S(1)}, u32[]{:S(2)}, u32[]{:S(2)}) collective-permute-start(f32[96,512]{1,0:T(8,128)S(1)} %collective-permute-done.8.refs_2_), channel_id=1, source_target_pairs={{0,7},{1,0},{2,1},{3,2},{4,3},{5,4},{6,5},{7,6},{8,15},{9,8},{10,9... | collective-permute-start | bytes 589832 | tf_op jit(solution)/shard_map/ppermute | solution.py:396
  76.5 3.1 %collective-permute-start.24 = (f32[96,512]{1,0:T(8,128)S(1)}, f32[96,512]{1,0:T(8,128)S(1)}, u32[]{:S(2)}, u32[]{:S(2)}) collective-permute-start(f32[96,512]{1,0:T(8,128)S(1)} %collective-permute-done.23.refs_3_), channel_id=1, source_target_pairs={{0,7},{1,0},{2,1},{3,2},{4,3},{5,4},{6,5},{7,6},{8,15},{9,8},{10,9... | collective-permute-start | bytes 589832 | tf_op jit(solution)/shard_map/ppermute | solution.py:396
  79.6 1.3 pad_add_fusion.count_ref
  80.9 0.1 select_reduce_fusion.order_ref
  81.0 2.9 %split_near.1 = (bf16[10,384,256]{2,1,0:T(8,128)(2,1)S(1)}, f32[192,192]{1,0:T(8,128)S(1)}) custom-call(f32[96,512]{1,0:T(8,128)S(1)} %add_add_fusion.1.refs_0_, f32[96,512]{1,0:T(8,128)S(1)} %collective-permute-done.7.refs_1_, f32[96,512]{1,0:T(8,128)S(1)} %collective-permute-done.8.refs_2_, f32[96,512]{1,0:T(8,128)S(1)} %collective-permute-done.11.refs_3_, ...), custom_call_target="tpu_custom_call" | custom-call | tf_op jit(solution)/shard_map/split_near/pallas_call | solution.py:172
  83.9 7.2 %adjoint_near.1.refs_0_ = f32[16,192,256]{2,1,0:T(8,128)S(1)} custom-call(s32[96]{0:T(128)S(1)} %select_reduce_fusion.order_ref, s32[2,96]{1,0:T(2,128)S(1)} %bitcast.50, s32[2]{0:T(128)S(1)} %pad_add_fusion.count_ref, s32[1]{0:T(128)} %bitcast.1.index_ref, bf16[96,256,256]{2,1,0:T(8,128)(2,1)} %tiles_ref.5, ...), custom_call_target="tpu_custom_call" | custom-call | tf_op jit(solution)/shard_map/adjoint_near/pallas_call | solution.py:268
  91.1 1.9 %split_far.1 = (bf16[6,384,256]{2,1,0:T(8,128)(2,1)S(1)}, f32[192,128]{1,0:T(8,128)S(1)}) custom-call(f32[96,512]{1,0:T(8,128)S(1)} %collective-permute-done.9.refs_0_, f32[96,512]{1,0:T(8,128)S(1)} %collective-permute-done.13.refs_1_, f32[96,512]{1,0:T(8,128)S(1)} %collective-permute-done.12.refs_2_, f32[96,512]{1,0:T(8,128)S(1)} %collective-permute-done.23.refs_3_, ...), custom_call_target="tpu_custom_call" | custom-call | tf_op jit(solution)/shard_map/split_far/pallas_call | solution.py:172
  93.0 5.8 %adjoint_far.1 = (f32[16,192,128]{2,1,0:T(8,128)S(1)}, f32[16,192,128]{2,1,0:T(8,128)S(1)}) custom-call(s32[96]{0:T(128)S(1)} %select_reduce_fusion.order_ref, s32[2,96]{1,0:T(2,128)S(1)} %bitcast.51, s32[2]{0:T(128)S(1)} %pad_add_fusion.count_ref, s32[1]{0:T(128)} %bitcast.1.index_ref, bf16[96,256,256]{2,1,0:T(8,128)(2,1)} %tiles_ref.5, ...), custom_call_target="tpu_custom_call" | custom-call | tf_op jit(solution)/shard_map/adjoint_far/pallas_call | solution.py:268
  98.8 0.3 collective-permute-start.35
  99.1 0.5 collective-permute-start.28
  99.6 3.0 %collective-permute-done.28 = f32[192,128]{1,0:T(8,128)S(1)} collective-permute-done((f32[192,128]{1,0:T(8,128)S(1)}, f32[192,128]{1,0:T(8,128)S(1)}, u32[]{:S(2)}, u32[]{:S(2)}) %collective-permute-start.28) | collective-permute-done | bytes 98336 | tf_op jit(solution)/shard_map/ppermute | solution.py:396
  102.7 4.9 %collective-permute-start.29 = (f32[192,128]{1,0:T(8,128)S(1)}, f32[192,128]{1,0:T(8,128)S(1)}, u32[]{:S(2)}, u32[]{:S(2)}) collective-permute-start(f32[192,128]{1,0:T(8,128)S(1)} %add.120), channel_id=1, source_target_pairs={{0,128},{8,40},{16,144},{24,56},{32,160},{40,8},{48,176},{56,24},{... | collective-permute-start | bytes 294920 | tf_op jit(solution)/shard_map/ppermute | solution.py:439
  107.6 0.2 add.129
  107.9 0.1 collective-permute-start.36
  108.1 2.0 %collective-permute-start.38 = (f32[4,192,128]{2,1,0:T(8,128)S(1)}, f32[4,192,128]{2,1,0:T(8,128)S(1)}, u32[]{:S(2)}, u32[]{:S(2)}) collective-permute-start(f32[4,192,128]{2,1,0:T(8,128)S(1)} %get-tuple-element.50), channel_id=1, source_target_pairs={{0,192},{8,56},{16,208},{24,8},{32,224},{40,24},{48,240},{56,40},{... | collective-permute-start | bytes 1179656 | tf_op jit(solution)/shard_map/ppermute | solution.py:439
  110.1 2.0 %collective-permute-start.30 = (f32[192,128]{1,0:T(8,128)S(1)}, f32[192,128]{1,0:T(8,128)S(1)}, u32[]{:S(2)}, u32[]{:S(2)}) collective-permute-start(f32[192,128]{1,0:T(8,128)S(1)} %add.120), channel_id=1, source_target_pairs={{0,64},{8,24},{16,80},{24,40},{32,96},{40,56},{48,112},{56,8},{64,... | collective-permute-start | bytes 294920 | tf_op jit(solution)/shard_map/ppermute | solution.py:439
  112.1 0.6 collective-permute-start.31
  112.7 7.1 %collective-permute-done.30 = f32[192,128]{1,0:T(8,128)S(1)} collective-permute-done((f32[192,128]{1,0:T(8,128)S(1)}, f32[192,128]{1,0:T(8,128)S(1)}, u32[]{:S(2)}, u32[]{:S(2)}) %collective-permute-start.30) | collective-permute-done | bytes 98336 | tf_op jit(solution)/shard_map/ppermute | solution.py:439
  119.8 2.7 %collective-permute-done.31 = f32[192,128]{1,0:T(8,128)S(1)} collective-permute-done((f32[192,128]{1,0:T(8,128)S(1)}, f32[192,128]{1,0:T(8,128)S(1)}, u32[]{:S(2)}, u32[]{:S(2)}) %collective-permute-start.31) | collective-permute-done | bytes 98336 | tf_op jit(solution)/shard_map/ppermute | solution.py:439
  122.6 2.6 %collective-permute-start.32 = (f32[192,128]{1,0:T(8,128)S(1)}, f32[192,128]{1,0:T(8,128)S(1)}, u32[]{:S(2)}, u32[]{:S(2)}) collective-permute-start(f32[192,128]{1,0:T(8,128)S(1)} %add_add_fusion.3), channel_id=1, source_target_pairs={{0,32},{8,136},{16,48},{24,152},{32,0},{40,168},{48,16},{56,184},{... | collective-permute-start | bytes 294920 | tf_op jit(solution)/shard_map/ppermute | solution.py:439
  125.1 3.2 %collective-permute-start.34 = (f32[192,128]{1,0:T(8,128)S(1)}, f32[192,128]{1,0:T(8,128)S(1)}, u32[]{:S(2)}, u32[]{:S(2)}) collective-permute-start(f32[192,128]{1,0:T(8,128)S(1)} %add_add_fusion.3), channel_id=1, source_target_pairs={{0,48},{8,200},{16,0},{24,216},{32,16},{40,232},{48,32},{56,248},{... | collective-permute-start | bytes 294920 | tf_op jit(solution)/shard_map/ppermute | solution.py:439
  128.4 0.1 fusion.1
  128.5 0.1 collective-permute-start.39
  128.6 0.9 collective-permute-start.40
  129.5 2.5 %collective-permute-start.41 = (f32[192,128]{1,0:T(8,128)S(1)}, f32[192,128]{1,0:T(8,128)S(1)}, u32[]{:S(2)}, u32[]{:S(2)}) collective-permute-start(f32[192,128]{1,0:T(8,128)S(1)} %get-tuple-element.53), channel_id=1, source_target_pairs={{0,48},{8,200},{16,0},{24,216},{32,16},{40,232},{48,32},{56,248},{... | collective-permute-start | bytes 294920 | tf_op jit(solution)/shard_map/ppermute | solution.py:439
  131.9 11.1 %factor.1.factor_ref = f32[192,192]{1,0:T(8,128)S(1)} custom-call(f32[192,128]{1,0:T(8,128)S(1)} %add_add_fusion.2.packed_ref), custom_call_target="tpu_custom_call" | custom-call | tf_op jit(solution)/shard_map/factor/pallas_call | solution.py:364
  143.0 1.2 shard_map.50
  144.3 1.0 shard_map.51
  (58 shorter events, 0.8 us)
Async XLA Ops:
  1.3 0.7 copy-start
  10.4 8.1 %collective-permute-start.17 = (f32[96,512]{1,0:T(8,128)S(1)}, f32[96,512]{1,0:T(8,128)S(1)}, u32[]{:S(2)}, u32[]{:S(2)}) collective-permute-start(f32[96,512]{1,0:T(8,128)S(1)} %get-tuple-element.35), channel_id=1, source_target_pairs={{0,7},{1,0},{2,1},{3,2},{4,3},{5,4},{6,5},{7,6},{8,15},{9,8},{10,9... | collective-permute-start | bytes 589832 | tf_op jit(solution)/shard_map/ppermute | solution.py:396
  15.2 8.8 %collective-permute-start = (f32[96,512]{1,0:T(8,128)S(1)}, f32[96,512]{1,0:T(8,128)S(1)}, u32[]{:S(2)}, u32[]{:S(2)}) collective-permute-start(f32[96,512]{1,0:T(8,128)S(1)} %get-tuple-element.24), channel_id=1, source_target_pairs={{0,1},{1,2},{2,3},{3,4},{4,5},{5,6},{6,7},{7,0},{8,9},{9,10},{10,1... | collective-permute-start | bytes 589832 | tf_op jit(solution)/shard_map/ppermute | solution.py:396
  15.2 10.9 %collective-permute-start.14 = (f32[96,512]{1,0:T(8,128)S(1)}, f32[96,512]{1,0:T(8,128)S(1)}, u32[]{:S(2)}, u32[]{:S(2)}) collective-permute-start(f32[96,512]{1,0:T(8,128)S(1)} %get-tuple-element.32), channel_id=1, source_target_pairs={{0,1},{1,2},{2,3},{3,4},{4,5},{5,6},{6,7},{7,0},{8,9},{9,10},{10,1... | collective-permute-start | bytes 589832 | tf_op jit(solution)/shard_map/ppermute | solution.py:396
  18.4 9.1 %collective-permute-start.18 = (f32[96,512]{1,0:T(8,128)S(1)}, f32[96,512]{1,0:T(8,128)S(1)}, u32[]{:S(2)}, u32[]{:S(2)}) collective-permute-start(f32[96,512]{1,0:T(8,128)S(1)} %add.115), channel_id=1, source_target_pairs={{0,7},{1,0},{2,1},{3,2},{4,3},{5,4},{6,5},{7,6},{8,15},{9,8},{10,9... | collective-permute-start | bytes 589832 | tf_op jit(solution)/shard_map/ppermute | solution.py:396
  22.2 9.2 %collective-permute-start.4 = (f32[96,512]{1,0:T(8,128)S(1)}, f32[96,512]{1,0:T(8,128)S(1)}, u32[]{:S(2)}, u32[]{:S(2)}) collective-permute-start(f32[96,512]{1,0:T(8,128)S(1)} %get-tuple-element.28), channel_id=1, source_target_pairs={{0,7},{1,0},{2,1},{3,2},{4,3},{5,4},{6,5},{7,6},{8,15},{9,8},{10,9... | collective-permute-start | bytes 589832 | tf_op jit(solution)/shard_map/ppermute | solution.py:396
  24.0 11.1 %collective-permute-start.1 = (f32[96,512]{1,0:T(8,128)S(1)}, f32[96,512]{1,0:T(8,128)S(1)}, u32[]{:S(2)}, u32[]{:S(2)}) collective-permute-start(f32[96,512]{1,0:T(8,128)S(1)} %add.106), channel_id=1, source_target_pairs={{0,1},{1,2},{2,3},{3,4},{4,5},{5,6},{6,7},{7,0},{8,9},{9,10},{10,1... | collective-permute-start | bytes 589832 | tf_op jit(solution)/shard_map/ppermute | solution.py:396
  26.1 9.4 %collective-permute-start.15 = (f32[96,512]{1,0:T(8,128)S(1)}, f32[96,512]{1,0:T(8,128)S(1)}, u32[]{:S(2)}, u32[]{:S(2)}) collective-permute-start(f32[96,512]{1,0:T(8,128)S(1)} %add.113), channel_id=1, source_target_pairs={{0,1},{1,2},{2,3},{3,4},{4,5},{5,6},{6,7},{7,0},{8,9},{9,10},{10,1... | collective-permute-start | bytes 589832 | tf_op jit(solution)/shard_map/ppermute | solution.py:396
  27.5 8.9 %collective-permute-start.19 = (f32[96,512]{1,0:T(8,128)S(1)}, f32[96,512]{1,0:T(8,128)S(1)}, u32[]{:S(2)}, u32[]{:S(2)}) collective-permute-start(f32[96,512]{1,0:T(8,128)S(1)} %add.116), channel_id=1, source_target_pairs={{0,7},{1,0},{2,1},{3,2},{4,3},{5,4},{6,5},{7,6},{8,15},{9,8},{10,9... | collective-permute-start | bytes 589832 | tf_op jit(solution)/shard_map/ppermute | solution.py:396
  31.4 8.8 %collective-permute-start.5 = (f32[96,512]{1,0:T(8,128)S(1)}, f32[96,512]{1,0:T(8,128)S(1)}, u32[]{:S(2)}, u32[]{:S(2)}) collective-permute-start(f32[96,512]{1,0:T(8,128)S(1)} %add.109), channel_id=1, source_target_pairs={{0,7},{1,0},{2,1},{3,2},{4,3},{5,4},{6,5},{7,6},{8,15},{9,8},{10,9... | collective-permute-start | bytes 589832 | tf_op jit(solution)/shard_map/ppermute | solution.py:396
  35.2 8.5 %collective-permute-start.2 = (f32[96,512]{1,0:T(8,128)S(1)}, f32[96,512]{1,0:T(8,128)S(1)}, u32[]{:S(2)}, u32[]{:S(2)}) collective-permute-start(f32[96,512]{1,0:T(8,128)S(1)} %add.107), channel_id=1, source_target_pairs={{0,1},{1,2},{2,3},{3,4},{4,5},{5,6},{6,7},{7,0},{8,9},{9,10},{10,1... | collective-permute-start | bytes 589832 | tf_op jit(solution)/shard_map/ppermute | solution.py:396
  35.5 8.9 %collective-permute-start.16 = (f32[96,512]{1,0:T(8,128)S(1)}, f32[96,512]{1,0:T(8,128)S(1)}, u32[]{:S(2)}, u32[]{:S(2)}) collective-permute-start(f32[96,512]{1,0:T(8,128)S(1)} %add.114), channel_id=1, source_target_pairs={{0,1},{1,2},{2,3},{3,4},{4,5},{5,6},{6,7},{7,0},{8,9},{9,10},{10,1... | collective-permute-start | bytes 589832 | tf_op jit(solution)/shard_map/ppermute | solution.py:396
  36.4 15.0 %copy-start.1 = (s32[96,2]{0,1:T(2,128)S(1)}, s32[96,2]{0,1:T(2,128)}, u32[]{:S(2)}) copy-start(s32[96,2]{0,1:T(2,128)} %param.4) | copy-start | bytes 2308
  36.4 8.7 %collective-permute-start.20 = (f32[96,512]{1,0:T(8,128)S(1)}, f32[96,512]{1,0:T(8,128)S(1)}, u32[]{:S(2)}, u32[]{:S(2)}) collective-permute-start(f32[96,512]{1,0:T(8,128)S(1)} %add.117), channel_id=1, source_target_pairs={{0,7},{1,0},{2,1},{3,2},{4,3},{5,4},{6,5},{7,6},{8,15},{9,8},{10,9... | collective-permute-start | bytes 589832 | tf_op jit(solution)/shard_map/ppermute | solution.py:396
  40.2 8.9 %collective-permute-start.6 = (f32[96,512]{1,0:T(8,128)S(1)}, f32[96,512]{1,0:T(8,128)S(1)}, u32[]{:S(2)}, u32[]{:S(2)}) collective-permute-start(f32[96,512]{1,0:T(8,128)S(1)} %add.110), channel_id=1, source_target_pairs={{0,7},{1,0},{2,1},{3,2},{4,3},{5,4},{6,5},{7,6},{8,15},{9,8},{10,9... | collective-permute-start | bytes 589832 | tf_op jit(solution)/shard_map/ppermute | solution.py:396
  43.7 7.5 %collective-permute-start.3 = (f32[96,512]{1,0:T(8,128)S(1)}, f32[96,512]{1,0:T(8,128)S(1)}, u32[]{:S(2)}, u32[]{:S(2)}) collective-permute-start(f32[96,512]{1,0:T(8,128)S(1)} %add.108), channel_id=1, source_target_pairs={{0,1},{1,2},{2,3},{3,4},{4,5},{5,6},{6,7},{7,0},{8,9},{9,10},{10,1... | collective-permute-start | bytes 589832 | tf_op jit(solution)/shard_map/ppermute | solution.py:396
  45.1 10.2 %collective-permute-start.21 = (f32[96,512]{1,0:T(8,128)S(1)}, f32[96,512]{1,0:T(8,128)S(1)}, u32[]{:S(2)}, u32[]{:S(2)}) collective-permute-start(f32[96,512]{1,0:T(8,128)S(1)} %add_add_fusion.refs_5_.refs_1_), channel_id=1, source_target_pairs={{0,7},{1,0},{2,1},{3,2},{4,3},{5,4},{6,5},{7,6},{8,15},{9,8},{10,9... | collective-permute-start | bytes 589832 | tf_op jit(solution)/shard_map/ppermute | solution.py:396
  51.3 8.8 %collective-permute-start.10 = (f32[96,512]{1,0:T(8,128)S(1)}, f32[96,512]{1,0:T(8,128)S(1)}, u32[]{:S(2)}, u32[]{:S(2)}) collective-permute-start(f32[96,512]{1,0:T(8,128)S(1)} %add_add_fusion.1.refs_0_), channel_id=1, source_target_pairs={{0,1},{1,2},{2,3},{3,4},{4,5},{5,6},{6,7},{7,0},{8,9},{9,10},{10,1... | collective-permute-start | bytes 589832 | tf_op jit(solution)/shard_map/ppermute | solution.py:396
  52.1 12.2 %collective-permute-start.25 = (f32[96,512]{1,0:T(8,128)S(1)}, f32[96,512]{1,0:T(8,128)S(1)}, u32[]{:S(2)}, u32[]{:S(2)}) collective-permute-start(f32[96,512]{1,0:T(8,128)S(1)} %add_add_fusion.refs_5_.refs_1_), channel_id=1, source_target_pairs={{0,1},{1,2},{2,3},{3,4},{4,5},{5,6},{6,7},{7,0},{8,9},{9,10},{10,1... | collective-permute-start | bytes 589832 | tf_op jit(solution)/shard_map/ppermute | solution.py:396
  52.1 12.2 %collective-permute-start.7 = (f32[96,512]{1,0:T(8,128)S(1)}, f32[96,512]{1,0:T(8,128)S(1)}, u32[]{:S(2)}, u32[]{:S(2)}) collective-permute-start(f32[96,512]{1,0:T(8,128)S(1)} %add_add_fusion.1.refs_0_), channel_id=1, source_target_pairs={{0,7},{1,0},{2,1},{3,2},{4,3},{5,4},{6,5},{7,6},{8,15},{9,8},{10,9... | collective-permute-start | bytes 589832 | tf_op jit(solution)/shard_map/ppermute | solution.py:396
  55.3 12.2 %collective-permute-start.22 = (f32[96,512]{1,0:T(8,128)S(1)}, f32[96,512]{1,0:T(8,128)S(1)}, u32[]{:S(2)}, u32[]{:S(2)}) collective-permute-start(f32[96,512]{1,0:T(8,128)S(1)} %collective-permute-done.21.refs_6_), channel_id=1, source_target_pairs={{0,7},{1,0},{2,1},{3,2},{4,3},{5,4},{6,5},{7,6},{8,15},{9,8},{10,9... | collective-permute-start | bytes 589832 | tf_op jit(solution)/shard_map/ppermute | solution.py:396
  60.0 9.0 %collective-permute-start.11 = (f32[96,512]{1,0:T(8,128)S(1)}, f32[96,512]{1,0:T(8,128)S(1)}, u32[]{:S(2)}, u32[]{:S(2)}) collective-permute-start(f32[96,512]{1,0:T(8,128)S(1)} %collective-permute-done.10.refs_4_), channel_id=1, source_target_pairs={{0,1},{1,2},{2,3},{3,4},{4,5},{5,6},{6,7},{7,0},{8,9},{9,10},{10,1... | collective-permute-start | bytes 589832 | tf_op jit(solution)/shard_map/ppermute | solution.py:396
  64.3 9.0 %collective-permute-start.26 = (f32[96,512]{1,0:T(8,128)S(1)}, f32[96,512]{1,0:T(8,128)S(1)}, u32[]{:S(2)}, u32[]{:S(2)}) collective-permute-start(f32[96,512]{1,0:T(8,128)S(1)} %collective-permute-done.25.refs_9_), channel_id=1, source_target_pairs={{0,1},{1,2},{2,3},{3,4},{4,5},{5,6},{6,7},{7,0},{8,9},{9,10},{10,1... | collective-permute-start | bytes 589832 | tf_op jit(solution)/shard_map/ppermute | solution.py:396
  64.3 9.0 %collective-permute-start.8 = (f32[96,512]{1,0:T(8,128)S(1)}, f32[96,512]{1,0:T(8,128)S(1)}, u32[]{:S(2)}, u32[]{:S(2)}) collective-permute-start(f32[96,512]{1,0:T(8,128)S(1)} %collective-permute-done.7.refs_1_), channel_id=1, source_target_pairs={{0,7},{1,0},{2,1},{3,2},{4,3},{5,4},{6,5},{7,6},{8,15},{9,8},{10,9... | collective-permute-start | bytes 589832 | tf_op jit(solution)/shard_map/ppermute | solution.py:396
  67.5 9.0 %collective-permute-start.23 = (f32[96,512]{1,0:T(8,128)S(1)}, f32[96,512]{1,0:T(8,128)S(1)}, u32[]{:S(2)}, u32[]{:S(2)}) collective-permute-start(f32[96,512]{1,0:T(8,128)S(1)} %collective-permute-done.22.refs_7_), channel_id=1, source_target_pairs={{0,7},{1,0},{2,1},{3,2},{4,3},{5,4},{6,5},{7,6},{8,15},{9,8},{10,9... | collective-permute-start | bytes 589832 | tf_op jit(solution)/shard_map/ppermute | solution.py:396
  69.0 10.5 %collective-permute-start.12 = (f32[96,512]{1,0:T(8,128)S(1)}, f32[96,512]{1,0:T(8,128)S(1)}, u32[]{:S(2)}, u32[]{:S(2)}) collective-permute-start(f32[96,512]{1,0:T(8,128)S(1)} %collective-permute-done.11.refs_3_), channel_id=1, source_target_pairs={{0,1},{1,2},{2,3},{3,4},{4,5},{5,6},{6,7},{7,0},{8,9},{9,10},{10,1... | collective-permute-start | bytes 589832 | tf_op jit(solution)/shard_map/ppermute | solution.py:396
  73.2 17.8 %collective-permute-start.27 = (f32[96,512]{1,0:T(8,128)S(1)}, f32[96,512]{1,0:T(8,128)S(1)}, u32[]{:S(2)}, u32[]{:S(2)}) collective-permute-start(f32[96,512]{1,0:T(8,128)S(1)} %collective-permute-done.26.refs_8_), channel_id=1, source_target_pairs={{0,1},{1,2},{2,3},{3,4},{4,5},{5,6},{6,7},{7,0},{8,9},{9,10},{10,1... | collective-permute-start | bytes 589832 | tf_op jit(solution)/shard_map/ppermute | solution.py:396
  73.3 17.8 %collective-permute-start.9 = (f32[96,512]{1,0:T(8,128)S(1)}, f32[96,512]{1,0:T(8,128)S(1)}, u32[]{:S(2)}, u32[]{:S(2)}) collective-permute-start(f32[96,512]{1,0:T(8,128)S(1)} %collective-permute-done.8.refs_2_), channel_id=1, source_target_pairs={{0,7},{1,0},{2,1},{3,2},{4,3},{5,4},{6,5},{7,6},{8,15},{9,8},{10,9... | collective-permute-start | bytes 589832 | tf_op jit(solution)/shard_map/ppermute | solution.py:396
  76.5 14.6 %collective-permute-start.24 = (f32[96,512]{1,0:T(8,128)S(1)}, f32[96,512]{1,0:T(8,128)S(1)}, u32[]{:S(2)}, u32[]{:S(2)}) collective-permute-start(f32[96,512]{1,0:T(8,128)S(1)} %collective-permute-done.23.refs_3_), channel_id=1, source_target_pairs={{0,7},{1,0},{2,1},{3,2},{4,3},{5,4},{6,5},{7,6},{8,15},{9,8},{10,9... | collective-permute-start | bytes 589832 | tf_op jit(solution)/shard_map/ppermute | solution.py:396
  79.6 11.6 %collective-permute-start.13 = (f32[96,512]{1,0:T(8,128)S(1)}, f32[96,512]{1,0:T(8,128)S(1)}, u32[]{:S(2)}, u32[]{:S(2)}) collective-permute-start(f32[96,512]{1,0:T(8,128)S(1)} %collective-permute-done.12.refs_2_), channel_id=1, source_target_pairs={{0,1},{1,2},{2,3},{3,4},{4,5},{5,6},{6,7},{7,0},{8,9},{9,10},{10,1... | collective-permute-start | bytes 589832 | tf_op jit(solution)/shard_map/ppermute | solution.py:396
  98.8 8.8 %collective-permute-start.35 = (f32[16,192,128]{2,1,0:T(8,128)S(1)}, f32[16,192,128]{2,1,0:T(8,128)S(1)}, u32[]{:S(2)}, u32[]{:S(2)}) collective-permute-start(f32[16,192,128]{2,1,0:T(8,128)S(1)} %get-tuple-element.45), channel_id=1, source_target_pairs={{0,8},{8,0},{1,9},{9,1},{2,10},{10,2},{3,11},{11,3},{4,12},{12,4},... | collective-permute-start | bytes 4718600 | tf_op jit(solution)/shard_map/ppermute | solution.py:396
  99.1 3.5 %collective-permute-start.28 = (f32[192,128]{1,0:T(8,128)S(1)}, f32[192,128]{1,0:T(8,128)S(1)}, u32[]{:S(2)}, u32[]{:S(2)}) collective-permute-start(f32[192,128]{1,0:T(8,128)S(1)} %get-tuple-element.41), channel_id=1, source_target_pairs={{0,8},{8,0},{1,9},{9,1},{2,10},{10,2},{3,11},{11,3},{4,12},{12,4},... | collective-permute-start | bytes 294920 | tf_op jit(solution)/shard_map/ppermute | solution.py:396
  102.7 9.4 %collective-permute-start.29 = (f32[192,128]{1,0:T(8,128)S(1)}, f32[192,128]{1,0:T(8,128)S(1)}, u32[]{:S(2)}, u32[]{:S(2)}) collective-permute-start(f32[192,128]{1,0:T(8,128)S(1)} %add.120), channel_id=1, source_target_pairs={{0,128},{8,40},{16,144},{24,56},{32,160},{40,8},{48,176},{56,24},{... | collective-permute-start | bytes 294920 | tf_op jit(solution)/shard_map/ppermute | solution.py:439
  107.9 17.2 %collective-permute-start.36 = (f32[4,192,128]{2,1,0:T(8,128)S(1)}, f32[4,192,128]{2,1,0:T(8,128)S(1)}, u32[]{:S(2)}, u32[]{:S(2)}) collective-permute-start(f32[4,192,128]{2,1,0:T(8,128)S(1)} %get-tuple-element.49), channel_id=1, source_target_pairs={{0,128},{8,40},{16,144},{24,56},{32,160},{40,8},{48,176},{56,24},{... | collective-permute-start | bytes 1179656 | tf_op jit(solution)/shard_map/ppermute | solution.py:439
  108.0 20.4 %collective-permute-start.37 = (f32[4,192,128]{2,1,0:T(8,128)S(1)}, f32[4,192,128]{2,1,0:T(8,128)S(1)}, u32[]{:S(2)}, u32[]{:S(2)}) collective-permute-start(f32[4,192,128]{2,1,0:T(8,128)S(1)} %get-tuple-element.51), channel_id=1, source_target_pairs={{0,64},{8,24},{16,80},{24,40},{32,96},{40,56},{48,112},{56,8},{64,... | collective-permute-start | bytes 1179656 | tf_op jit(solution)/shard_map/ppermute | solution.py:439
  108.1 20.3 %collective-permute-start.38 = (f32[4,192,128]{2,1,0:T(8,128)S(1)}, f32[4,192,128]{2,1,0:T(8,128)S(1)}, u32[]{:S(2)}, u32[]{:S(2)}) collective-permute-start(f32[4,192,128]{2,1,0:T(8,128)S(1)} %get-tuple-element.50), channel_id=1, source_target_pairs={{0,192},{8,56},{16,208},{24,8},{32,224},{40,24},{48,240},{56,40},{... | collective-permute-start | bytes 1179656 | tf_op jit(solution)/shard_map/ppermute | solution.py:439
  110.1 9.7 %collective-permute-start.30 = (f32[192,128]{1,0:T(8,128)S(1)}, f32[192,128]{1,0:T(8,128)S(1)}, u32[]{:S(2)}, u32[]{:S(2)}) collective-permute-start(f32[192,128]{1,0:T(8,128)S(1)} %add.120), channel_id=1, source_target_pairs={{0,64},{8,24},{16,80},{24,40},{32,96},{40,56},{48,112},{56,8},{64,... | collective-permute-start | bytes 294920 | tf_op jit(solution)/shard_map/ppermute | solution.py:439
  112.1 10.4 %collective-permute-start.31 = (f32[192,128]{1,0:T(8,128)S(1)}, f32[192,128]{1,0:T(8,128)S(1)}, u32[]{:S(2)}, u32[]{:S(2)}) collective-permute-start(f32[192,128]{1,0:T(8,128)S(1)} %add.120), channel_id=1, source_target_pairs={{0,192},{8,56},{16,208},{24,8},{32,224},{40,24},{48,240},{56,40},{... | collective-permute-start | bytes 294920 | tf_op jit(solution)/shard_map/ppermute | solution.py:439
  122.6 6.9 %collective-permute-start.32 = (f32[192,128]{1,0:T(8,128)S(1)}, f32[192,128]{1,0:T(8,128)S(1)}, u32[]{:S(2)}, u32[]{:S(2)}) collective-permute-start(f32[192,128]{1,0:T(8,128)S(1)} %add_add_fusion.3), channel_id=1, source_target_pairs={{0,32},{8,136},{16,48},{24,152},{32,0},{40,168},{48,16},{56,184},{... | collective-permute-start | bytes 294920 | tf_op jit(solution)/shard_map/ppermute | solution.py:439
  125.1 6.8 %collective-permute-start.33 = (f32[192,128]{1,0:T(8,128)S(1)}, f32[192,128]{1,0:T(8,128)S(1)}, u32[]{:S(2)}, u32[]{:S(2)}) collective-permute-start(f32[192,128]{1,0:T(8,128)S(1)} %add_add_fusion.3), channel_id=1, source_target_pairs={{0,16},{8,72},{16,32},{24,88},{32,48},{40,104},{48,0},{56,120},{64... | collective-permute-start | bytes 294920 | tf_op jit(solution)/shard_map/ppermute | solution.py:439
  125.1 6.8 %collective-permute-start.34 = (f32[192,128]{1,0:T(8,128)S(1)}, f32[192,128]{1,0:T(8,128)S(1)}, u32[]{:S(2)}, u32[]{:S(2)}) collective-permute-start(f32[192,128]{1,0:T(8,128)S(1)} %add_add_fusion.3), channel_id=1, source_target_pairs={{0,48},{8,200},{16,0},{24,216},{32,16},{40,232},{48,32},{56,248},{... | collective-permute-start | bytes 294920 | tf_op jit(solution)/shard_map/ppermute | solution.py:439
  128.5 15.8 %collective-permute-start.39 = (f32[192,128]{1,0:T(8,128)S(1)}, f32[192,128]{1,0:T(8,128)S(1)}, u32[]{:S(2)}, u32[]{:S(2)}) collective-permute-start(f32[192,128]{1,0:T(8,128)S(1)} %get-tuple-element.52), channel_id=1, source_target_pairs={{0,32},{8,136},{16,48},{24,152},{32,0},{40,168},{48,16},{56,184},{... | collective-permute-start | bytes 294920 | tf_op jit(solution)/shard_map/ppermute | solution.py:439
  128.6 15.7 %collective-permute-start.40 = (f32[192,128]{1,0:T(8,128)S(1)}, f32[192,128]{1,0:T(8,128)S(1)}, u32[]{:S(2)}, u32[]{:S(2)}) collective-permute-start(f32[192,128]{1,0:T(8,128)S(1)} %get-tuple-element.54), channel_id=1, source_target_pairs={{0,16},{8,72},{16,32},{24,88},{32,48},{40,104},{48,0},{56,120},{64... | collective-permute-start | bytes 294920 | tf_op jit(solution)/shard_map/ppermute | solution.py:439
  129.5 14.8 %collective-permute-start.41 = (f32[192,128]{1,0:T(8,128)S(1)}, f32[192,128]{1,0:T(8,128)S(1)}, u32[]{:S(2)}, u32[]{:S(2)}) collective-permute-start(f32[192,128]{1,0:T(8,128)S(1)} %get-tuple-element.53), channel_id=1, source_target_pairs={{0,48},{8,200},{16,0},{24,216},{32,16},{40,232},{48,32},{56,248},{... | collective-permute-start | bytes 294920 | tf_op jit(solution)/shard_map/ppermute | solution.py:439

commit v2 on v1

--- a/solution.py
+++ b/solution.py
@@ -19,6 +19,8 @@
 CH = RT * TB // NZ
 SLOTS = 8
 UNROLL = 4
+NEAR = (0, 1, 2, 6, 7)
+FAR = (3, 4, 5)
 STEPS = NT // SLOTS
 HIGHEST = lax.Precision.HIGHEST
 
@@ -45,77 +47,166 @@
     return (index >> 6) & 3, (index >> 4) & 3, (index >> 3) & 1, index & 7
 
 
-def sketch_body(coords_ref, live_ref, index_ref, tiles_ref, *refs):
-    outs = refs[: 2 * NZ]
-    omega_ref, acc_ref, buf_ref, sems = refs[2 * NZ :]
-    steps = (live_ref[0] + SLOTS - 1) >> 3
-
-    def copy(step):
-        return pltpu.make_async_copy(
-            tiles_ref.at[pl.ds(step * SLOTS, SLOTS)],
-            buf_ref.at[pl.ds(step * SLOTS, SLOTS)],
-            sems.at[step],
-        )
-
-    def fetch(step, carry):
-        copy(step).start()
-        return carry
-
-    lax.fori_loop(0, steps, fetch, 0)
+def relative_row(coords_ref, slot, z):
+    return (coords_ref[0, slot] - 2 * z) & (RT - 1)
+
+
+def place_of(i, dists):
+    if dists == FAR:
+        return jnp.clip(i - 2 * FAR[0], 0, 2 * len(FAR) - 1)
+    return jnp.clip(jnp.where(i >= 12, i - 6, i), 0, 2 * len(NEAR) - 1)
+
+
+def sketch_tiles(steps, total, slot_at, coords_ref, z, omega_ref, buf_ref, acc_ref, dists, ready):
+    def work(step, carry):
+        carry = ready(slot_at(step * UNROLL + UNROLL - 1), carry)
+        for t in range(UNROLL):
+            rank = step * UNROLL + t
+            slot = slot_at(rank)
+            i = place_of(relative_row(coords_ref, slot, z), dists)
+            i = jnp.where(rank < total, i, 2 * len(dists))
+            acc_ref[i] += dot_nt(omega_ref[coords_ref[1, slot]], buf_ref[slot])
+        return carry
+
+    return lax.fori_loop(0, steps, work, 0)
+
+
+def store_parts(outs, acc_ref, n):
+    for c in range(n):
+        for half in range(2):
+            for e in range(2):
+                outs[half * n + c][:, e * TB : (e + 1) * TB] = acc_ref[
+                    2 * c + e, half * KH : (half + 1) * KH, :
+                ]
+
+
+def sketch_far_body(coords_ref, live_ref, index_ref, tiles_ref, *refs):
+    n = len(FAR)
+    outs = refs[: 2 * n]
+    omega_ref, buf_ref, near_ref, far_ref, count_ref, acc_ref, sems = refs[2 * n :]
+    batches = (live_ref[0] + SLOTS - 1) >> 3
+    z = place_on_mesh(index_ref)[3]
+
+    def copy(batch):
+        part = pl.ds(batch * SLOTS, SLOTS)
+        return pltpu.make_async_copy(tiles_ref.at[part], buf_ref.at[part], sems.at[batch])
+
+    def fetch(batch, carry):
+        copy(batch).start()
+        return carry
+
+    def land(batch, carry):
+        copy(batch).wait()
+        return carry
+
+    lax.fori_loop(0, batches, fetch, 0)
     k_ids = lax.broadcasted_iota(jnp.int32, (K, TB), 0)
     g_ids = lax.broadcasted_iota(jnp.int32, (K, TB), 1)
     base = g_ids * K + k_ids
-    z = place_on_mesh(index_ref)[3]
-
-    def fill(j, carry):
+
+    def fill(j, found):
         h = base + (z * CT + j) * (TB * K)
         h = h * 747796405 + 1442695040
         h = h ^ (h >> 15)
         h = h * 1103515245 + 12345
         h = h ^ (h >> 13)
         omega_ref[j] = (1 - 2 * ((h >> 9) & 1)).astype(jnp.float32).astype(jnp.bfloat16)
-        acc_ref[j] = jnp.zeros((K, TB), jnp.float32)
-        return carry
-
-    lax.fori_loop(0, CT, fill, 0)
-
-    def work(step, carry):
-        copy(step).wait()
-        for t in range(SLOTS):
-            slot = step * SLOTS + t
-            i = (coords_ref[0, slot] - 2 * z) & (RT - 1)
-            i = jnp.where(slot < live_ref[0], i, RT)
-            acc_ref[i] += dot_nt(omega_ref[coords_ref[1, slot]], buf_ref[slot])
-        return carry
-
-    lax.fori_loop(0, steps, work, 0)
-    for d in range(NZ):
-        for half in range(2):
-            for e in range(2):
-                outs[half * NZ + d][:, e * TB : (e + 1) * TB] = acc_ref[
-                    2 * d + e, half * KH : (half + 1) * KH, :
-                ]
-
-
-def sketch_call(coords, live, index, tiles):
+        near, far = found
+        for t in range(NT // CT):
+            slot = j * (NT // CT) + t
+            i = relative_row(coords_ref, slot, z)
+            inside = jnp.where((i >= 2 * FAR[0]) & (i < 2 * FAR[-1] + 2), 1, 0)
+            live = jnp.where(slot < live_ref[0], 1, 0)
+            far_ref[far] = slot
+            near_ref[near] = slot
+            far += live * inside
+            near += live * (1 - inside)
+        return near, far
+
+    near, far = lax.fori_loop(0, CT, fill, (jnp.int32(0), jnp.int32(0)))
+    count_ref[0] = near
+    count_ref[1] = far
+    acc_ref[...] = jnp.zeros(acc_ref.shape, jnp.float32)
+
+    def slot_at(rank):
+        return far_ref[jnp.minimum(rank, far - 1)]
+
+    def ready(slot, landed):
+        upto = (slot >> 3) + 1
+        lax.fori_loop(landed, upto, land, 0)
+        return upto
+
+    steps = (far + UNROLL - 1) >> 2
+    landed = sketch_tiles(
+        steps, far, slot_at, coords_ref, z, omega_ref, buf_ref, acc_ref, FAR, ready
+    )
+    store_parts(outs, acc_ref, n)
+    lax.fori_loop(landed, batches, land, 0)
+
+
+def sketch_near_body(coords_ref, index_ref, near_ref, count_ref, omega_ref, buf_ref, *refs):
+    n = len(NEAR)
+    outs, acc_ref = refs[: 2 * n], refs[2 * n]
+    total = count_ref[0]
+    z = place_on_mesh(index_ref)[3]
+    acc_ref[...] = jnp.zeros(acc_ref.shape, jnp.float32)
+
+    def slot_at(rank):
+        return near_ref[jnp.minimum(rank, total - 1)]
+
+    steps = (total + UNROLL - 1) >> 2
+    sketch_tiles(
+        steps, total, slot_at, coords_ref, z, omega_ref, buf_ref, acc_ref, NEAR, lambda _, c: c
+    )
+    store_parts(outs, acc_ref, n)
+
+
+def sketch_near_call(coords, index, near, count, omega, held, shape, limit):
+    m = len(NEAR)
     return pl.pallas_call(
-        sketch_body,
-        name="sketch",
-        in_specs=[SMEM_SPEC, SMEM_SPEC, SMEM_SPEC, HBM_SPEC],
-        out_specs=[VMEM_SPEC] * (2 * NZ),
+        sketch_near_body,
+        name="sketch_near",
+        in_specs=[SMEM_SPEC] * 4 + [VMEM_SPEC] * 2,
+        out_specs=[VMEM_SPEC] * (2 * m),
+        scratch_shapes=[pltpu.VMEM((2 * m + 1, K, TB), jnp.float32)],
+        out_shape=[shape] * (2 * m),
+        compiler_params=limit,
+    )(coords, index, near, count, omega, held)
+
+
+def sketch_calls(coords, live, index, tiles):
+    shape = jax.ShapeDtypeStruct((KH, CH), jnp.float32)
+    limit = pltpu.CompilerParams(vmem_limit_bytes=24 << 20)
+    n = len(FAR)
+    got = pl.pallas_call(
+        sketch_far_body,
+        name="sketch_far",
+        in_specs=[SMEM_SPEC] * 3 + [HBM_SPEC],
+        out_specs=[VMEM_SPEC] * (2 * n + 2) + [SMEM_SPEC] * 3,
         scratch_shapes=[
-            pltpu.VMEM((CT, K, TB), jnp.bfloat16),
-            pltpu.VMEM((RT + 1, K, TB), jnp.float32),
-            pltpu.VMEM((NT, TB, TB), jnp.bfloat16),
+            pltpu.VMEM((2 * n + 1, K, TB), jnp.float32),
             pltpu.SemaphoreType.DMA((STEPS,)),
         ],
-        out_shape=[jax.ShapeDtypeStruct((KH, CH), jnp.float32)] * (2 * NZ),
-        compiler_params=pltpu.CompilerParams(vmem_limit_bytes=24 << 20),
+        out_shape=[shape] * (2 * n)
+        + [
+            jax.ShapeDtypeStruct((CT, K, TB), jnp.bfloat16),
+            jax.ShapeDtypeStruct((NT, TB, TB), jnp.bfloat16),
+            jax.ShapeDtypeStruct((NT,), jnp.int32),
+            jax.ShapeDtypeStruct((NT,), jnp.int32),
+            jax.ShapeDtypeStruct((2,), jnp.int32),
+        ],
+        compiler_params=limit,
     )(coords, live, index, tiles)
-
-
-NEAR = (0, 1, 2, 6, 7)
-FAR = (3, 4, 5)
+    omega, held, near, far, count = got[2 * n :]
+    rest = sketch_near_call(coords, index, near, count, omega, held, shape, limit)
+    m = len(NEAR)
+    parts = [[None] * NZ for _ in range(2)]
+    for half in range(2):
+        for c, d in enumerate(FAR):
+            parts[half][d] = got[half * n + c]
+        for c, d in enumerate(NEAR):
+            parts[half][d] = rest[half * m + c]
+    return parts, held, near, far, count
 
 
 def split_body(*refs, n, last):
@@ -184,30 +275,17 @@
 
 
 def adjoint_body(
-    order_ref, coords_ref, count_ref, index_ref, tiles_ref, split_ref, *refs, dists, last
+    list_ref, coords_ref, count_ref, index_ref, buf_ref, split_ref, *refs, dists, last
 ):
     if last:
         acc_in, keep_ref, give_ref = refs[:3]
     else:
         acc_out = refs[0]
-    acc_ref, buf_ref, sems = refs[-3:]
-    first = count_ref[0] if last else 0
+    acc_ref = refs[-1]
     total = count_ref[1] if last else count_ref[0]
     steps = (total + UNROLL - 1) >> 2
     x, y, core, z = place_on_mesh(index_ref)
 
-    def copy(step, t):
-        rank = step * UNROLL + t
-        slot = order_ref[jnp.minimum(first + rank, NT - 1)]
-        return pltpu.make_async_copy(tiles_ref.at[slot], buf_ref.at[rank], sems.at[step])
-
-    def fetch(step, carry):
-        for t in range(UNROLL):
-            copy(step, t).start()
-        return carry
-
-    lax.fori_loop(0, steps, fetch, 0)
-
     def clear(j, carry):
         acc_ref[j] = acc_in[j] if last else jnp.zeros((K, TB), jnp.float32)
         return carry
@@ -216,13 +294,11 @@
 
     def work(step, carry):
         for t in range(UNROLL):
-            copy(step, t).wait()
-        for t in range(UNROLL):
             rank = step * UNROLL + t
-            slot = order_ref[jnp.minimum(first + rank, NT - 1)]
-            i = place_of((coords_ref[0, slot] - 2 * z) & (RT - 1), dists)
+            slot = list_ref[jnp.minimum(rank, total - 1)]
+            i = place_of(relative_row(coords_ref, slot, z), dists)
             j = jnp.where(rank < total, coords_ref[1, slot], CT)
-            part = dot_nn(split_ref[i], buf_ref[rank])
+            part = dot_nn(split_ref[i], buf_ref[slot])
             acc_ref[j] += part[:K] + part[K:]
         return carry
 
@@ -251,33 +327,23 @@
         lax.fori_loop(0, CT, save, 0)
 
 
-def place_of(i, dists):
-    if dists == FAR:
-        return jnp.clip(i - 2 * FAR[0], 0, 2 * len(FAR) - 1)
-    return jnp.clip(jnp.where(i >= 12, i - 6, i), 0, 2 * len(NEAR) - 1)
-
-
 def chip_of(x, y, dx, dy):
     return ((x + dx) & 3) * 4 + ((y + dy) & 3)
 
 
-def adjoint_call(order, coords, count, index, tiles, split, dists, carried=()):
+def adjoint_call(slots, coords, count, index, held, split, dists, carried=()):
     last = bool(carried)
     part = (CT, K, 128)
     outs = [part, part] if last else [(CT, K, TB)]
     return pl.pallas_call(
         functools.partial(adjoint_body, dists=dists, last=last),
         name="adjoint_far" if last else "adjoint_near",
-        in_specs=[SMEM_SPEC] * 4 + [HBM_SPEC] + [VMEM_SPEC] * (1 + len(carried)),
+        in_specs=[SMEM_SPEC] * 4 + [VMEM_SPEC] * (2 + len(carried)),
         out_specs=[VMEM_SPEC] * len(outs),
-        scratch_shapes=[
-            pltpu.VMEM((CT + 1, K, TB), jnp.float32),
-            pltpu.VMEM((NT, TB, TB), jnp.bfloat16),
-            pltpu.SemaphoreType.DMA((NT // UNROLL,)),
-        ],
+        scratch_shapes=[pltpu.VMEM((CT + 1, K, TB), jnp.float32)],
         out_shape=[jax.ShapeDtypeStruct(o, jnp.float32) for o in outs],
-        compiler_params=pltpu.CompilerParams(vmem_limit_bytes=24 << 20),
-    )(order, coords, count, index, tiles, split, *carried)
+        compiler_params=pltpu.CompilerParams(vmem_limit_bytes=8 << 20),
+    )(slots, coords, count, index, held, split, *carried)
 
 
 def inverse_factor(block, rows_ref):
@@ -401,7 +467,7 @@
     for half, part in enumerate(parts):
         up, down = (4, 3) if half == 0 else (3, 4)
         chains.append([part[up], part[NZ - down], up, down])
-    for _ in range(4):
+    for _ in range(1, 5):
         for chain, part in zip(chains, parts):
             if chain[2]:
                 chain[0] = shift(chain[0], "z", NZ, 1)
@@ -450,24 +516,18 @@
     index = lax.axis_index(("x", "y", "core", "z")).astype(jnp.int32).reshape(1)
     coords = tile_coords.T
     tiles = pltpu.with_memory_space_constraint(tiles, pltpu.HBM)
-    parts = sketch_call(coords, live_counts, index, tiles)
-    slots = jnp.arange(NT, dtype=jnp.int32)
-    live = slots < live_counts[0]
-    relative = (coords[0] - 2 * (index[0] & (NZ - 1))) & (RT - 1)
-    far = (relative >= 2 * FAR[0]) & (relative < 2 * FAR[-1] + 2)
-    key = jnp.where(live, far.astype(jnp.int32), 2) * NT + slots
-    rank = jnp.sum((key[:, None] > key[None, :]).astype(jnp.int32), axis=1)
-    order = jnp.sum(jnp.where(rank[:, None] == slots[None, :], slots[:, None], 0), axis=0)
-    count = jnp.stack([jnp.sum(live & ~far), jnp.sum(live & far)]).astype(jnp.int32)
-    own = reduce_z([parts[:NZ], parts[NZ:]])
+    parts, held, near_slots, far_slots, count = sketch_calls(coords, live_counts, index, tiles)
+    own = reduce_z(parts)
     found = gather_z(own)
     near = [got[d] for got in found for d in NEAR]
     near_split, near_gram = split_call(near)
-    carried = adjoint_call(order, coords, count, index, tiles, near_split, NEAR)
+    carried = adjoint_call(near_slots, coords, count, index, held, near_split, NEAR)
     rest = [got[d] for got in found for d in FAR]
     far_split, gram = split_call(rest, (near_gram,))
     gram = gram + shift(gram, "core", 2, 1)
-    keep, give = adjoint_call(order, coords, count, index, tiles, far_split, FAR, carried)
+    keep, give = adjoint_call(
+        far_slots, coords, count, index, held, far_split, FAR, carried
+    )
     gram = exchange([gram] * 4, 0)
     blocks = (keep + shift(give, "core", 2, 1)).reshape(4, 4, K, 128)
     gram = exchange([gram] * 4, 1)

time: 148 us -> 141 us (0.953)
  waiting for transfers between devices: 35.6 us -> 32.7 us
  other arithmetic: 3.07 us -> 0.74 us
  starting transfers between devices: 64.9 us -> 62.7 us
    pallas_call x1 -> x2, Pallas kernels: 8.38 us -> 11.7 us  [the longest x1 6.41 us: sketch_calls(): pl.pallas_call(sketch_far_body, name='sketch_far', in_specs=[SMEM_SPEC] *...]
    pallas_call x2, Pallas kernels: 13.1 us -> 10.8 us  [adjoint_call(): pl.pallas_call(functools.partial(adjoint_body, dists=dists, last=last), n...]
    ppermute x12, waiting for transfers between devices: 9.86 us -> 8.04 us  [shift_xy(): return lax.ppermute(x, ('x', 'y', 'core'), pairs)]
  transfers between devices with their start and end apart: 42 -> 42, of which waited for: 17 -> 13; matrix products, arithmetic and copies ran while one was open for 2% -> 1% of each run, Pallas kernels for 15% -> 19%
where the time goes in v2:
time: 141 us; the launch traced here: 139 us
  starting transfers between devices  62.7 us (44%)
  Pallas kernels  40.5 us (29%)
  waiting for transfers between devices  32.7 us (23%)
  between operations  1.52 us (1%)
    ppermute x30, starting transfers between devices, shift(): return lax.ppermute(x, axis, [(i, (i + by) % size) for i in range(size)])  44.8 us
    ppermute x30, waiting for transfers between devices, shift(): return lax.ppermute(x, axis, [(i, (i + by) % size) for i in range(size)])  24.7 us
    ppermute x12, starting transfers between devices, shift_xy(): return lax.ppermute(x, ('x', 'y', 'core'), pairs)  17.9 us
    pallas_call x1, Pallas kernels, factor_call(): pl.pallas_call(functools.partial(factor_body, scale=scale), name='factor'...  11.1 us
    pallas_call x2, Pallas kernels, adjoint_call(): pl.pallas_call(functools.partial(adjoint_body, dists=dists, last=last), n...  10.8 us
    ppermute x12, waiting for transfers between devices, shift_xy(): return lax.ppermute(x, ('x', 'y', 'core'), pairs)  8.04 us
    pallas_call x1, Pallas kernels, sketch_calls(): pl.pallas_call(sketch_far_body, name='sketch_far', in_specs=[SMEM_SPEC] *...  6.41 us
    pallas_call x1, Pallas kernels, sketch_near_call(): pl.pallas_call(sketch_near_body, name='sketch_near', in_specs=[SMEM_SPEC]...  5.32 us
  transfers between devices with their start and end apart: 42, of which 13 were waited for; matrix products, arithmetic and copies ran while one was open for 1% of the time, Pallas kernels for 19%

profile of v2, /device:TPU:2, one launch (start us, length us, event | category | flops | bytes accessed | tf_op | source)
XLA Modules:
  0.0 138.9 jit_solution(15614445125262839784)
XLA Ops:
  1.3 0.7 copy-done
  2.0 6.4 %sketch_far.1 = (f32[96,512]{1,0:T(8,128)S(1)}, f32[96,512]{1,0:T(8,128)S(1)}, f32[96,512]{1,0:T(8,128)S(1)}, f32[96,512]{1,0:T(8,128)S(1)}, f32[96,512]{1,0:T(8...) custom-call(s32[2,96]{1,0:T(2,128)S(1)} %bitcast.20, ...), custom_call_target="tpu_custom_call" | custom-call | tf_op jit(solution)/shard_map/sketch_far/pallas_call | solution.py:181
  8.4 5.3 %collective-permute-start.17 = (f32[96,512]{1,0:T(8,128)S(1)}, f32[96,512]{1,0:T(8,128)S(1)}, u32[]{:S(2)}, u32[]{:S(2)}) collective-permute-start(f32[96,512]{1,0:T(8,128)S(1)} %get-tuple-element.44), channel_id=1, source_target_pairs={{0,7},{1,0},{2,1},{3,2},{4,3},{5,4},{6,5},{7,6},{8,15},{9,8},{10,9... | collective-permute-start | bytes 589832 | tf_op jit(solution)/shard_map/ppermute | solution.py:462
  13.7 3.3 %collective-permute-done.17 = f32[96,512]{1,0:T(8,128)S(1)} collective-permute-done((f32[96,512]{1,0:T(8,128)S(1)}, f32[96,512]{1,0:T(8,128)S(1)}, u32[]{:S(2)}, u32[]{:S(2)}) %collective-permute-start.17) | collective-permute-done | bytes 196640 | tf_op jit(solution)/shard_map/ppermute | solution.py:462
  17.0 3.8 %collective-permute-start.18 = (f32[96,512]{1,0:T(8,128)S(1)}, f32[96,512]{1,0:T(8,128)S(1)}, u32[]{:S(2)}, u32[]{:S(2)}) collective-permute-start(f32[96,512]{1,0:T(8,128)S(1)} %add.105), channel_id=1, source_target_pairs={{0,7},{1,0},{2,1},{3,2},{4,3},{5,4},{6,5},{7,6},{8,15},{9,8},{10,9... | collective-permute-start | bytes 589832 | tf_op jit(solution)/shard_map/ppermute | solution.py:462
  20.8 0.9 collective-permute-start.4
  21.7 5.3 %sketch_near.1 = (f32[96,512]{1,0:T(8,128)S(1)}, f32[96,512]{1,0:T(8,128)S(1)}, f32[96,512]{1,0:T(8,128)S(1)}, f32[96,512]{1,0:T(8,128)S(1)}, f32[96,512]{1,0:T(...) custom-call(s32[2,96]{1,0:T(2,128)S(1)} %bitcast.21, ...), custom_call_target="tpu_custom_call" | custom-call | tf_op jit(solution)/shard_map/sketch_near/pallas_call | solution.py:166
  27.1 1.5 %collective-permute-start.1 = (f32[96,512]{1,0:T(8,128)S(1)}, f32[96,512]{1,0:T(8,128)S(1)}, u32[]{:S(2)}, u32[]{:S(2)}) collective-permute-start(f32[96,512]{1,0:T(8,128)S(1)} %add.96), channel_id=1, source_target_pairs={{0,1},{1,2},{2,3},{3,4},{4,5},{5,6},{6,7},{7,0},{8,9},{9,10},{10,1... | collective-permute-start | bytes 589832 | tf_op jit(solution)/shard_map/ppermute | solution.py:462
  28.6 0.1 collective-permute-start.15
  28.8 3.3 %collective-permute-start.19 = (f32[96,512]{1,0:T(8,128)S(1)}, f32[96,512]{1,0:T(8,128)S(1)}, u32[]{:S(2)}, u32[]{:S(2)}) collective-permute-start(f32[96,512]{1,0:T(8,128)S(1)} %add.106), channel_id=1, source_target_pairs={{0,7},{1,0},{2,1},{3,2},{4,3},{5,4},{6,5},{7,6},{8,15},{9,8},{10,9... | collective-permute-start | bytes 589832 | tf_op jit(solution)/shard_map/ppermute | solution.py:462
  32.1 0.7 collective-permute-start.5
  32.8 2.4 %collective-permute-done.1 = f32[96,512]{1,0:T(8,128)S(1)} collective-permute-done((f32[96,512]{1,0:T(8,128)S(1)}, f32[96,512]{1,0:T(8,128)S(1)}, u32[]{:S(2)}, u32[]{:S(2)}) %collective-permute-start.1) | collective-permute-done | bytes 196640 | tf_op jit(solution)/shard_map/ppermute | solution.py:462
  35.2 0.1 collective-permute-start.2
  35.3 4.1 %collective-permute-done.15 = f32[96,512]{1,0:T(8,128)S(1)} collective-permute-done((f32[96,512]{1,0:T(8,128)S(1)}, f32[96,512]{1,0:T(8,128)S(1)}, u32[]{:S(2)}, u32[]{:S(2)}) %collective-permute-start.15) | collective-permute-done | bytes 196640 | tf_op jit(solution)/shard_map/ppermute | solution.py:462
  39.4 0.1 collective-permute-start.16
  39.6 3.3 %collective-permute-start.20 = (f32[96,512]{1,0:T(8,128)S(1)}, f32[96,512]{1,0:T(8,128)S(1)}, u32[]{:S(2)}, u32[]{:S(2)}) collective-permute-start(f32[96,512]{1,0:T(8,128)S(1)} %add.107), channel_id=1, source_target_pairs={{0,7},{1,0},{2,1},{3,2},{4,3},{5,4},{6,5},{7,6},{8,15},{9,8},{10,9... | collective-permute-start | bytes 589832 | tf_op jit(solution)/shard_map/ppermute | solution.py:462
  42.9 0.1 collective-permute-start.6
  43.0 0.6 collective-permute-done.2
  43.7 1.6 %collective-permute-start.3 = (f32[96,512]{1,0:T(8,128)S(1)}, f32[96,512]{1,0:T(8,128)S(1)}, u32[]{:S(2)}, u32[]{:S(2)}) collective-permute-start(f32[96,512]{1,0:T(8,128)S(1)} %add.98), channel_id=1, source_target_pairs={{0,1},{1,2},{2,3},{3,4},{4,5},{5,6},{6,7},{7,0},{8,9},{9,10},{10,1... | collective-permute-start | bytes 589832 | tf_op jit(solution)/shard_map/ppermute | solution.py:462
  45.3 2.1 %collective-permute-done.16 = f32[96,512]{1,0:T(8,128)S(1)} collective-permute-done((f32[96,512]{1,0:T(8,128)S(1)}, f32[96,512]{1,0:T(8,128)S(1)}, u32[]{:S(2)}, u32[]{:S(2)}) %collective-permute-start.16) | collective-permute-done | bytes 196640 | tf_op jit(solution)/shard_map/ppermute | solution.py:462
  47.4 0.2 collective-permute-done.20
  47.6 3.8 %collective-permute-start.21 = (f32[96,512]{1,0:T(8,128)S(1)}, f32[96,512]{1,0:T(8,128)S(1)}, u32[]{:S(2)}, u32[]{:S(2)}) collective-permute-start(f32[96,512]{1,0:T(8,128)S(1)} %add_add_fusion.refs_5_.refs_1_), channel_id=1, source_target_pairs={{0,7},{1,0},{2,1},{3,2},{4,3},{5,4},{6,5},{7,6},{8,15},{9,8},{10,9... | collective-permute-start | bytes 589832 | tf_op jit(solution)/shard_map/ppermute | solution.py:462
  51.4 1.3 collective-permute-start.10
  52.7 0.3 collective-permute-start.25
  53.0 3.0 %collective-permute-start.7 = (f32[96,512]{1,0:T(8,128)S(1)}, f32[96,512]{1,0:T(8,128)S(1)}, u32[]{:S(2)}, u32[]{:S(2)}) collective-permute-start(f32[96,512]{1,0:T(8,128)S(1)} %add_add_fusion.1.refs_0_), channel_id=1, source_target_pairs={{0,7},{1,0},{2,1},{3,2},{4,3},{5,4},{6,5},{7,6},{8,15},{9,8},{10,9... | collective-permute-start | bytes 589832 | tf_op jit(solution)/shard_map/ppermute | solution.py:462
  56.0 0.0 collective-permute-done.21.refs_6_
  56.0 3.7 %collective-permute-start.22 = (f32[96,512]{1,0:T(8,128)S(1)}, f32[96,512]{1,0:T(8,128)S(1)}, u32[]{:S(2)}, u32[]{:S(2)}) collective-permute-start(f32[96,512]{1,0:T(8,128)S(1)} %collective-permute-done.21.refs_6_), channel_id=1, source_target_pairs={{0,7},{1,0},{2,1},{3,2},{4,3},{5,4},{6,5},{7,6},{8,15},{9,8},{10,9... | collective-permute-start | bytes 589832 | tf_op jit(solution)/shard_map/ppermute | solution.py:462
  59.7 0.6 collective-permute-done.10.refs_4_
  60.3 0.2 collective-permute-start.11
  60.5 4.0 %collective-permute-done.25.refs_9_ = f32[96,512]{1,0:T(8,128)S(1)} collective-permute-done((f32[96,512]{1,0:T(8,128)S(1)}, f32[96,512]{1,0:T(8,128)S(1)}, u32[]{:S(2)}, u32[]{:S(2)}) %collective-permute-start.25) | collective-permute-done | bytes 196640 | tf_op jit(solution)/shard_map/ppermute | solution.py:462
  64.5 0.2 collective-permute-start.26
  64.7 3.0 %collective-permute-start.8 = (f32[96,512]{1,0:T(8,128)S(1)}, f32[96,512]{1,0:T(8,128)S(1)}, u32[]{:S(2)}, u32[]{:S(2)}) collective-permute-start(f32[96,512]{1,0:T(8,128)S(1)} %collective-permute-done.7.refs_1_), channel_id=1, source_target_pairs={{0,7},{1,0},{2,1},{3,2},{4,3},{5,4},{6,5},{7,6},{8,15},{9,8},{10,9... | collective-permute-start | bytes 589832 | tf_op jit(solution)/shard_map/ppermute | solution.py:462
  67.7 1.0 collective-permute-start.23
  68.7 0.6 collective-permute-done.11.refs_3_
  69.3 0.5 collective-permute-start.12
  69.8 3.7 %collective-permute-done.26.refs_8_ = f32[96,512]{1,0:T(8,128)S(1)} collective-permute-done((f32[96,512]{1,0:T(8,128)S(1)}, f32[96,512]{1,0:T(8,128)S(1)}, u32[]{:S(2)}, u32[]{:S(2)}) %collective-permute-start.26) | collective-permute-done | bytes 196640 | tf_op jit(solution)/shard_map/ppermute | solution.py:462
  73.5 3.2 %collective-permute-start.9 = (f32[96,512]{1,0:T(8,128)S(1)}, f32[96,512]{1,0:T(8,128)S(1)}, u32[]{:S(2)}, u32[]{:S(2)}) collective-permute-start(f32[96,512]{1,0:T(8,128)S(1)} %collective-permute-done.8.refs_2_), channel_id=1, source_target_pairs={{0,7},{1,0},{2,1},{3,2},{4,3},{5,4},{6,5},{7,6},{8,15},{9,8},{10,9... | collective-permute-start | bytes 589832 | tf_op jit(solution)/shard_map/ppermute | solution.py:462
  76.7 3.1 %collective-permute-start.24 = (f32[96,512]{1,0:T(8,128)S(1)}, f32[96,512]{1,0:T(8,128)S(1)}, u32[]{:S(2)}, u32[]{:S(2)}) collective-permute-start(f32[96,512]{1,0:T(8,128)S(1)} %collective-permute-done.23.refs_3_), channel_id=1, source_target_pairs={{0,7},{1,0},{2,1},{3,2},{4,3},{5,4},{6,5},{7,6},{8,15},{9,8},{10,9... | collective-permute-start | bytes 589832 | tf_op jit(solution)/shard_map/ppermute | solution.py:462
  79.8 2.9 %split_near.1 = (bf16[10,384,256]{2,1,0:T(8,128)(2,1)S(1)}, f32[192,192]{1,0:T(8,128)S(1)}) custom-call(f32[96,512]{1,0:T(8,128)S(1)} %add_add_fusion.1.refs_0_, f32[96,512]{1,0:T(8,128)S(1)} %collective-permute-done.7.refs_1_, f32[96,512]{1,0:T(8,128)S(1)} %collective-permute-done.8.refs_2_, f32[96,512]{1,0:T(8,128)S(1)} %collective-permute-done.11.refs_3_, ...), custom_call_target="tpu_custom_call" | custom-call | tf_op jit(solution)/shard_map/split_near/pallas_call | solution.py:263
  82.7 6.1 %adjoint_near.1.refs_0_ = f32[16,192,256]{2,1,0:T(8,128)S(1)} custom-call(s32[96]{0:T(128)S(1)} %get-tuple-element.31.near_ref.list_ref, s32[2,96]{1,0:T(2,128)S(1)} %bitcast.22, s32[2]{0:T(128)S(1)} %get-tuple-element.32.count_ref, s32[1]{0:T(128)} %bitcast.1.index_ref, bf16[96,256,256]{2,1,0:T(8,128)(2,1)S(1)} %get-tuple-element.34.buf_ref, ...), custom_call_target="tpu_custom_call" | custom-call | tf_op jit(solution)/shard_map/adjoint_near/pallas_call | solution.py:338
  88.9 1.9 %split_far.1 = (bf16[6,384,256]{2,1,0:T(8,128)(2,1)S(1)}, f32[192,128]{1,0:T(8,128)S(1)}) custom-call(f32[96,512]{1,0:T(8,128)S(1)} %collective-permute-done.9.refs_0_, f32[96,512]{1,0:T(8,128)S(1)} %collective-permute-done.13.refs_1_, f32[96,512]{1,0:T(8,128)S(1)} %collective-permute-done.12.refs_2_, f32[96,512]{1,0:T(8,128)S(1)} %collective-permute-done.23.refs_3_, ...), custom_call_target="tpu_custom_call" | custom-call | tf_op jit(solution)/shard_map/split_far/pallas_call | solution.py:263
  90.7 4.6 %adjoint_far.1 = (f32[16,192,128]{2,1,0:T(8,128)S(1)}, f32[16,192,128]{2,1,0:T(8,128)S(1)}) custom-call(s32[96]{0:T(128)S(1)} %get-tuple-element.51.list_ref, s32[2,96]{1,0:T(2,128)S(1)} %bitcast.23, s32[2]{0:T(128)S(1)} %get-tuple-element.32.count_ref, s32[1]{0:T(128)} %bitcast.1.index_ref, bf16[96,256,256]{2,1,0:T(8,128)(2,1)S(1)} %get-tuple-element.34.buf_ref, ...), custom_call_target="tpu_custom_call" | custom-call | tf_op jit(solution)/shard_map/adjoint_far/pallas_call | solution.py:338
  95.3 0.3 collective-permute-start.35
  95.7 0.5 collective-permute-start.28
  96.2 3.0 %collective-permute-done.28 = f32[192,128]{1,0:T(8,128)S(1)} collective-permute-done((f32[192,128]{1,0:T(8,128)S(1)}, f32[192,128]{1,0:T(8,128)S(1)}, u32[]{:S(2)}, u32[]{:S(2)}) %collective-permute-start.28) | collective-permute-done | bytes 98336 | tf_op jit(solution)/shard_map/ppermute | solution.py:462
  99.2 2.3 %collective-permute-start.29 = (f32[192,128]{1,0:T(8,128)S(1)}, f32[192,128]{1,0:T(8,128)S(1)}, u32[]{:S(2)}, u32[]{:S(2)}) collective-permute-start(f32[192,128]{1,0:T(8,128)S(1)} %add.110), channel_id=1, source_target_pairs={{0,128},{8,40},{16,144},{24,56},{32,160},{40,8},{48,176},{56,24},{... | collective-permute-start | bytes 294920 | tf_op jit(solution)/shard_map/ppermute | solution.py:505
  101.5 0.2 add.117
  101.7 0.1 fusion.5
  101.8 1.4 %collective-permute-start.36 = (f32[4,192,128]{2,1,0:T(8,128)S(1)}, f32[4,192,128]{2,1,0:T(8,128)S(1)}, u32[]{:S(2)}, u32[]{:S(2)}) collective-permute-start(f32[4,192,128]{2,1,0:T(8,128)S(1)} %get-tuple-element.56), channel_id=1, source_target_pairs={{0,128},{8,40},{16,144},{24,56},{32,160},{40,8},{48,176},{56,24},{... | collective-permute-start | bytes 1179656 | tf_op jit(solution)/shard_map/ppermute | solution.py:505
  103.2 0.6 collective-permute-start.37
  103.8 1.4 %collective-permute-start.38 = (f32[4,192,128]{2,1,0:T(8,128)S(1)}, f32[4,192,128]{2,1,0:T(8,128)S(1)}, u32[]{:S(2)}, u32[]{:S(2)}) collective-permute-start(f32[4,192,128]{2,1,0:T(8,128)S(1)} %get-tuple-element.57), channel_id=1, source_target_pairs={{0,192},{8,56},{16,208},{24,8},{32,224},{40,24},{48,240},{56,40},{... | collective-permute-start | bytes 1179656 | tf_op jit(solution)/shard_map/ppermute | solution.py:505
  105.2 0.7 collective-permute-start.30
  106.0 2.4 %collective-permute-start.31 = (f32[192,128]{1,0:T(8,128)S(1)}, f32[192,128]{1,0:T(8,128)S(1)}, u32[]{:S(2)}, u32[]{:S(2)}) collective-permute-start(f32[192,128]{1,0:T(8,128)S(1)} %add.110), channel_id=1, source_target_pairs={{0,192},{8,56},{16,208},{24,8},{32,224},{40,24},{48,240},{56,40},{... | collective-permute-start | bytes 294920 | tf_op jit(solution)/shard_map/ppermute | solution.py:505
  108.4 7.8 %collective-permute-done.30 = f32[192,128]{1,0:T(8,128)S(1)} collective-permute-done((f32[192,128]{1,0:T(8,128)S(1)}, f32[192,128]{1,0:T(8,128)S(1)}, u32[]{:S(2)}, u32[]{:S(2)}) %collective-permute-start.30) | collective-permute-done | bytes 98336 | tf_op jit(solution)/shard_map/ppermute | solution.py:505
  116.2 0.2 collective-permute-done.31
  116.4 1.7 %collective-permute-start.32 = (f32[192,128]{1,0:T(8,128)S(1)}, f32[192,128]{1,0:T(8,128)S(1)}, u32[]{:S(2)}, u32[]{:S(2)}) collective-permute-start(f32[192,128]{1,0:T(8,128)S(1)} %add_add_fusion.3), channel_id=1, source_target_pairs={{0,32},{8,136},{16,48},{24,152},{32,0},{40,168},{48,16},{56,184},{... | collective-permute-start | bytes 294920 | tf_op jit(solution)/shard_map/ppermute | solution.py:505
  118.2 3.2 %collective-permute-start.34 = (f32[192,128]{1,0:T(8,128)S(1)}, f32[192,128]{1,0:T(8,128)S(1)}, u32[]{:S(2)}, u32[]{:S(2)}) collective-permute-start(f32[192,128]{1,0:T(8,128)S(1)} %add_add_fusion.3), channel_id=1, source_target_pairs={{0,48},{8,200},{16,0},{24,216},{32,16},{40,232},{48,32},{56,248},{... | collective-permute-start | bytes 294920 | tf_op jit(solution)/shard_map/ppermute | solution.py:505
  121.4 0.1 fusion.1
  121.6 0.8 collective-permute-start.39
  122.3 0.9 collective-permute-start.40
  123.2 2.3 %collective-permute-start.41 = (f32[192,128]{1,0:T(8,128)S(1)}, f32[192,128]{1,0:T(8,128)S(1)}, u32[]{:S(2)}, u32[]{:S(2)}) collective-permute-start(f32[192,128]{1,0:T(8,128)S(1)} %get-tuple-element.60), channel_id=1, source_target_pairs={{0,48},{8,200},{16,0},{24,216},{32,16},{40,232},{48,32},{56,248},{... | collective-permute-start | bytes 294920 | tf_op jit(solution)/shard_map/ppermute | solution.py:505
  125.6 11.1 %factor.1.factor_ref = f32[192,192]{1,0:T(8,128)S(1)} custom-call(f32[192,128]{1,0:T(8,128)S(1)} %add_add_fusion.2.packed_ref), custom_call_target="tpu_custom_call" | custom-call | tf_op jit(solution)/shard_map/factor/pallas_call | solution.py:430
  136.7 1.2 shard_map.50
  138.0 1.0 shard_map.51
  (51 shorter events, 0.6 us)
Async XLA Ops:
  1.3 0.7 copy-start
  8.4 8.6 %collective-permute-start.17 = (f32[96,512]{1,0:T(8,128)S(1)}, f32[96,512]{1,0:T(8,128)S(1)}, u32[]{:S(2)}, u32[]{:S(2)}) collective-permute-start(f32[96,512]{1,0:T(8,128)S(1)} %get-tuple-element.44), channel_id=1, source_target_pairs={{0,7},{1,0},{2,1},{3,2},{4,3},{5,4},{6,5},{7,6},{8,15},{9,8},{10,9... | collective-permute-start | bytes 589832 | tf_op jit(solution)/shard_map/ppermute | solution.py:462
  13.7 13.4 %collective-permute-start = (f32[96,512]{1,0:T(8,128)S(1)}, f32[96,512]{1,0:T(8,128)S(1)}, u32[]{:S(2)}, u32[]{:S(2)}) collective-permute-start(f32[96,512]{1,0:T(8,128)S(1)} %get-tuple-element.29), channel_id=1, source_target_pairs={{0,1},{1,2},{2,3},{3,4},{4,5},{5,6},{6,7},{7,0},{8,9},{9,10},{10,1... | collective-permute-start | bytes 589832 | tf_op jit(solution)/shard_map/ppermute | solution.py:462
  13.7 14.9 %collective-permute-start.14 = (f32[96,512]{1,0:T(8,128)S(1)}, f32[96,512]{1,0:T(8,128)S(1)}, u32[]{:S(2)}, u32[]{:S(2)}) collective-permute-start(f32[96,512]{1,0:T(8,128)S(1)} %get-tuple-element.41), channel_id=1, source_target_pairs={{0,1},{1,2},{2,3},{3,4},{4,5},{5,6},{6,7},{7,0},{8,9},{9,10},{10,1... | collective-permute-start | bytes 589832 | tf_op jit(solution)/shard_map/ppermute | solution.py:462
  17.0 11.7 %collective-permute-start.18 = (f32[96,512]{1,0:T(8,128)S(1)}, f32[96,512]{1,0:T(8,128)S(1)}, u32[]{:S(2)}, u32[]{:S(2)}) collective-permute-start(f32[96,512]{1,0:T(8,128)S(1)} %add.105), channel_id=1, source_target_pairs={{0,7},{1,0},{2,1},{3,2},{4,3},{5,4},{6,5},{7,6},{8,15},{9,8},{10,9... | collective-permute-start | bytes 589832 | tf_op jit(solution)/shard_map/ppermute | solution.py:462
  20.8 11.3 %collective-permute-start.4 = (f32[96,512]{1,0:T(8,128)S(1)}, f32[96,512]{1,0:T(8,128)S(1)}, u32[]{:S(2)}, u32[]{:S(2)}) collective-permute-start(f32[96,512]{1,0:T(8,128)S(1)} %get-tuple-element.37), channel_id=1, source_target_pairs={{0,7},{1,0},{2,1},{3,2},{4,3},{5,4},{6,5},{7,6},{8,15},{9,8},{10,9... | collective-permute-start | bytes 589832 | tf_op jit(solution)/shard_map/ppermute | solution.py:462
  27.1 8.1 %collective-permute-start.1 = (f32[96,512]{1,0:T(8,128)S(1)}, f32[96,512]{1,0:T(8,128)S(1)}, u32[]{:S(2)}, u32[]{:S(2)}) collective-permute-start(f32[96,512]{1,0:T(8,128)S(1)} %add.96), channel_id=1, source_target_pairs={{0,1},{1,2},{2,3},{3,4},{4,5},{5,6},{6,7},{7,0},{8,9},{9,10},{10,1... | collective-permute-start | bytes 589832 | tf_op jit(solution)/shard_map/ppermute | solution.py:462
  28.6 10.8 %collective-permute-start.15 = (f32[96,512]{1,0:T(8,128)S(1)}, f32[96,512]{1,0:T(8,128)S(1)}, u32[]{:S(2)}, u32[]{:S(2)}) collective-permute-start(f32[96,512]{1,0:T(8,128)S(1)} %add.103), channel_id=1, source_target_pairs={{0,1},{1,2},{2,3},{3,4},{4,5},{5,6},{6,7},{7,0},{8,9},{9,10},{10,1... | collective-permute-start | bytes 589832 | tf_op jit(solution)/shard_map/ppermute | solution.py:462
  28.8 10.8 %collective-permute-start.19 = (f32[96,512]{1,0:T(8,128)S(1)}, f32[96,512]{1,0:T(8,128)S(1)}, u32[]{:S(2)}, u32[]{:S(2)}) collective-permute-start(f32[96,512]{1,0:T(8,128)S(1)} %add.106), channel_id=1, source_target_pairs={{0,7},{1,0},{2,1},{3,2},{4,3},{5,4},{6,5},{7,6},{8,15},{9,8},{10,9... | collective-permute-start | bytes 589832 | tf_op jit(solution)/shard_map/ppermute | solution.py:462
  32.1 10.8 %collective-permute-start.5 = (f32[96,512]{1,0:T(8,128)S(1)}, f32[96,512]{1,0:T(8,128)S(1)}, u32[]{:S(2)}, u32[]{:S(2)}) collective-permute-start(f32[96,512]{1,0:T(8,128)S(1)} %add.99), channel_id=1, source_target_pairs={{0,7},{1,0},{2,1},{3,2},{4,3},{5,4},{6,5},{7,6},{8,15},{9,8},{10,9... | collective-permute-start | bytes 589832 | tf_op jit(solution)/shard_map/ppermute | solution.py:462
  35.2 8.4 %collective-permute-start.2 = (f32[96,512]{1,0:T(8,128)S(1)}, f32[96,512]{1,0:T(8,128)S(1)}, u32[]{:S(2)}, u32[]{:S(2)}) collective-permute-start(f32[96,512]{1,0:T(8,128)S(1)} %add.97), channel_id=1, source_target_pairs={{0,1},{1,2},{2,3},{3,4},{4,5},{5,6},{6,7},{7,0},{8,9},{9,10},{10,1... | collective-permute-start | bytes 589832 | tf_op jit(solution)/shard_map/ppermute | solution.py:462
  39.4 7.9 %collective-permute-start.16 = (f32[96,512]{1,0:T(8,128)S(1)}, f32[96,512]{1,0:T(8,128)S(1)}, u32[]{:S(2)}, u32[]{:S(2)}) collective-permute-start(f32[96,512]{1,0:T(8,128)S(1)} %add.104), channel_id=1, source_target_pairs={{0,1},{1,2},{2,3},{3,4},{4,5},{5,6},{6,7},{7,0},{8,9},{9,10},{10,1... | collective-permute-start | bytes 589832 | tf_op jit(solution)/shard_map/ppermute | solution.py:462
  39.6 8.0 %collective-permute-start.20 = (f32[96,512]{1,0:T(8,128)S(1)}, f32[96,512]{1,0:T(8,128)S(1)}, u32[]{:S(2)}, u32[]{:S(2)}) collective-permute-start(f32[96,512]{1,0:T(8,128)S(1)} %add.107), channel_id=1, source_target_pairs={{0,7},{1,0},{2,1},{3,2},{4,3},{5,4},{6,5},{7,6},{8,15},{9,8},{10,9... | collective-permute-start | bytes 589832 | tf_op jit(solution)/shard_map/ppermute | solution.py:462
  42.9 8.5 %collective-permute-start.6 = (f32[96,512]{1,0:T(8,128)S(1)}, f32[96,512]{1,0:T(8,128)S(1)}, u32[]{:S(2)}, u32[]{:S(2)}) collective-permute-start(f32[96,512]{1,0:T(8,128)S(1)} %add.100), channel_id=1, source_target_pairs={{0,7},{1,0},{2,1},{3,2},{4,3},{5,4},{6,5},{7,6},{8,15},{9,8},{10,9... | collective-permute-start | bytes 589832 | tf_op jit(solution)/shard_map/ppermute | solution.py:462
  43.7 7.7 %collective-permute-start.3 = (f32[96,512]{1,0:T(8,128)S(1)}, f32[96,512]{1,0:T(8,128)S(1)}, u32[]{:S(2)}, u32[]{:S(2)}) collective-permute-start(f32[96,512]{1,0:T(8,128)S(1)} %add.98), channel_id=1, source_target_pairs={{0,1},{1,2},{2,3},{3,4},{4,5},{5,6},{6,7},{7,0},{8,9},{9,10},{10,1... | collective-permute-start | bytes 589832 | tf_op jit(solution)/shard_map/ppermute | solution.py:462
  47.6 8.4 %collective-permute-start.21 = (f32[96,512]{1,0:T(8,128)S(1)}, f32[96,512]{1,0:T(8,128)S(1)}, u32[]{:S(2)}, u32[]{:S(2)}) collective-permute-start(f32[96,512]{1,0:T(8,128)S(1)} %add_add_fusion.refs_5_.refs_1_), channel_id=1, source_target_pairs={{0,7},{1,0},{2,1},{3,2},{4,3},{5,4},{6,5},{7,6},{8,15},{9,8},{10,9... | collective-permute-start | bytes 589832 | tf_op jit(solution)/shard_map/ppermute | solution.py:462
  51.4 8.8 %collective-permute-start.10 = (f32[96,512]{1,0:T(8,128)S(1)}, f32[96,512]{1,0:T(8,128)S(1)}, u32[]{:S(2)}, u32[]{:S(2)}) collective-permute-start(f32[96,512]{1,0:T(8,128)S(1)} %add_add_fusion.1.refs_0_), channel_id=1, source_target_pairs={{0,1},{1,2},{2,3},{3,4},{4,5},{5,6},{6,7},{7,0},{8,9},{9,10},{10,1... | collective-permute-start | bytes 589832 | tf_op jit(solution)/shard_map/ppermute | solution.py:462
  52.7 11.8 %collective-permute-start.25 = (f32[96,512]{1,0:T(8,128)S(1)}, f32[96,512]{1,0:T(8,128)S(1)}, u32[]{:S(2)}, u32[]{:S(2)}) collective-permute-start(f32[96,512]{1,0:T(8,128)S(1)} %add_add_fusion.refs_5_.refs_1_), channel_id=1, source_target_pairs={{0,1},{1,2},{2,3},{3,4},{4,5},{5,6},{6,7},{7,0},{8,9},{9,10},{10,1... | collective-permute-start | bytes 589832 | tf_op jit(solution)/shard_map/ppermute | solution.py:462
  53.0 11.7 %collective-permute-start.7 = (f32[96,512]{1,0:T(8,128)S(1)}, f32[96,512]{1,0:T(8,128)S(1)}, u32[]{:S(2)}, u32[]{:S(2)}) collective-permute-start(f32[96,512]{1,0:T(8,128)S(1)} %add_add_fusion.1.refs_0_), channel_id=1, source_target_pairs={{0,7},{1,0},{2,1},{3,2},{4,3},{5,4},{6,5},{7,6},{8,15},{9,8},{10,9... | collective-permute-start | bytes 589832 | tf_op jit(solution)/shard_map/ppermute | solution.py:462
  56.0 11.7 %collective-permute-start.22 = (f32[96,512]{1,0:T(8,128)S(1)}, f32[96,512]{1,0:T(8,128)S(1)}, u32[]{:S(2)}, u32[]{:S(2)}) collective-permute-start(f32[96,512]{1,0:T(8,128)S(1)} %collective-permute-done.21.refs_6_), channel_id=1, source_target_pairs={{0,7},{1,0},{2,1},{3,2},{4,3},{5,4},{6,5},{7,6},{8,15},{9,8},{10,9... | collective-permute-start | bytes 589832 | tf_op jit(solution)/shard_map/ppermute | solution.py:462
  60.3 9.0 %collective-permute-start.11 = (f32[96,512]{1,0:T(8,128)S(1)}, f32[96,512]{1,0:T(8,128)S(1)}, u32[]{:S(2)}, u32[]{:S(2)}) collective-permute-start(f32[96,512]{1,0:T(8,128)S(1)} %collective-permute-done.10.refs_4_), channel_id=1, source_target_pairs={{0,1},{1,2},{2,3},{3,4},{4,5},{5,6},{6,7},{7,0},{8,9},{9,10},{10,1... | collective-permute-start | bytes 589832 | tf_op jit(solution)/shard_map/ppermute | solution.py:462
  64.5 9.0 %collective-permute-start.26 = (f32[96,512]{1,0:T(8,128)S(1)}, f32[96,512]{1,0:T(8,128)S(1)}, u32[]{:S(2)}, u32[]{:S(2)}) collective-permute-start(f32[96,512]{1,0:T(8,128)S(1)} %collective-permute-done.25.refs_9_), channel_id=1, source_target_pairs={{0,1},{1,2},{2,3},{3,4},{4,5},{5,6},{6,7},{7,0},{8,9},{9,10},{10,1... | collective-permute-start | bytes 589832 | tf_op jit(solution)/shard_map/ppermute | solution.py:462
  64.7 8.8 %collective-permute-start.8 = (f32[96,512]{1,0:T(8,128)S(1)}, f32[96,512]{1,0:T(8,128)S(1)}, u32[]{:S(2)}, u32[]{:S(2)}) collective-permute-start(f32[96,512]{1,0:T(8,128)S(1)} %collective-permute-done.7.refs_1_), channel_id=1, source_target_pairs={{0,7},{1,0},{2,1},{3,2},{4,3},{5,4},{6,5},{7,6},{8,15},{9,8},{10,9... | collective-permute-start | bytes 589832 | tf_op jit(solution)/shard_map/ppermute | solution.py:462
  67.7 9.0 %collective-permute-start.23 = (f32[96,512]{1,0:T(8,128)S(1)}, f32[96,512]{1,0:T(8,128)S(1)}, u32[]{:S(2)}, u32[]{:S(2)}) collective-permute-start(f32[96,512]{1,0:T(8,128)S(1)} %collective-permute-done.22.refs_7_), channel_id=1, source_target_pairs={{0,7},{1,0},{2,1},{3,2},{4,3},{5,4},{6,5},{7,6},{8,15},{9,8},{10,9... | collective-permute-start | bytes 589832 | tf_op jit(solution)/shard_map/ppermute | solution.py:462
  69.3 10.5 %collective-permute-start.12 = (f32[96,512]{1,0:T(8,128)S(1)}, f32[96,512]{1,0:T(8,128)S(1)}, u32[]{:S(2)}, u32[]{:S(2)}) collective-permute-start(f32[96,512]{1,0:T(8,128)S(1)} %collective-permute-done.11.refs_3_), channel_id=1, source_target_pairs={{0,1},{1,2},{2,3},{3,4},{4,5},{5,6},{6,7},{7,0},{8,9},{9,10},{10,1... | collective-permute-start | bytes 589832 | tf_op jit(solution)/shard_map/ppermute | solution.py:462
  73.5 15.3 %collective-permute-start.27 = (f32[96,512]{1,0:T(8,128)S(1)}, f32[96,512]{1,0:T(8,128)S(1)}, u32[]{:S(2)}, u32[]{:S(2)}) collective-permute-start(f32[96,512]{1,0:T(8,128)S(1)} %collective-permute-done.26.refs_8_), channel_id=1, source_target_pairs={{0,1},{1,2},{2,3},{3,4},{4,5},{5,6},{6,7},{7,0},{8,9},{9,10},{10,1... | collective-permute-start | bytes 589832 | tf_op jit(solution)/shard_map/ppermute | solution.py:462
  73.5 15.3 %collective-permute-start.9 = (f32[96,512]{1,0:T(8,128)S(1)}, f32[96,512]{1,0:T(8,128)S(1)}, u32[]{:S(2)}, u32[]{:S(2)}) collective-permute-start(f32[96,512]{1,0:T(8,128)S(1)} %collective-permute-done.8.refs_2_), channel_id=1, source_target_pairs={{0,7},{1,0},{2,1},{3,2},{4,3},{5,4},{6,5},{7,6},{8,15},{9,8},{10,9... | collective-permute-start | bytes 589832 | tf_op jit(solution)/shard_map/ppermute | solution.py:462
  76.7 12.1 %collective-permute-start.24 = (f32[96,512]{1,0:T(8,128)S(1)}, f32[96,512]{1,0:T(8,128)S(1)}, u32[]{:S(2)}, u32[]{:S(2)}) collective-permute-start(f32[96,512]{1,0:T(8,128)S(1)} %collective-permute-done.23.refs_3_), channel_id=1, source_target_pairs={{0,7},{1,0},{2,1},{3,2},{4,3},{5,4},{6,5},{7,6},{8,15},{9,8},{10,9... | collective-permute-start | bytes 589832 | tf_op jit(solution)/shard_map/ppermute | solution.py:462
  79.8 9.0 %collective-permute-start.13 = (f32[96,512]{1,0:T(8,128)S(1)}, f32[96,512]{1,0:T(8,128)S(1)}, u32[]{:S(2)}, u32[]{:S(2)}) collective-permute-start(f32[96,512]{1,0:T(8,128)S(1)} %collective-permute-done.12.refs_2_), channel_id=1, source_target_pairs={{0,1},{1,2},{2,3},{3,4},{4,5},{5,6},{6,7},{7,0},{8,9},{9,10},{10,1... | collective-permute-start | bytes 589832 | tf_op jit(solution)/shard_map/ppermute | solution.py:462
  95.3 6.2 %collective-permute-start.35 = (f32[16,192,128]{2,1,0:T(8,128)S(1)}, f32[16,192,128]{2,1,0:T(8,128)S(1)}, u32[]{:S(2)}, u32[]{:S(2)}) collective-permute-start(f32[16,192,128]{2,1,0:T(8,128)S(1)} %get-tuple-element.55), channel_id=1, source_target_pairs={{0,8},{8,0},{1,9},{9,1},{2,10},{10,2},{3,11},{11,3},{4,12},{12,4},... | collective-permute-start | bytes 4718600 | tf_op jit(solution)/shard_map/ppermute | solution.py:462
  95.7 3.5 %collective-permute-start.28 = (f32[192,128]{1,0:T(8,128)S(1)}, f32[192,128]{1,0:T(8,128)S(1)}, u32[]{:S(2)}, u32[]{:S(2)}) collective-permute-start(f32[192,128]{1,0:T(8,128)S(1)} %get-tuple-element.50), channel_id=1, source_target_pairs={{0,8},{8,0},{1,9},{9,1},{2,10},{10,2},{3,11},{11,3},{4,12},{12,4},... | collective-permute-start | bytes 294920 | tf_op jit(solution)/shard_map/ppermute | solution.py:462
  99.2 6.8 %collective-permute-start.29 = (f32[192,128]{1,0:T(8,128)S(1)}, f32[192,128]{1,0:T(8,128)S(1)}, u32[]{:S(2)}, u32[]{:S(2)}) collective-permute-start(f32[192,128]{1,0:T(8,128)S(1)} %add.110), channel_id=1, source_target_pairs={{0,128},{8,40},{16,144},{24,56},{32,160},{40,8},{48,176},{56,24},{... | collective-permute-start | bytes 294920 | tf_op jit(solution)/shard_map/ppermute | solution.py:505
  101.8 16.4 %collective-permute-start.36 = (f32[4,192,128]{2,1,0:T(8,128)S(1)}, f32[4,192,128]{2,1,0:T(8,128)S(1)}, u32[]{:S(2)}, u32[]{:S(2)}) collective-permute-start(f32[4,192,128]{2,1,0:T(8,128)S(1)} %get-tuple-element.56), channel_id=1, source_target_pairs={{0,128},{8,40},{16,144},{24,56},{32,160},{40,8},{48,176},{56,24},{... | collective-permute-start | bytes 1179656 | tf_op jit(solution)/shard_map/ppermute | solution.py:505
  103.2 18.2 %collective-permute-start.37 = (f32[4,192,128]{2,1,0:T(8,128)S(1)}, f32[4,192,128]{2,1,0:T(8,128)S(1)}, u32[]{:S(2)}, u32[]{:S(2)}) collective-permute-start(f32[4,192,128]{2,1,0:T(8,128)S(1)} %get-tuple-element.58), channel_id=1, source_target_pairs={{0,64},{8,24},{16,80},{24,40},{32,96},{40,56},{48,112},{56,8},{64,... | collective-permute-start | bytes 1179656 | tf_op jit(solution)/shard_map/ppermute | solution.py:505
  103.8 17.6 %collective-permute-start.38 = (f32[4,192,128]{2,1,0:T(8,128)S(1)}, f32[4,192,128]{2,1,0:T(8,128)S(1)}, u32[]{:S(2)}, u32[]{:S(2)}) collective-permute-start(f32[4,192,128]{2,1,0:T(8,128)S(1)} %get-tuple-element.57), channel_id=1, source_target_pairs={{0,192},{8,56},{16,208},{24,8},{32,224},{40,24},{48,240},{56,40},{... | collective-permute-start | bytes 1179656 | tf_op jit(solution)/shard_map/ppermute | solution.py:505
  105.2 11.0 %collective-permute-start.30 = (f32[192,128]{1,0:T(8,128)S(1)}, f32[192,128]{1,0:T(8,128)S(1)}, u32[]{:S(2)}, u32[]{:S(2)}) collective-permute-start(f32[192,128]{1,0:T(8,128)S(1)} %add.110), channel_id=1, source_target_pairs={{0,64},{8,24},{16,80},{24,40},{32,96},{40,56},{48,112},{56,8},{64,... | collective-permute-start | bytes 294920 | tf_op jit(solution)/shard_map/ppermute | solution.py:505
  106.0 10.4 %collective-permute-start.31 = (f32[192,128]{1,0:T(8,128)S(1)}, f32[192,128]{1,0:T(8,128)S(1)}, u32[]{:S(2)}, u32[]{:S(2)}) collective-permute-start(f32[192,128]{1,0:T(8,128)S(1)} %add.110), channel_id=1, source_target_pairs={{0,192},{8,56},{16,208},{24,8},{32,224},{40,24},{48,240},{56,40},{... | collective-permute-start | bytes 294920 | tf_op jit(solution)/shard_map/ppermute | solution.py:505
  116.4 6.8 %collective-permute-start.32 = (f32[192,128]{1,0:T(8,128)S(1)}, f32[192,128]{1,0:T(8,128)S(1)}, u32[]{:S(2)}, u32[]{:S(2)}) collective-permute-start(f32[192,128]{1,0:T(8,128)S(1)} %add_add_fusion.3), channel_id=1, source_target_pairs={{0,32},{8,136},{16,48},{24,152},{32,0},{40,168},{48,16},{56,184},{... | collective-permute-start | bytes 294920 | tf_op jit(solution)/shard_map/ppermute | solution.py:505
  118.2 7.4 %collective-permute-start.33 = (f32[192,128]{1,0:T(8,128)S(1)}, f32[192,128]{1,0:T(8,128)S(1)}, u32[]{:S(2)}, u32[]{:S(2)}) collective-permute-start(f32[192,128]{1,0:T(8,128)S(1)} %add_add_fusion.3), channel_id=1, source_target_pairs={{0,16},{8,72},{16,32},{24,88},{32,48},{40,104},{48,0},{56,120},{64... | collective-permute-start | bytes 294920 | tf_op jit(solution)/shard_map/ppermute | solution.py:505
  118.2 7.4 %collective-permute-start.34 = (f32[192,128]{1,0:T(8,128)S(1)}, f32[192,128]{1,0:T(8,128)S(1)}, u32[]{:S(2)}, u32[]{:S(2)}) collective-permute-start(f32[192,128]{1,0:T(8,128)S(1)} %add_add_fusion.3), channel_id=1, source_target_pairs={{0,48},{8,200},{16,0},{24,216},{32,16},{40,232},{48,32},{56,248},{... | collective-permute-start | bytes 294920 | tf_op jit(solution)/shard_map/ppermute | solution.py:505
  121.6 16.4 %collective-permute-start.39 = (f32[192,128]{1,0:T(8,128)S(1)}, f32[192,128]{1,0:T(8,128)S(1)}, u32[]{:S(2)}, u32[]{:S(2)}) collective-permute-start(f32[192,128]{1,0:T(8,128)S(1)} %get-tuple-element.59), channel_id=1, source_target_pairs={{0,32},{8,136},{16,48},{24,152},{32,0},{40,168},{48,16},{56,184},{... | collective-permute-start | bytes 294920 | tf_op jit(solution)/shard_map/ppermute | solution.py:505
  122.3 15.6 %collective-permute-start.40 = (f32[192,128]{1,0:T(8,128)S(1)}, f32[192,128]{1,0:T(8,128)S(1)}, u32[]{:S(2)}, u32[]{:S(2)}) collective-permute-start(f32[192,128]{1,0:T(8,128)S(1)} %get-tuple-element.61), channel_id=1, source_target_pairs={{0,16},{8,72},{16,32},{24,88},{32,48},{40,104},{48,0},{56,120},{64... | collective-permute-start | bytes 294920 | tf_op jit(solution)/shard_map/ppermute | solution.py:505
  123.2 14.7 %collective-permute-start.41 = (f32[192,128]{1,0:T(8,128)S(1)}, f32[192,128]{1,0:T(8,128)S(1)}, u32[]{:S(2)}, u32[]{:S(2)}) collective-permute-start(f32[192,128]{1,0:T(8,128)S(1)} %get-tuple-element.60), channel_id=1, source_target_pairs={{0,48},{8,200},{16,0},{24,216},{32,16},{40,232},{48,32},{56,248},{... | collective-permute-start | bytes 294920 | tf_op jit(solution)/shard_map/ppermute | solution.py:505

commit v3 on v2

--- a/solution.py
+++ b/solution.py
@@ -57,33 +57,12 @@
     return jnp.clip(jnp.where(i >= 12, i - 6, i), 0, 2 * len(NEAR) - 1)
 
 
-def sketch_tiles(steps, total, slot_at, coords_ref, z, omega_ref, buf_ref, acc_ref, dists, ready):
-    def work(step, carry):
-        carry = ready(slot_at(step * UNROLL + UNROLL - 1), carry)
-        for t in range(UNROLL):
-            rank = step * UNROLL + t
-            slot = slot_at(rank)
-            i = place_of(relative_row(coords_ref, slot, z), dists)
-            i = jnp.where(rank < total, i, 2 * len(dists))
-            acc_ref[i] += dot_nt(omega_ref[coords_ref[1, slot]], buf_ref[slot])
-        return carry
-
-    return lax.fori_loop(0, steps, work, 0)
-
-
-def store_parts(outs, acc_ref, n):
-    for c in range(n):
-        for half in range(2):
-            for e in range(2):
-                outs[half * n + c][:, e * TB : (e + 1) * TB] = acc_ref[
-                    2 * c + e, half * KH : (half + 1) * KH, :
-                ]
-
-
-def sketch_far_body(coords_ref, live_ref, index_ref, tiles_ref, *refs):
-    n = len(FAR)
-    outs = refs[: 2 * n]
-    omega_ref, buf_ref, near_ref, far_ref, count_ref, acc_ref, sems = refs[2 * n :]
+AHEAD = 6
+
+
+def sketch_body(coords_ref, live_ref, index_ref, tiles_ref, *refs):
+    outs = refs[: 2 * NZ]
+    buf_ref, near_ref, far_ref, count_ref, omega_ref, acc_ref, sems = refs[2 * NZ :]
     batches = (live_ref[0] + SLOTS - 1) >> 3
     z = place_on_mesh(index_ref)[3]
 
@@ -95,11 +74,7 @@
         copy(batch).start()
         return carry
 
-    def land(batch, carry):
-        copy(batch).wait()
-        return carry
-
-    lax.fori_loop(0, batches, fetch, 0)
+    lax.fori_loop(0, jnp.minimum(batches, AHEAD), fetch, 0)
     k_ids = lax.broadcasted_iota(jnp.int32, (K, TB), 0)
     g_ids = lax.broadcasted_iota(jnp.int32, (K, TB), 1)
     base = g_ids * K + k_ids
@@ -111,6 +86,7 @@
         h = h * 1103515245 + 12345
         h = h ^ (h >> 13)
         omega_ref[j] = (1 - 2 * ((h >> 9) & 1)).astype(jnp.float32).astype(jnp.bfloat16)
+        acc_ref[j] = jnp.zeros((K, TB), jnp.float32)
         near, far = found
         for t in range(NT // CT):
             slot = j * (NT // CT) + t
@@ -126,87 +102,49 @@
     near, far = lax.fori_loop(0, CT, fill, (jnp.int32(0), jnp.int32(0)))
     count_ref[0] = near
     count_ref[1] = far
-    acc_ref[...] = jnp.zeros(acc_ref.shape, jnp.float32)
-
-    def slot_at(rank):
-        return far_ref[jnp.minimum(rank, far - 1)]
-
-    def ready(slot, landed):
-        upto = (slot >> 3) + 1
-        lax.fori_loop(landed, upto, land, 0)
-        return upto
-
-    steps = (far + UNROLL - 1) >> 2
-    landed = sketch_tiles(
-        steps, far, slot_at, coords_ref, z, omega_ref, buf_ref, acc_ref, FAR, ready
-    )
-    store_parts(outs, acc_ref, n)
-    lax.fori_loop(landed, batches, land, 0)
-
-
-def sketch_near_body(coords_ref, index_ref, near_ref, count_ref, omega_ref, buf_ref, *refs):
-    n = len(NEAR)
-    outs, acc_ref = refs[: 2 * n], refs[2 * n]
-    total = count_ref[0]
-    z = place_on_mesh(index_ref)[3]
-    acc_ref[...] = jnp.zeros(acc_ref.shape, jnp.float32)
-
-    def slot_at(rank):
-        return near_ref[jnp.minimum(rank, total - 1)]
-
-    steps = (total + UNROLL - 1) >> 2
-    sketch_tiles(
-        steps, total, slot_at, coords_ref, z, omega_ref, buf_ref, acc_ref, NEAR, lambda _, c: c
-    )
-    store_parts(outs, acc_ref, n)
-
-
-def sketch_near_call(coords, index, near, count, omega, held, shape, limit):
-    m = len(NEAR)
-    return pl.pallas_call(
-        sketch_near_body,
-        name="sketch_near",
-        in_specs=[SMEM_SPEC] * 4 + [VMEM_SPEC] * 2,
-        out_specs=[VMEM_SPEC] * (2 * m),
-        scratch_shapes=[pltpu.VMEM((2 * m + 1, K, TB), jnp.float32)],
-        out_shape=[shape] * (2 * m),
-        compiler_params=limit,
-    )(coords, index, near, count, omega, held)
-
-
-def sketch_calls(coords, live, index, tiles):
-    shape = jax.ShapeDtypeStruct((KH, CH), jnp.float32)
-    limit = pltpu.CompilerParams(vmem_limit_bytes=24 << 20)
-    n = len(FAR)
+
+    def work(batch, carry):
+        @pl.when(batch + AHEAD < batches)
+        def _():
+            copy(batch + AHEAD).start()
+
+        copy(batch).wait()
+        for t in range(SLOTS):
+            slot = batch * SLOTS + t
+            i = jnp.where(slot < live_ref[0], relative_row(coords_ref, slot, z), RT)
+            acc_ref[i] += dot_nt(omega_ref[coords_ref[1, slot]], buf_ref[slot])
+        return carry
+
+    lax.fori_loop(0, batches, work, 0)
+    for d in range(NZ):
+        for half in range(2):
+            for e in range(2):
+                outs[half * NZ + d][:, e * TB : (e + 1) * TB] = acc_ref[
+                    2 * d + e, half * KH : (half + 1) * KH, :
+                ]
+
+
+def sketch_call(coords, live, index, tiles):
     got = pl.pallas_call(
-        sketch_far_body,
-        name="sketch_far",
+        sketch_body,
+        name="sketch",
         in_specs=[SMEM_SPEC] * 3 + [HBM_SPEC],
-        out_specs=[VMEM_SPEC] * (2 * n + 2) + [SMEM_SPEC] * 3,
+        out_specs=[VMEM_SPEC] * (2 * NZ + 1) + [SMEM_SPEC] * 3,
         scratch_shapes=[
-            pltpu.VMEM((2 * n + 1, K, TB), jnp.float32),
+            pltpu.VMEM((CT, K, TB), jnp.bfloat16),
+            pltpu.VMEM((RT + 1, K, TB), jnp.float32),
             pltpu.SemaphoreType.DMA((STEPS,)),
         ],
-        out_shape=[shape] * (2 * n)
+        out_shape=[jax.ShapeDtypeStruct((KH, CH), jnp.float32)] * (2 * NZ)
         + [
-            jax.ShapeDtypeStruct((CT, K, TB), jnp.bfloat16),
             jax.ShapeDtypeStruct((NT, TB, TB), jnp.bfloat16),
             jax.ShapeDtypeStruct((NT,), jnp.int32),
             jax.ShapeDtypeStruct((NT,), jnp.int32),
             jax.ShapeDtypeStruct((2,), jnp.int32),
         ],
-        compiler_params=limit,
+        compiler_params=pltpu.CompilerParams(vmem_limit_bytes=24 << 20),
     )(coords, live, index, tiles)
-    omega, held, near, far, count = got[2 * n :]
-    rest = sketch_near_call(coords, index, near, count, omega, held, shape, limit)
-    m = len(NEAR)
-    parts = [[None] * NZ for _ in range(2)]
-    for half in range(2):
-        for c, d in enumerate(FAR):
-            parts[half][d] = got[half * n + c]
-        for c, d in enumerate(NEAR):
-            parts[half][d] = rest[half * m + c]
-    return parts, held, near, far, count
+    return [got[:NZ], got[NZ : 2 * NZ]], *got[2 * NZ :]
 
 
 def split_body(*refs, n, last):
@@ -516,7 +454,7 @@
     index = lax.axis_index(("x", "y", "core", "z")).astype(jnp.int32).reshape(1)
     coords = tile_coords.T
     tiles = pltpu.with_memory_space_constraint(tiles, pltpu.HBM)
-    parts, held, near_slots, far_slots, count = sketch_calls(coords, live_counts, index, tiles)
+    parts, held, near_slots, far_slots, count = sketch_call(coords, live_counts, index, tiles)
     own = reduce_z(parts)
     found = gather_z(own)
     near = [got[d] for got in found for d in NEAR]

time: 141 us -> 144 us (1.021)
  waiting for transfers between devices: 32.7 us -> 36.1 us
  Pallas kernels: 40.5 us -> 37.7 us
  starting transfers between devices: 62.7 us -> 65 us
    pallas_call x2 -> x1, Pallas kernels: 11.7 us -> 8.9 us  [sketch_call(): pl.pallas_call(sketch_body, name='sketch', in_specs=[SMEM_SPEC] * 3 + [HB...]
    ppermute x12, waiting for transfers between devices: 8.04 us -> 9.86 us  [shift_xy(): return lax.ppermute(x, ('x', 'y', 'core'), pairs)]
    ppermute x30, waiting for transfers between devices: 24.7 us -> 26.3 us  [shift(): return lax.ppermute(x, axis, [(i, (i + by) % size) for i in range(size)])]
    ppermute x30, starting transfers between devices: 44.8 us -> 46.3 us  [shift(): return lax.ppermute(x, axis, [(i, (i + by) % size) for i in range(size)])]
  transfers between devices with their start and end apart: 42 -> 42, of which waited for: 13 -> 17; matrix products, arithmetic and copies ran while one was open for 1% -> 1% of each run, Pallas kernels for 19% -> 15%
where the time goes in v3:
time: 144 us; the launch traced here: 142 us
  starting transfers between devices  65 us (45%)
  Pallas kernels  37.7 us (26%)
  waiting for transfers between devices  36.1 us (25%)
  between operations  1.56 us (1%)
    ppermute x30, starting transfers between devices, shift(): return lax.ppermute(x, axis, [(i, (i + by) % size) for i in range(size)])  46.3 us
    ppermute x30, waiting for transfers between devices, shift(): return lax.ppermute(x, axis, [(i, (i + by) % size) for i in range(size)])  26.3 us
    ppermute x12, starting transfers between devices, shift_xy(): return lax.ppermute(x, ('x', 'y', 'core'), pairs)  18.7 us
    pallas_call x1, Pallas kernels, factor_call(): pl.pallas_call(functools.partial(factor_body, scale=scale), name='factor'...  11.1 us
    pallas_call x2, Pallas kernels, adjoint_call(): pl.pallas_call(functools.partial(adjoint_body, dists=dists, last=last), n...  10.8 us
    ppermute x12, waiting for transfers between devices, shift_xy(): return lax.ppermute(x, ('x', 'y', 'core'), pairs)  9.86 us
    pallas_call x1, Pallas kernels, sketch_call(): pl.pallas_call(sketch_body, name='sketch', in_specs=[SMEM_SPEC] * 3 + [HB...  8.9 us
    pallas_call x2, Pallas kernels, split_call(): pl.pallas_call(functools.partial(split_body, n=n, last=bool(carried)), na...  4.74 us
  transfers between devices with their start and end apart: 42, of which 17 were waited for; matrix products, arithmetic and copies ran while one was open for 1% of the time, Pallas kernels for 15%

profile of v3, /device:TPU:2, one launch (start us, length us, event | category | flops | bytes accessed | tf_op | source)
XLA Modules:
  0.0 141.9 jit_solution(13151597407141921362)
XLA Ops:
  1.3 0.7 copy-done
  2.0 8.9 %sketch.1 = (f32[96,512]{1,0:T(8,128)S(1)}, f32[96,512]{1,0:T(8,128)S(1)}, f32[96,512]{1,0:T(8,128)S(1)}, f32[96,512]{1,0:T(8,128)S(1)}, f32[96,512]{1,0:T(8,128...) custom-call(s32[2,96]{1,0:T(2,128)S(1)} %bitcast.20, ...), custom_call_target="tpu_custom_call" | custom-call | tf_op jit(solution)/shard_map/sketch/pallas_call | solution.py:128
  10.9 4.9 %collective-permute-start.17 = (f32[96,512]{1,0:T(8,128)S(1)}, f32[96,512]{1,0:T(8,128)S(1)}, u32[]{:S(2)}, u32[]{:S(2)}) collective-permute-start(f32[96,512]{1,0:T(8,128)S(1)} %get-tuple-element.39), channel_id=1, source_target_pairs={{0,7},{1,0},{2,1},{3,2},{4,3},{5,4},{6,5},{7,6},{8,15},{9,8},{10,9... | collective-permute-start | bytes 589832 | tf_op jit(solution)/shard_map/ppermute | solution.py:400
  15.7 3.2 %collective-permute-done.17 = f32[96,512]{1,0:T(8,128)S(1)} collective-permute-done((f32[96,512]{1,0:T(8,128)S(1)}, f32[96,512]{1,0:T(8,128)S(1)}, u32[]{:S(2)}, u32[]{:S(2)}) %collective-permute-start.17) | collective-permute-done | bytes 196640 | tf_op jit(solution)/shard_map/ppermute | solution.py:400
  19.0 3.8 %collective-permute-start.18 = (f32[96,512]{1,0:T(8,128)S(1)}, f32[96,512]{1,0:T(8,128)S(1)}, u32[]{:S(2)}, u32[]{:S(2)}) collective-permute-start(f32[96,512]{1,0:T(8,128)S(1)} %add.105), channel_id=1, source_target_pairs={{0,7},{1,0},{2,1},{3,2},{4,3},{5,4},{6,5},{7,6},{8,15},{9,8},{10,9... | collective-permute-start | bytes 589832 | tf_op jit(solution)/shard_map/ppermute | solution.py:400
  22.7 0.9 collective-permute-start.4
  23.7 0.9 collective-permute-done
  24.6 0.3 collective-permute-start.1
  24.9 1.8 %collective-permute-done.14 = f32[96,512]{1,0:T(8,128)S(1)} collective-permute-done((f32[96,512]{1,0:T(8,128)S(1)}, f32[96,512]{1,0:T(8,128)S(1)}, u32[]{:S(2)}, u32[]{:S(2)}) %collective-permute-start.14) | collective-permute-done | bytes 196640 | tf_op jit(solution)/shard_map/ppermute | solution.py:400
  26.7 0.1 collective-permute-start.15
  26.8 1.3 collective-permute-done.18
  28.1 3.8 %collective-permute-start.19 = (f32[96,512]{1,0:T(8,128)S(1)}, f32[96,512]{1,0:T(8,128)S(1)}, u32[]{:S(2)}, u32[]{:S(2)}) collective-permute-start(f32[96,512]{1,0:T(8,128)S(1)} %add.106), channel_id=1, source_target_pairs={{0,7},{1,0},{2,1},{3,2},{4,3},{5,4},{6,5},{7,6},{8,15},{9,8},{10,9... | collective-permute-start | bytes 589832 | tf_op jit(solution)/shard_map/ppermute | solution.py:400
  31.8 0.1 collective-permute-done.4
  31.9 3.8 %collective-permute-start.5 = (f32[96,512]{1,0:T(8,128)S(1)}, f32[96,512]{1,0:T(8,128)S(1)}, u32[]{:S(2)}, u32[]{:S(2)}) collective-permute-start(f32[96,512]{1,0:T(8,128)S(1)} %add.99), channel_id=1, source_target_pairs={{0,7},{1,0},{2,1},{3,2},{4,3},{5,4},{6,5},{7,6},{8,15},{9,8},{10,9... | collective-permute-start | bytes 589832 | tf_op jit(solution)/shard_map/ppermute | solution.py:400
  35.7 0.1 collective-permute-start.2
  35.8 0.2 collective-permute-done.15
  36.0 0.1 collective-permute-start.16
  36.1 0.8 collective-permute-done.19
  36.9 3.8 %collective-permute-start.20 = (f32[96,512]{1,0:T(8,128)S(1)}, f32[96,512]{1,0:T(8,128)S(1)}, u32[]{:S(2)}, u32[]{:S(2)}) collective-permute-start(f32[96,512]{1,0:T(8,128)S(1)} %add.107), channel_id=1, source_target_pairs={{0,7},{1,0},{2,1},{3,2},{4,3},{5,4},{6,5},{7,6},{8,15},{9,8},{10,9... | collective-permute-start | bytes 589832 | tf_op jit(solution)/shard_map/ppermute | solution.py:400
  40.7 3.5 %collective-permute-start.6 = (f32[96,512]{1,0:T(8,128)S(1)}, f32[96,512]{1,0:T(8,128)S(1)}, u32[]{:S(2)}, u32[]{:S(2)}) collective-permute-start(f32[96,512]{1,0:T(8,128)S(1)} %add.100), channel_id=1, source_target_pairs={{0,7},{1,0},{2,1},{3,2},{4,3},{5,4},{6,5},{7,6},{8,15},{9,8},{10,9... | collective-permute-start | bytes 589832 | tf_op jit(solution)/shard_map/ppermute | solution.py:400
  44.3 0.1 collective-permute-start.3
  44.4 0.5 collective-permute-done.16
  44.9 0.7 collective-permute-done.20
  45.7 3.9 %collective-permute-start.21 = (f32[96,512]{1,0:T(8,128)S(1)}, f32[96,512]{1,0:T(8,128)S(1)}, u32[]{:S(2)}, u32[]{:S(2)}) collective-permute-start(f32[96,512]{1,0:T(8,128)S(1)} %add_add_fusion.refs_5_.refs_1_), channel_id=1, source_target_pairs={{0,7},{1,0},{2,1},{3,2},{4,3},{5,4},{6,5},{7,6},{8,15},{9,8},{10,9... | collective-permute-start | bytes 589832 | tf_op jit(solution)/shard_map/ppermute | solution.py:400
  49.6 2.3 %collective-permute-done.3 = f32[96,512]{1,0:T(8,128)S(1)} collective-permute-done((f32[96,512]{1,0:T(8,128)S(1)}, f32[96,512]{1,0:T(8,128)S(1)}, u32[]{:S(2)}, u32[]{:S(2)}) %collective-permute-start.3) | collective-permute-done | bytes 196640 | tf_op jit(solution)/shard_map/ppermute | solution.py:400
  51.9 0.1 collective-permute-start.10
  52.0 0.1 collective-permute-start.25
  52.1 3.2 %collective-permute-start.7 = (f32[96,512]{1,0:T(8,128)S(1)}, f32[96,512]{1,0:T(8,128)S(1)}, u32[]{:S(2)}, u32[]{:S(2)}) collective-permute-start(f32[96,512]{1,0:T(8,128)S(1)} %add_add_fusion.1.refs_0_), channel_id=1, source_target_pairs={{0,7},{1,0},{2,1},{3,2},{4,3},{5,4},{6,5},{7,6},{8,15},{9,8},{10,9... | collective-permute-start | bytes 589832 | tf_op jit(solution)/shard_map/ppermute | solution.py:400
  55.3 3.3 %collective-permute-start.22 = (f32[96,512]{1,0:T(8,128)S(1)}, f32[96,512]{1,0:T(8,128)S(1)}, u32[]{:S(2)}, u32[]{:S(2)}) collective-permute-start(f32[96,512]{1,0:T(8,128)S(1)} %collective-permute-done.21.refs_6_), channel_id=1, source_target_pairs={{0,7},{1,0},{2,1},{3,2},{4,3},{5,4},{6,5},{7,6},{8,15},{9,8},{10,9... | collective-permute-start | bytes 589832 | tf_op jit(solution)/shard_map/ppermute | solution.py:400
  58.6 2.2 %collective-permute-done.10.refs_4_ = f32[96,512]{1,0:T(8,128)S(1)} collective-permute-done((f32[96,512]{1,0:T(8,128)S(1)}, f32[96,512]{1,0:T(8,128)S(1)}, u32[]{:S(2)}, u32[]{:S(2)}) %collective-permute-start.10) | collective-permute-done | bytes 196640 | tf_op jit(solution)/shard_map/ppermute | solution.py:400
  60.8 4.2 %collective-permute-done.25.refs_9_ = f32[96,512]{1,0:T(8,128)S(1)} collective-permute-done((f32[96,512]{1,0:T(8,128)S(1)}, f32[96,512]{1,0:T(8,128)S(1)}, u32[]{:S(2)}, u32[]{:S(2)}) %collective-permute-start.25) | collective-permute-done | bytes 196640 | tf_op jit(solution)/shard_map/ppermute | solution.py:400
  65.0 3.2 %collective-permute-start.8 = (f32[96,512]{1,0:T(8,128)S(1)}, f32[96,512]{1,0:T(8,128)S(1)}, u32[]{:S(2)}, u32[]{:S(2)}) collective-permute-start(f32[96,512]{1,0:T(8,128)S(1)} %collective-permute-done.7.refs_1_), channel_id=1, source_target_pairs={{0,7},{1,0},{2,1},{3,2},{4,3},{5,4},{6,5},{7,6},{8,15},{9,8},{10,9... | collective-permute-start | bytes 589832 | tf_op jit(solution)/shard_map/ppermute | solution.py:400
  68.3 0.1 collective-permute-start.23
  68.3 1.4 %collective-permute-done.11.refs_3_ = f32[96,512]{1,0:T(8,128)S(1)} collective-permute-done((f32[96,512]{1,0:T(8,128)S(1)}, f32[96,512]{1,0:T(8,128)S(1)}, u32[]{:S(2)}, u32[]{:S(2)}) %collective-permute-start.11) | collective-permute-done | bytes 196640 | tf_op jit(solution)/shard_map/ppermute | solution.py:400
  69.8 0.5 collective-permute-start.12
  70.3 3.7 %collective-permute-done.26.refs_8_ = f32[96,512]{1,0:T(8,128)S(1)} collective-permute-done((f32[96,512]{1,0:T(8,128)S(1)}, f32[96,512]{1,0:T(8,128)S(1)}, u32[]{:S(2)}, u32[]{:S(2)}) %collective-permute-start.26) | collective-permute-done | bytes 196640 | tf_op jit(solution)/shard_map/ppermute | solution.py:400
  74.0 3.2 %collective-permute-start.9 = (f32[96,512]{1,0:T(8,128)S(1)}, f32[96,512]{1,0:T(8,128)S(1)}, u32[]{:S(2)}, u32[]{:S(2)}) collective-permute-start(f32[96,512]{1,0:T(8,128)S(1)} %collective-permute-done.8.refs_2_), channel_id=1, source_target_pairs={{0,7},{1,0},{2,1},{3,2},{4,3},{5,4},{6,5},{7,6},{8,15},{9,8},{10,9... | collective-permute-start | bytes 589832 | tf_op jit(solution)/shard_map/ppermute | solution.py:400
  77.2 3.1 %collective-permute-start.24 = (f32[96,512]{1,0:T(8,128)S(1)}, f32[96,512]{1,0:T(8,128)S(1)}, u32[]{:S(2)}, u32[]{:S(2)}) collective-permute-start(f32[96,512]{1,0:T(8,128)S(1)} %collective-permute-done.23.refs_3_), channel_id=1, source_target_pairs={{0,7},{1,0},{2,1},{3,2},{4,3},{5,4},{6,5},{7,6},{8,15},{9,8},{10,9... | collective-permute-start | bytes 589832 | tf_op jit(solution)/shard_map/ppermute | solution.py:400
  80.3 2.9 %split_near.1 = (bf16[10,384,256]{2,1,0:T(8,128)(2,1)S(1)}, f32[192,192]{1,0:T(8,128)S(1)}) custom-call(f32[96,512]{1,0:T(8,128)S(1)} %add_add_fusion.1.refs_0_, f32[96,512]{1,0:T(8,128)S(1)} %collective-permute-done.7.refs_1_, f32[96,512]{1,0:T(8,128)S(1)} %collective-permute-done.8.refs_2_, f32[96,512]{1,0:T(8,128)S(1)} %collective-permute-done.11.refs_3_, ...), custom_call_target="tpu_custom_call" | custom-call | tf_op jit(solution)/shard_map/split_near/pallas_call | solution.py:201
  83.2 6.1 %adjoint_near.1.refs_0_ = f32[16,192,256]{2,1,0:T(8,128)S(1)} custom-call(s32[96]{0:T(128)S(1)} %get-tuple-element.50.list_ref, s32[2,96]{1,0:T(2,128)S(1)} %bitcast.21, s32[2]{0:T(128)S(1)} %get-tuple-element.47.count_ref, s32[1]{0:T(128)} %bitcast.1.index_ref, bf16[96,256,256]{2,1,0:T(8,128)(2,1)S(1)} %get-tuple-element.48.buf_ref, ...), custom_call_target="tpu_custom_call" | custom-call | tf_op jit(solution)/shard_map/adjoint_near/pallas_call | solution.py:276
  89.4 1.9 %split_far.1 = (bf16[6,384,256]{2,1,0:T(8,128)(2,1)S(1)}, f32[192,128]{1,0:T(8,128)S(1)}) custom-call(f32[96,512]{1,0:T(8,128)S(1)} %collective-permute-done.9.refs_0_, f32[96,512]{1,0:T(8,128)S(1)} %collective-permute-done.13.refs_1_, f32[96,512]{1,0:T(8,128)S(1)} %collective-permute-done.12.refs_2_, f32[96,512]{1,0:T(8,128)S(1)} %collective-permute-done.23.refs_3_, ...), custom_call_target="tpu_custom_call" | custom-call | tf_op jit(solution)/shard_map/split_far/pallas_call | solution.py:201
  91.3 4.7 %adjoint_far.1 = (f32[16,192,128]{2,1,0:T(8,128)S(1)}, f32[16,192,128]{2,1,0:T(8,128)S(1)}) custom-call(s32[96]{0:T(128)S(1)} %get-tuple-element.46.list_ref, s32[2,96]{1,0:T(2,128)S(1)} %bitcast.22, s32[2]{0:T(128)S(1)} %get-tuple-element.47.count_ref, s32[1]{0:T(128)} %bitcast.1.index_ref, bf16[96,256,256]{2,1,0:T(8,128)(2,1)S(1)} %get-tuple-element.48.buf_ref, ...), custom_call_target="tpu_custom_call" | custom-call | tf_op jit(solution)/shard_map/adjoint_far/pallas_call | solution.py:276
  95.9 0.1 collective-permute-start.35
  96.0 0.5 collective-permute-start.28
  96.5 3.0 %collective-permute-done.28 = f32[192,128]{1,0:T(8,128)S(1)} collective-permute-done((f32[192,128]{1,0:T(8,128)S(1)}, f32[192,128]{1,0:T(8,128)S(1)}, u32[]{:S(2)}, u32[]{:S(2)}) %collective-permute-start.28) | collective-permute-done | bytes 98336 | tf_op jit(solution)/shard_map/ppermute | solution.py:400
  99.6 4.6 %collective-permute-start.29 = (f32[192,128]{1,0:T(8,128)S(1)}, f32[192,128]{1,0:T(8,128)S(1)}, u32[]{:S(2)}, u32[]{:S(2)}) collective-permute-start(f32[192,128]{1,0:T(8,128)S(1)} %add.110), channel_id=1, source_target_pairs={{0,128},{8,40},{16,144},{24,56},{32,160},{40,8},{48,176},{56,24},{... | collective-permute-start | bytes 294920 | tf_op jit(solution)/shard_map/ppermute | solution.py:443
  104.2 0.2 add.117
  104.4 0.1 fusion.5
  104.4 0.1 collective-permute-start.36
  104.5 0.1 collective-permute-start.37
  104.6 2.0 %collective-permute-start.38 = (f32[4,192,128]{2,1,0:T(8,128)S(1)}, f32[4,192,128]{2,1,0:T(8,128)S(1)}, u32[]{:S(2)}, u32[]{:S(2)}) collective-permute-start(f32[4,192,128]{2,1,0:T(8,128)S(1)} %get-tuple-element.55), channel_id=1, source_target_pairs={{0,192},{8,56},{16,208},{24,8},{32,224},{40,24},{48,240},{56,40},{... | collective-permute-start | bytes 1179656 | tf_op jit(solution)/shard_map/ppermute | solution.py:443
  106.6 2.0 %collective-permute-start.30 = (f32[192,128]{1,0:T(8,128)S(1)}, f32[192,128]{1,0:T(8,128)S(1)}, u32[]{:S(2)}, u32[]{:S(2)}) collective-permute-start(f32[192,128]{1,0:T(8,128)S(1)} %add.110), channel_id=1, source_target_pairs={{0,64},{8,24},{16,80},{24,40},{32,96},{40,56},{48,112},{56,8},{64,... | collective-permute-start | bytes 294920 | tf_op jit(solution)/shard_map/ppermute | solution.py:443
  108.6 0.6 collective-permute-start.31
  109.2 7.2 %collective-permute-done.30 = f32[192,128]{1,0:T(8,128)S(1)} collective-permute-done((f32[192,128]{1,0:T(8,128)S(1)}, f32[192,128]{1,0:T(8,128)S(1)}, u32[]{:S(2)}, u32[]{:S(2)}) %collective-permute-start.30) | collective-permute-done | bytes 98336 | tf_op jit(solution)/shard_map/ppermute | solution.py:443
  116.4 2.7 %collective-permute-done.31 = f32[192,128]{1,0:T(8,128)S(1)} collective-permute-done((f32[192,128]{1,0:T(8,128)S(1)}, f32[192,128]{1,0:T(8,128)S(1)}, u32[]{:S(2)}, u32[]{:S(2)}) %collective-permute-start.31) | collective-permute-done | bytes 98336 | tf_op jit(solution)/shard_map/ppermute | solution.py:443
  119.1 2.6 %collective-permute-start.32 = (f32[192,128]{1,0:T(8,128)S(1)}, f32[192,128]{1,0:T(8,128)S(1)}, u32[]{:S(2)}, u32[]{:S(2)}) collective-permute-start(f32[192,128]{1,0:T(8,128)S(1)} %add_add_fusion.3), channel_id=1, source_target_pairs={{0,32},{8,136},{16,48},{24,152},{32,0},{40,168},{48,16},{56,184},{... | collective-permute-start | bytes 294920 | tf_op jit(solution)/shard_map/ppermute | solution.py:443
  121.8 3.2 %collective-permute-start.34 = (f32[192,128]{1,0:T(8,128)S(1)}, f32[192,128]{1,0:T(8,128)S(1)}, u32[]{:S(2)}, u32[]{:S(2)}) collective-permute-start(f32[192,128]{1,0:T(8,128)S(1)} %add_add_fusion.3), channel_id=1, source_target_pairs={{0,48},{8,200},{16,0},{24,216},{32,16},{40,232},{48,32},{56,248},{... | collective-permute-start | bytes 294920 | tf_op jit(solution)/shard_map/ppermute | solution.py:443
  125.0 0.1 fusion.1
  125.1 0.1 collective-permute-start.39
  125.2 0.9 collective-permute-start.40
  126.1 2.5 %collective-permute-start.41 = (f32[192,128]{1,0:T(8,128)S(1)}, f32[192,128]{1,0:T(8,128)S(1)}, u32[]{:S(2)}, u32[]{:S(2)}) collective-permute-start(f32[192,128]{1,0:T(8,128)S(1)} %get-tuple-element.58), channel_id=1, source_target_pairs={{0,48},{8,200},{16,0},{24,216},{32,16},{40,232},{48,32},{56,248},{... | collective-permute-start | bytes 294920 | tf_op jit(solution)/shard_map/ppermute | solution.py:443
  128.6 11.1 %factor.1.factor_ref = f32[192,192]{1,0:T(8,128)S(1)} custom-call(f32[192,128]{1,0:T(8,128)S(1)} %add_add_fusion.2.packed_ref), custom_call_target="tpu_custom_call" | custom-call | tf_op jit(solution)/shard_map/factor/pallas_call | solution.py:368
  139.7 1.2 shard_map.50
  141.0 1.0 shard_map.51
  (50 shorter events, 0.6 us)
Async XLA Ops:
  1.3 0.7 copy-start
  10.9 8.1 %collective-permute-start.17 = (f32[96,512]{1,0:T(8,128)S(1)}, f32[96,512]{1,0:T(8,128)S(1)}, u32[]{:S(2)}, u32[]{:S(2)}) collective-permute-start(f32[96,512]{1,0:T(8,128)S(1)} %get-tuple-element.39), channel_id=1, source_target_pairs={{0,7},{1,0},{2,1},{3,2},{4,3},{5,4},{6,5},{7,6},{8,15},{9,8},{10,9... | collective-permute-start | bytes 589832 | tf_op jit(solution)/shard_map/ppermute | solution.py:400
  15.7 8.8 %collective-permute-start = (f32[96,512]{1,0:T(8,128)S(1)}, f32[96,512]{1,0:T(8,128)S(1)}, u32[]{:S(2)}, u32[]{:S(2)}) collective-permute-start(f32[96,512]{1,0:T(8,128)S(1)} %get-tuple-element.28), channel_id=1, source_target_pairs={{0,1},{1,2},{2,3},{3,4},{4,5},{5,6},{6,7},{7,0},{8,9},{9,10},{10,1... | collective-permute-start | bytes 589832 | tf_op jit(solution)/shard_map/ppermute | solution.py:400
  15.7 10.9 %collective-permute-start.14 = (f32[96,512]{1,0:T(8,128)S(1)}, f32[96,512]{1,0:T(8,128)S(1)}, u32[]{:S(2)}, u32[]{:S(2)}) collective-permute-start(f32[96,512]{1,0:T(8,128)S(1)} %get-tuple-element.36), channel_id=1, source_target_pairs={{0,1},{1,2},{2,3},{3,4},{4,5},{5,6},{6,7},{7,0},{8,9},{9,10},{10,1... | collective-permute-start | bytes 589832 | tf_op jit(solution)/shard_map/ppermute | solution.py:400
  19.0 9.1 %collective-permute-start.18 = (f32[96,512]{1,0:T(8,128)S(1)}, f32[96,512]{1,0:T(8,128)S(1)}, u32[]{:S(2)}, u32[]{:S(2)}) collective-permute-start(f32[96,512]{1,0:T(8,128)S(1)} %add.105), channel_id=1, source_target_pairs={{0,7},{1,0},{2,1},{3,2},{4,3},{5,4},{6,5},{7,6},{8,15},{9,8},{10,9... | collective-permute-start | bytes 589832 | tf_op jit(solution)/shard_map/ppermute | solution.py:400
  22.7 9.1 %collective-permute-start.4 = (f32[96,512]{1,0:T(8,128)S(1)}, f32[96,512]{1,0:T(8,128)S(1)}, u32[]{:S(2)}, u32[]{:S(2)}) collective-permute-start(f32[96,512]{1,0:T(8,128)S(1)} %get-tuple-element.32), channel_id=1, source_target_pairs={{0,7},{1,0},{2,1},{3,2},{4,3},{5,4},{6,5},{7,6},{8,15},{9,8},{10,9... | collective-permute-start | bytes 589832 | tf_op jit(solution)/shard_map/ppermute | solution.py:400
  24.6 11.1 %collective-permute-start.1 = (f32[96,512]{1,0:T(8,128)S(1)}, f32[96,512]{1,0:T(8,128)S(1)}, u32[]{:S(2)}, u32[]{:S(2)}) collective-permute-start(f32[96,512]{1,0:T(8,128)S(1)} %add.96), channel_id=1, source_target_pairs={{0,1},{1,2},{2,3},{3,4},{4,5},{5,6},{6,7},{7,0},{8,9},{9,10},{10,1... | collective-permute-start | bytes 589832 | tf_op jit(solution)/shard_map/ppermute | solution.py:400
  26.7 9.3 %collective-permute-start.15 = (f32[96,512]{1,0:T(8,128)S(1)}, f32[96,512]{1,0:T(8,128)S(1)}, u32[]{:S(2)}, u32[]{:S(2)}) collective-permute-start(f32[96,512]{1,0:T(8,128)S(1)} %add.103), channel_id=1, source_target_pairs={{0,1},{1,2},{2,3},{3,4},{4,5},{5,6},{6,7},{7,0},{8,9},{9,10},{10,1... | collective-permute-start | bytes 589832 | tf_op jit(solution)/shard_map/ppermute | solution.py:400
  28.1 8.9 %collective-permute-start.19 = (f32[96,512]{1,0:T(8,128)S(1)}, f32[96,512]{1,0:T(8,128)S(1)}, u32[]{:S(2)}, u32[]{:S(2)}) collective-permute-start(f32[96,512]{1,0:T(8,128)S(1)} %add.106), channel_id=1, source_target_pairs={{0,7},{1,0},{2,1},{3,2},{4,3},{5,4},{6,5},{7,6},{8,15},{9,8},{10,9... | collective-permute-start | bytes 589832 | tf_op jit(solution)/shard_map/ppermute | solution.py:400
  31.9 8.8 %collective-permute-start.5 = (f32[96,512]{1,0:T(8,128)S(1)}, f32[96,512]{1,0:T(8,128)S(1)}, u32[]{:S(2)}, u32[]{:S(2)}) collective-permute-start(f32[96,512]{1,0:T(8,128)S(1)} %add.99), channel_id=1, source_target_pairs={{0,7},{1,0},{2,1},{3,2},{4,3},{5,4},{6,5},{7,6},{8,15},{9,8},{10,9... | collective-permute-start | bytes 589832 | tf_op jit(solution)/shard_map/ppermute | solution.py:400
  35.7 8.6 %collective-permute-start.2 = (f32[96,512]{1,0:T(8,128)S(1)}, f32[96,512]{1,0:T(8,128)S(1)}, u32[]{:S(2)}, u32[]{:S(2)}) collective-permute-start(f32[96,512]{1,0:T(8,128)S(1)} %add.97), channel_id=1, source_target_pairs={{0,1},{1,2},{2,3},{3,4},{4,5},{5,6},{6,7},{7,0},{8,9},{9,10},{10,1... | collective-permute-start | bytes 589832 | tf_op jit(solution)/shard_map/ppermute | solution.py:400
  36.0 8.9 %collective-permute-start.16 = (f32[96,512]{1,0:T(8,128)S(1)}, f32[96,512]{1,0:T(8,128)S(1)}, u32[]{:S(2)}, u32[]{:S(2)}) collective-permute-start(f32[96,512]{1,0:T(8,128)S(1)} %add.104), channel_id=1, source_target_pairs={{0,1},{1,2},{2,3},{3,4},{4,5},{5,6},{6,7},{7,0},{8,9},{9,10},{10,1... | collective-permute-start | bytes 589832 | tf_op jit(solution)/shard_map/ppermute | solution.py:400
  36.9 8.7 %collective-permute-start.20 = (f32[96,512]{1,0:T(8,128)S(1)}, f32[96,512]{1,0:T(8,128)S(1)}, u32[]{:S(2)}, u32[]{:S(2)}) collective-permute-start(f32[96,512]{1,0:T(8,128)S(1)} %add.107), channel_id=1, source_target_pairs={{0,7},{1,0},{2,1},{3,2},{4,3},{5,4},{6,5},{7,6},{8,15},{9,8},{10,9... | collective-permute-start | bytes 589832 | tf_op jit(solution)/shard_map/ppermute | solution.py:400
  40.7 8.9 %collective-permute-start.6 = (f32[96,512]{1,0:T(8,128)S(1)}, f32[96,512]{1,0:T(8,128)S(1)}, u32[]{:S(2)}, u32[]{:S(2)}) collective-permute-start(f32[96,512]{1,0:T(8,128)S(1)} %add.100), channel_id=1, source_target_pairs={{0,7},{1,0},{2,1},{3,2},{4,3},{5,4},{6,5},{7,6},{8,15},{9,8},{10,9... | collective-permute-start | bytes 589832 | tf_op jit(solution)/shard_map/ppermute | solution.py:400
  44.3 7.6 %collective-permute-start.3 = (f32[96,512]{1,0:T(8,128)S(1)}, f32[96,512]{1,0:T(8,128)S(1)}, u32[]{:S(2)}, u32[]{:S(2)}) collective-permute-start(f32[96,512]{1,0:T(8,128)S(1)} %add.98), channel_id=1, source_target_pairs={{0,1},{1,2},{2,3},{3,4},{4,5},{5,6},{6,7},{7,0},{8,9},{9,10},{10,1... | collective-permute-start | bytes 589832 | tf_op jit(solution)/shard_map/ppermute | solution.py:400
  45.7 9.7 %collective-permute-start.21 = (f32[96,512]{1,0:T(8,128)S(1)}, f32[96,512]{1,0:T(8,128)S(1)}, u32[]{:S(2)}, u32[]{:S(2)}) collective-permute-start(f32[96,512]{1,0:T(8,128)S(1)} %add_add_fusion.refs_5_.refs_1_), channel_id=1, source_target_pairs={{0,7},{1,0},{2,1},{3,2},{4,3},{5,4},{6,5},{7,6},{8,15},{9,8},{10,9... | collective-permute-start | bytes 589832 | tf_op jit(solution)/shard_map/ppermute | solution.py:400
  51.9 8.9 %collective-permute-start.10 = (f32[96,512]{1,0:T(8,128)S(1)}, f32[96,512]{1,0:T(8,128)S(1)}, u32[]{:S(2)}, u32[]{:S(2)}) collective-permute-start(f32[96,512]{1,0:T(8,128)S(1)} %add_add_fusion.1.refs_0_), channel_id=1, source_target_pairs={{0,1},{1,2},{2,3},{3,4},{4,5},{5,6},{6,7},{7,0},{8,9},{9,10},{10,1... | collective-permute-start | bytes 589832 | tf_op jit(solution)/shard_map/ppermute | solution.py:400
  52.0 13.0 %collective-permute-start.25 = (f32[96,512]{1,0:T(8,128)S(1)}, f32[96,512]{1,0:T(8,128)S(1)}, u32[]{:S(2)}, u32[]{:S(2)}) collective-permute-start(f32[96,512]{1,0:T(8,128)S(1)} %add_add_fusion.refs_5_.refs_1_), channel_id=1, source_target_pairs={{0,1},{1,2},{2,3},{3,4},{4,5},{5,6},{6,7},{7,0},{8,9},{9,10},{10,1... | collective-permute-start | bytes 589832 | tf_op jit(solution)/shard_map/ppermute | solution.py:400
  52.1 12.9 %collective-permute-start.7 = (f32[96,512]{1,0:T(8,128)S(1)}, f32[96,512]{1,0:T(8,128)S(1)}, u32[]{:S(2)}, u32[]{:S(2)}) collective-permute-start(f32[96,512]{1,0:T(8,128)S(1)} %add_add_fusion.1.refs_0_), channel_id=1, source_target_pairs={{0,7},{1,0},{2,1},{3,2},{4,3},{5,4},{6,5},{7,6},{8,15},{9,8},{10,9... | collective-permute-start | bytes 589832 | tf_op jit(solution)/shard_map/ppermute | solution.py:400
  55.3 12.9 %collective-permute-start.22 = (f32[96,512]{1,0:T(8,128)S(1)}, f32[96,512]{1,0:T(8,128)S(1)}, u32[]{:S(2)}, u32[]{:S(2)}) collective-permute-start(f32[96,512]{1,0:T(8,128)S(1)} %collective-permute-done.21.refs_6_), channel_id=1, source_target_pairs={{0,7},{1,0},{2,1},{3,2},{4,3},{5,4},{6,5},{7,6},{8,15},{9,8},{10,9... | collective-permute-start | bytes 589832 | tf_op jit(solution)/shard_map/ppermute | solution.py:400
  60.8 9.0 %collective-permute-start.11 = (f32[96,512]{1,0:T(8,128)S(1)}, f32[96,512]{1,0:T(8,128)S(1)}, u32[]{:S(2)}, u32[]{:S(2)}) collective-permute-start(f32[96,512]{1,0:T(8,128)S(1)} %collective-permute-done.10.refs_4_), channel_id=1, source_target_pairs={{0,1},{1,2},{2,3},{3,4},{4,5},{5,6},{6,7},{7,0},{8,9},{9,10},{10,1... | collective-permute-start | bytes 589832 | tf_op jit(solution)/shard_map/ppermute | solution.py:400
  65.0 9.0 %collective-permute-start.26 = (f32[96,512]{1,0:T(8,128)S(1)}, f32[96,512]{1,0:T(8,128)S(1)}, u32[]{:S(2)}, u32[]{:S(2)}) collective-permute-start(f32[96,512]{1,0:T(8,128)S(1)} %collective-permute-done.25.refs_9_), channel_id=1, source_target_pairs={{0,1},{1,2},{2,3},{3,4},{4,5},{5,6},{6,7},{7,0},{8,9},{9,10},{10,1... | collective-permute-start | bytes 589832 | tf_op jit(solution)/shard_map/ppermute | solution.py:400
  65.0 9.0 %collective-permute-start.8 = (f32[96,512]{1,0:T(8,128)S(1)}, f32[96,512]{1,0:T(8,128)S(1)}, u32[]{:S(2)}, u32[]{:S(2)}) collective-permute-start(f32[96,512]{1,0:T(8,128)S(1)} %collective-permute-done.7.refs_1_), channel_id=1, source_target_pairs={{0,7},{1,0},{2,1},{3,2},{4,3},{5,4},{6,5},{7,6},{8,15},{9,8},{10,9... | collective-permute-start | bytes 589832 | tf_op jit(solution)/shard_map/ppermute | solution.py:400
  68.3 9.0 %collective-permute-start.23 = (f32[96,512]{1,0:T(8,128)S(1)}, f32[96,512]{1,0:T(8,128)S(1)}, u32[]{:S(2)}, u32[]{:S(2)}) collective-permute-start(f32[96,512]{1,0:T(8,128)S(1)} %collective-permute-done.22.refs_7_), channel_id=1, source_target_pairs={{0,7},{1,0},{2,1},{3,2},{4,3},{5,4},{6,5},{7,6},{8,15},{9,8},{10,9... | collective-permute-start | bytes 589832 | tf_op jit(solution)/shard_map/ppermute | solution.py:400
  69.8 10.5 %collective-permute-start.12 = (f32[96,512]{1,0:T(8,128)S(1)}, f32[96,512]{1,0:T(8,128)S(1)}, u32[]{:S(2)}, u32[]{:S(2)}) collective-permute-start(f32[96,512]{1,0:T(8,128)S(1)} %collective-permute-done.11.refs_3_), channel_id=1, source_target_pairs={{0,1},{1,2},{2,3},{3,4},{4,5},{5,6},{6,7},{7,0},{8,9},{9,10},{10,1... | collective-permute-start | bytes 589832 | tf_op jit(solution)/shard_map/ppermute | solution.py:400
  74.0 15.3 %collective-permute-start.27 = (f32[96,512]{1,0:T(8,128)S(1)}, f32[96,512]{1,0:T(8,128)S(1)}, u32[]{:S(2)}, u32[]{:S(2)}) collective-permute-start(f32[96,512]{1,0:T(8,128)S(1)} %collective-permute-done.26.refs_8_), channel_id=1, source_target_pairs={{0,1},{1,2},{2,3},{3,4},{4,5},{5,6},{6,7},{7,0},{8,9},{9,10},{10,1... | collective-permute-start | bytes 589832 | tf_op jit(solution)/shard_map/ppermute | solution.py:400
  74.0 15.4 %collective-permute-start.9 = (f32[96,512]{1,0:T(8,128)S(1)}, f32[96,512]{1,0:T(8,128)S(1)}, u32[]{:S(2)}, u32[]{:S(2)}) collective-permute-start(f32[96,512]{1,0:T(8,128)S(1)} %collective-permute-done.8.refs_2_), channel_id=1, source_target_pairs={{0,7},{1,0},{2,1},{3,2},{4,3},{5,4},{6,5},{7,6},{8,15},{9,8},{10,9... | collective-permute-start | bytes 589832 | tf_op jit(solution)/shard_map/ppermute | solution.py:400
  77.2 12.1 %collective-permute-start.24 = (f32[96,512]{1,0:T(8,128)S(1)}, f32[96,512]{1,0:T(8,128)S(1)}, u32[]{:S(2)}, u32[]{:S(2)}) collective-permute-start(f32[96,512]{1,0:T(8,128)S(1)} %collective-permute-done.23.refs_3_), channel_id=1, source_target_pairs={{0,7},{1,0},{2,1},{3,2},{4,3},{5,4},{6,5},{7,6},{8,15},{9,8},{10,9... | collective-permute-start | bytes 589832 | tf_op jit(solution)/shard_map/ppermute | solution.py:400
  80.3 9.1 %collective-permute-start.13 = (f32[96,512]{1,0:T(8,128)S(1)}, f32[96,512]{1,0:T(8,128)S(1)}, u32[]{:S(2)}, u32[]{:S(2)}) collective-permute-start(f32[96,512]{1,0:T(8,128)S(1)} %collective-permute-done.12.refs_2_), channel_id=1, source_target_pairs={{0,1},{1,2},{2,3},{3,4},{4,5},{5,6},{6,7},{7,0},{8,9},{9,10},{10,1... | collective-permute-start | bytes 589832 | tf_op jit(solution)/shard_map/ppermute | solution.py:400
  95.9 8.2 %collective-permute-start.35 = (f32[16,192,128]{2,1,0:T(8,128)S(1)}, f32[16,192,128]{2,1,0:T(8,128)S(1)}, u32[]{:S(2)}, u32[]{:S(2)}) collective-permute-start(f32[16,192,128]{2,1,0:T(8,128)S(1)} %get-tuple-element.53), channel_id=1, source_target_pairs={{0,8},{8,0},{1,9},{9,1},{2,10},{10,2},{3,11},{11,3},{4,12},{12,4},... | collective-permute-start | bytes 4718600 | tf_op jit(solution)/shard_map/ppermute | solution.py:400
  96.0 3.5 %collective-permute-start.28 = (f32[192,128]{1,0:T(8,128)S(1)}, f32[192,128]{1,0:T(8,128)S(1)}, u32[]{:S(2)}, u32[]{:S(2)}) collective-permute-start(f32[192,128]{1,0:T(8,128)S(1)} %get-tuple-element.45), channel_id=1, source_target_pairs={{0,8},{8,0},{1,9},{9,1},{2,10},{10,2},{3,11},{11,3},{4,12},{12,4},... | collective-permute-start | bytes 294920 | tf_op jit(solution)/shard_map/ppermute | solution.py:400
  99.6 9.0 %collective-permute-start.29 = (f32[192,128]{1,0:T(8,128)S(1)}, f32[192,128]{1,0:T(8,128)S(1)}, u32[]{:S(2)}, u32[]{:S(2)}) collective-permute-start(f32[192,128]{1,0:T(8,128)S(1)} %add.110), channel_id=1, source_target_pairs={{0,128},{8,40},{16,144},{24,56},{32,160},{40,8},{48,176},{56,24},{... | collective-permute-start | bytes 294920 | tf_op jit(solution)/shard_map/ppermute | solution.py:443
  104.4 17.3 %collective-permute-start.36 = (f32[4,192,128]{2,1,0:T(8,128)S(1)}, f32[4,192,128]{2,1,0:T(8,128)S(1)}, u32[]{:S(2)}, u32[]{:S(2)}) collective-permute-start(f32[4,192,128]{2,1,0:T(8,128)S(1)} %get-tuple-element.54), channel_id=1, source_target_pairs={{0,128},{8,40},{16,144},{24,56},{32,160},{40,8},{48,176},{56,24},{... | collective-permute-start | bytes 1179656 | tf_op jit(solution)/shard_map/ppermute | solution.py:443
  104.5 20.5 %collective-permute-start.37 = (f32[4,192,128]{2,1,0:T(8,128)S(1)}, f32[4,192,128]{2,1,0:T(8,128)S(1)}, u32[]{:S(2)}, u32[]{:S(2)}) collective-permute-start(f32[4,192,128]{2,1,0:T(8,128)S(1)} %get-tuple-element.56), channel_id=1, source_target_pairs={{0,64},{8,24},{16,80},{24,40},{32,96},{40,56},{48,112},{56,8},{64,... | collective-permute-start | bytes 1179656 | tf_op jit(solution)/shard_map/ppermute | solution.py:443
  104.6 20.4 %collective-permute-start.38 = (f32[4,192,128]{2,1,0:T(8,128)S(1)}, f32[4,192,128]{2,1,0:T(8,128)S(1)}, u32[]{:S(2)}, u32[]{:S(2)}) collective-permute-start(f32[4,192,128]{2,1,0:T(8,128)S(1)} %get-tuple-element.55), channel_id=1, source_target_pairs={{0,192},{8,56},{16,208},{24,8},{32,224},{40,24},{48,240},{56,40},{... | collective-permute-start | bytes 1179656 | tf_op jit(solution)/shard_map/ppermute | solution.py:443
  106.6 9.8 %collective-permute-start.30 = (f32[192,128]{1,0:T(8,128)S(1)}, f32[192,128]{1,0:T(8,128)S(1)}, u32[]{:S(2)}, u32[]{:S(2)}) collective-permute-start(f32[192,128]{1,0:T(8,128)S(1)} %add.110), channel_id=1, source_target_pairs={{0,64},{8,24},{16,80},{24,40},{32,96},{40,56},{48,112},{56,8},{64,... | collective-permute-start | bytes 294920 | tf_op jit(solution)/shard_map/ppermute | solution.py:443
  108.6 10.4 %collective-permute-start.31 = (f32[192,128]{1,0:T(8,128)S(1)}, f32[192,128]{1,0:T(8,128)S(1)}, u32[]{:S(2)}, u32[]{:S(2)}) collective-permute-start(f32[192,128]{1,0:T(8,128)S(1)} %add.110), channel_id=1, source_target_pairs={{0,192},{8,56},{16,208},{24,8},{32,224},{40,24},{48,240},{56,40},{... | collective-permute-start | bytes 294920 | tf_op jit(solution)/shard_map/ppermute | solution.py:443
  119.1 7.0 %collective-permute-start.32 = (f32[192,128]{1,0:T(8,128)S(1)}, f32[192,128]{1,0:T(8,128)S(1)}, u32[]{:S(2)}, u32[]{:S(2)}) collective-permute-start(f32[192,128]{1,0:T(8,128)S(1)} %add_add_fusion.3), channel_id=1, source_target_pairs={{0,32},{8,136},{16,48},{24,152},{32,0},{40,168},{48,16},{56,184},{... | collective-permute-start | bytes 294920 | tf_op jit(solution)/shard_map/ppermute | solution.py:443
  121.8 6.8 %collective-permute-start.33 = (f32[192,128]{1,0:T(8,128)S(1)}, f32[192,128]{1,0:T(8,128)S(1)}, u32[]{:S(2)}, u32[]{:S(2)}) collective-permute-start(f32[192,128]{1,0:T(8,128)S(1)} %add_add_fusion.3), channel_id=1, source_target_pairs={{0,16},{8,72},{16,32},{24,88},{32,48},{40,104},{48,0},{56,120},{64... | collective-permute-start | bytes 294920 | tf_op jit(solution)/shard_map/ppermute | solution.py:443
  121.8 6.8 %collective-permute-start.34 = (f32[192,128]{1,0:T(8,128)S(1)}, f32[192,128]{1,0:T(8,128)S(1)}, u32[]{:S(2)}, u32[]{:S(2)}) collective-permute-start(f32[192,128]{1,0:T(8,128)S(1)} %add_add_fusion.3), channel_id=1, source_target_pairs={{0,48},{8,200},{16,0},{24,216},{32,16},{40,232},{48,32},{56,248},{... | collective-permute-start | bytes 294920 | tf_op jit(solution)/shard_map/ppermute | solution.py:443
  125.1 15.8 %collective-permute-start.39 = (f32[192,128]{1,0:T(8,128)S(1)}, f32[192,128]{1,0:T(8,128)S(1)}, u32[]{:S(2)}, u32[]{:S(2)}) collective-permute-start(f32[192,128]{1,0:T(8,128)S(1)} %get-tuple-element.57), channel_id=1, source_target_pairs={{0,32},{8,136},{16,48},{24,152},{32,0},{40,168},{48,16},{56,184},{... | collective-permute-start | bytes 294920 | tf_op jit(solution)/shard_map/ppermute | solution.py:443
  125.2 15.7 %collective-permute-start.40 = (f32[192,128]{1,0:T(8,128)S(1)}, f32[192,128]{1,0:T(8,128)S(1)}, u32[]{:S(2)}, u32[]{:S(2)}) collective-permute-start(f32[192,128]{1,0:T(8,128)S(1)} %get-tuple-element.59), channel_id=1, source_target_pairs={{0,16},{8,72},{16,32},{24,88},{32,48},{40,104},{48,0},{56,120},{64... | collective-permute-start | bytes 294920 | tf_op jit(solution)/shard_map/ppermute | solution.py:443
  126.1 14.8 %collective-permute-start.41 = (f32[192,128]{1,0:T(8,128)S(1)}, f32[192,128]{1,0:T(8,128)S(1)}, u32[]{:S(2)}, u32[]{:S(2)}) collective-permute-start(f32[192,128]{1,0:T(8,128)S(1)} %get-tuple-element.58), channel_id=1, source_target_pairs={{0,48},{8,200},{16,0},{24,216},{32,16},{40,232},{48,32},{56,248},{... | collective-permute-start | bytes 294920 | tf_op jit(solution)/shard_map/ppermute | solution.py:443

commit v4 on v3

--- a/solution.py
+++ b/solution.py
@@ -57,12 +57,9 @@
     return jnp.clip(jnp.where(i >= 12, i - 6, i), 0, 2 * len(NEAR) - 1)
 
 
-AHEAD = 6
-
-
 def sketch_body(coords_ref, live_ref, index_ref, tiles_ref, *refs):
     outs = refs[: 2 * NZ]
-    buf_ref, near_ref, far_ref, count_ref, omega_ref, acc_ref, sems = refs[2 * NZ :]
+    buf_ref, omega_ref, acc_ref, sems = refs[2 * NZ :]
     batches = (live_ref[0] + SLOTS - 1) >> 3
     z = place_on_mesh(index_ref)[3]
 
@@ -74,12 +71,12 @@
         copy(batch).start()
         return carry
 
-    lax.fori_loop(0, jnp.minimum(batches, AHEAD), fetch, 0)
+    lax.fori_loop(0, batches, fetch, 0)
     k_ids = lax.broadcasted_iota(jnp.int32, (K, TB), 0)
     g_ids = lax.broadcasted_iota(jnp.int32, (K, TB), 1)
     base = g_ids * K + k_ids
 
-    def fill(j, found):
+    def fill(j, carry):
         h = base + (z * CT + j) * (TB * K)
         h = h * 747796405 + 1442695040
         h = h ^ (h >> 15)
@@ -87,31 +84,15 @@
         h = h ^ (h >> 13)
         omega_ref[j] = (1 - 2 * ((h >> 9) & 1)).astype(jnp.float32).astype(jnp.bfloat16)
         acc_ref[j] = jnp.zeros((K, TB), jnp.float32)
-        near, far = found
-        for t in range(NT // CT):
-            slot = j * (NT // CT) + t
-            i = relative_row(coords_ref, slot, z)
-            inside = jnp.where((i >= 2 * FAR[0]) & (i < 2 * FAR[-1] + 2), 1, 0)
-            live = jnp.where(slot < live_ref[0], 1, 0)
-            far_ref[far] = slot
-            near_ref[near] = slot
-            far += live * inside
-            near += live * (1 - inside)
-        return near, far
-
-    near, far = lax.fori_loop(0, CT, fill, (jnp.int32(0), jnp.int32(0)))
-    count_ref[0] = near
-    count_ref[1] = far
+        return carry
+
+    lax.fori_loop(0, CT, fill, 0)
 
     def work(batch, carry):
-        @pl.when(batch + AHEAD < batches)
-        def _():
-            copy(batch + AHEAD).start()
-
         copy(batch).wait()
         for t in range(SLOTS):
             slot = batch * SLOTS + t
-            i = jnp.where(slot < live_ref[0], relative_row(coords_ref, slot, z), RT)
+            i = jnp.where(slot < live_ref[0], coords_ref[0, slot], RT)
             acc_ref[i] += dot_nt(omega_ref[coords_ref[1, slot]], buf_ref[slot])
         return carry
 
@@ -120,8 +101,39 @@
         for half in range(2):
             for e in range(2):
                 outs[half * NZ + d][:, e * TB : (e + 1) * TB] = acc_ref[
-                    2 * d + e, half * KH : (half + 1) * KH, :
+                    (2 * (d + z) + e) & (RT - 1), half * KH : (half + 1) * KH, :
                 ]
+
+
+def lists_body(coords_ref, live_ref, index_ref, near_ref, far_ref, count_ref):
+    z = place_on_mesh(index_ref)[3]
+
+    def enter(slot, found):
+        near, far = found
+        i = relative_row(coords_ref, slot, z)
+        inside = jnp.where((i >= 2 * FAR[0]) & (i < 2 * FAR[-1] + 2), 1, 0)
+        far_ref[far] = slot
+        near_ref[near] = slot
+        return near + 1 - inside, far + inside
+
+    near, far = lax.fori_loop(0, live_ref[0], enter, (jnp.int32(0), jnp.int32(0)))
+    count_ref[0] = near
+    count_ref[1] = far
+
+
+def lists_call(coords, live, index):
+    return pl.pallas_call(
+        lists_body,
+        name="lists",
+        in_specs=[SMEM_SPEC] * 3,
+        out_specs=[SMEM_SPEC] * 3,
+        out_shape=[
+            jax.ShapeDtypeStruct((NT,), jnp.int32),
+            jax.ShapeDtypeStruct((NT,), jnp.int32),
+            jax.ShapeDtypeStruct((2,), jnp.int32),
+        ],
+        compiler_params=pltpu.CompilerParams(vmem_limit_bytes=4 << 20),
+    )(coords, live, index)
 
 
 def sketch_call(coords, live, index, tiles):
@@ -129,22 +141,17 @@
         sketch_body,
         name="sketch",
         in_specs=[SMEM_SPEC] * 3 + [HBM_SPEC],
-        out_specs=[VMEM_SPEC] * (2 * NZ + 1) + [SMEM_SPEC] * 3,
+        out_specs=[VMEM_SPEC] * (2 * NZ + 1),
         scratch_shapes=[
             pltpu.VMEM((CT, K, TB), jnp.bfloat16),
             pltpu.VMEM((RT + 1, K, TB), jnp.float32),
             pltpu.SemaphoreType.DMA((STEPS,)),
         ],
         out_shape=[jax.ShapeDtypeStruct((KH, CH), jnp.float32)] * (2 * NZ)
-        + [
-            jax.ShapeDtypeStruct((NT, TB, TB), jnp.bfloat16),
-            jax.ShapeDtypeStruct((NT,), jnp.int32),
-            jax.ShapeDtypeStruct((NT,), jnp.int32),
-            jax.ShapeDtypeStruct((2,), jnp.int32),
-        ],
+        + [jax.ShapeDtypeStruct((NT, TB, TB), jnp.bfloat16)],
         compiler_params=pltpu.CompilerParams(vmem_limit_bytes=24 << 20),
     )(coords, live, index, tiles)
-    return [got[:NZ], got[NZ : 2 * NZ]], *got[2 * NZ :]
+    return [got[:NZ], got[NZ : 2 * NZ]], got[2 * NZ]
 
 
 def split_body(*refs, n, last):
@@ -290,33 +297,46 @@
     ).astype(jnp.float32)
     work = jnp.concatenate([eye, block], axis=1)
     first = 0
-    for k in range(0, NB, 2):
+    for k in range(0, NB, 4):
         o = k - first
         rows = NB - first
-        a = jnp.broadcast_to(work[:, NB + k : NB + k + 1], (rows, 2 * NB))
-        b = jnp.broadcast_to(work[:, NB + k + 1 : NB + k + 2], (rows, 2 * NB))
-        p = a[o : o + 1]
-        q = a[o + 1 : o + 2]
-        r = b[o + 1 : o + 2]
-        r0 = work[o : o + 1]
-        r1 = work[o + 1 : o + 2]
+        cols = [
+            jnp.broadcast_to(work[:, NB + k + m : NB + k + m + 1], (rows, 2 * NB)) for m in range(4)
+        ]
+        r0, r1, r2, r3 = (work[o + m : o + m + 1] for m in range(4))
+        p, q, r = cols[0][o : o + 1], cols[1][o : o + 1], cols[1][o + 1 : o + 2]
+        b02, b12, d22 = (cols[2][o + m : o + m + 1] for m in range(3))
+        b03, b13, d23, d33 = (cols[3][o + m : o + m + 1] for m in range(4))
         inv = 1.0 / (p * r - q * q)
-        u0 = (r * r0 - q * r1) * inv
-        u1 = (p * r1 - q * r0) * inv
+        h02, h12 = (r * b02 - q * b12) * inv, (p * b12 - q * b02) * inv
+        h03, h13 = (r * b03 - q * b13) * inv, (p * b13 - q * b03) * inv
+        s22 = d22 - (b02 * h02 + b12 * h12)
+        s23 = d23 - (b02 * h03 + b12 * h13)
+        s33 = d33 - (b03 * h03 + b13 * h13)
+        inv_s = 1.0 / (s22 * s33 - s23 * s23)
+        t2 = r2 - (h02 * r0 + h12 * r1)
+        t3 = r3 - (h03 * r0 + h13 * r1)
+        u2 = (s33 * t2 - s23 * t3) * inv_s
+        u3 = (s22 * t3 - s23 * t2) * inv_s
+        u0 = (r * r0 - q * r1) * inv - (h02 * u2 + h03 * u3)
+        u1 = (p * r1 - q * r0) * inv - (h12 * u2 + h13 * u3)
+        ratio = q / p
         rows_ref[k : k + 1, :] = r0 * lax.rsqrt(p)
-        ratio = q / p
         rows_ref[k + 1 : k + 2, :] = (r1 - ratio * r0) * lax.rsqrt(r - ratio * q)
-        if k + 2 == NB:
+        ratio = s23 / s22
+        rows_ref[k + 2 : k + 3, :] = t2 * lax.rsqrt(s22)
+        rows_ref[k + 3 : k + 4, :] = (t3 - ratio * t2) * lax.rsqrt(s33 - ratio * s23)
+        if k + 4 == NB:
             break
-        skip = (k + 2) // 8 * 8 - first
+        skip = (k + 4) // 8 * 8 - first
         if skip:
-            work, a, b = work[skip:], a[skip:], b[skip:]
+            work = work[skip:]
+            cols = [c[skip:] for c in cols]
             first += skip
-        if (k + 2) % 8:
-            below = lax.broadcasted_iota(jnp.int32, a.shape, 0) >= k + 2 - first
-            a = jnp.where(below, a, 0.0)
-            b = jnp.where(below, b, 0.0)
-        work = work - (a * u0 + b * u1)
+        if (k + 4) % 8:
+            below = lax.broadcasted_iota(jnp.int32, work.shape, 0) >= k + 4 - first
+            cols = [jnp.where(below, c, 0.0) for c in cols]
+        work = work - ((cols[0] * u0 + cols[1] * u1) + (cols[2] * u2 + cols[3] * u3))
     return rows_ref[:, :NB]
 
 
@@ -454,7 +474,8 @@
     index = lax.axis_index(("x", "y", "core", "z")).astype(jnp.int32).reshape(1)
     coords = tile_coords.T
     tiles = pltpu.with_memory_space_constraint(tiles, pltpu.HBM)
-    parts, held, near_slots, far_slots, count = sketch_call(coords, live_counts, index, tiles)
+    parts, held = sketch_call(coords, live_counts, index, tiles)
+    near_slots, far_slots, count = lists_call(coords, live_counts, index)
     own = reduce_z(parts)
     found = gather_z(own)
     near = [got[d] for got in found for d in NEAR]

time: 144 us -> 143 us (level)
    pallas_call x1, Pallas kernels: 11.1 us -> 8.55 us  [factor_call(): pl.pallas_call(functools.partial(factor_body, scale=scale), name='factor'...]
    pallas_call x0 -> x1, Pallas kernels: none -> 1.9 us  [lists_call(): pl.pallas_call(lists_body, name='lists', in_specs=[SMEM_SPEC] * 3, out_sp...]
  transfers between devices with their start and end apart: 42 -> 42, of which waited for: 17 -> 16; matrix products, arithmetic and copies ran while one was open for 1% -> 1% of each run, Pallas kernels for 15% -> 15%
where the time goes in v4:
time: 143 us; the launch traced here: 141 us
  starting transfers between devices  65 us (45%)
  Pallas kernels  36.5 us (26%)
  waiting for transfers between devices  36.2 us (25%)
  between operations  1.57 us (1%)
    ppermute x30, starting transfers between devices, shift(): return lax.ppermute(x, axis, [(i, (i + by) % size) for i in range(size)])  46.3 us
    ppermute x30, waiting for transfers between devices, shift(): return lax.ppermute(x, axis, [(i, (i + by) % size) for i in range(size)])  26.3 us
    ppermute x12, starting transfers between devices, shift_xy(): return lax.ppermute(x, ('x', 'y', 'core'), pairs)  18.7 us
    pallas_call x2, Pallas kernels, adjoint_call(): pl.pallas_call(functools.partial(adjoint_body, dists=dists, last=last), n...  10.8 us
    ppermute x12, waiting for transfers between devices, shift_xy(): return lax.ppermute(x, ('x', 'y', 'core'), pairs)  9.86 us
    pallas_call x1, Pallas kernels, factor_call(): pl.pallas_call(functools.partial(factor_body, scale=scale), name='factor'...  8.55 us
    pallas_call x1, Pallas kernels, sketch_call(): pl.pallas_call(sketch_body, name='sketch', in_specs=[SMEM_SPEC] * 3 + [HB...  8.39 us
    pallas_call x2, Pallas kernels, split_call(): pl.pallas_call(functools.partial(split_body, n=n, last=bool(carried)), na...  4.74 us
  transfers between devices with their start and end apart: 42, of which 16 were waited for; matrix products, arithmetic and copies ran while one was open for 1% of the time, Pallas kernels for 15%

profile of v4, /device:TPU:2, one launch (start us, length us, event | category | flops | bytes accessed | tf_op | source)
XLA Modules:
  0.0 140.7 jit_solution(8775368310794800651)
XLA Ops:
  1.3 0.7 copy-done
  2.0 8.4 %sketch.1 = (f32[96,512]{1,0:T(8,128)S(1)}, f32[96,512]{1,0:T(8,128)S(1)}, f32[96,512]{1,0:T(8,128)S(1)}, f32[96,512]{1,0:T(8,128)S(1)}, f32[96,512]{1,0:T(8,128...) custom-call(s32[2,96]{1,0:T(2,128)S(1)} %bitcast.20, ...), custom_call_target="tpu_custom_call" | custom-call | tf_op jit(solution)/shard_map/sketch/pallas_call | solution.py:140
  10.4 4.9 %collective-permute-start.17 = (f32[96,512]{1,0:T(8,128)S(1)}, f32[96,512]{1,0:T(8,128)S(1)}, u32[]{:S(2)}, u32[]{:S(2)}) collective-permute-start(f32[96,512]{1,0:T(8,128)S(1)} %get-tuple-element.39), channel_id=1, source_target_pairs={{0,7},{1,0},{2,1},{3,2},{4,3},{5,4},{6,5},{7,6},{8,15},{9,8},{10,9... | collective-permute-start | bytes 589832 | tf_op jit(solution)/shard_map/ppermute | solution.py:420
  15.2 3.2 %collective-permute-done.17 = f32[96,512]{1,0:T(8,128)S(1)} collective-permute-done((f32[96,512]{1,0:T(8,128)S(1)}, f32[96,512]{1,0:T(8,128)S(1)}, u32[]{:S(2)}, u32[]{:S(2)}) %collective-permute-start.17) | collective-permute-done | bytes 196640 | tf_op jit(solution)/shard_map/ppermute | solution.py:420
  18.4 3.8 %collective-permute-start.18 = (f32[96,512]{1,0:T(8,128)S(1)}, f32[96,512]{1,0:T(8,128)S(1)}, u32[]{:S(2)}, u32[]{:S(2)}) collective-permute-start(f32[96,512]{1,0:T(8,128)S(1)} %add.105), channel_id=1, source_target_pairs={{0,7},{1,0},{2,1},{3,2},{4,3},{5,4},{6,5},{7,6},{8,15},{9,8},{10,9... | collective-permute-start | bytes 589832 | tf_op jit(solution)/shard_map/ppermute | solution.py:420
  22.2 0.9 collective-permute-start.4
  23.1 0.9 collective-permute-done
  24.1 0.3 collective-permute-start.1
  24.4 1.8 %collective-permute-done.14 = f32[96,512]{1,0:T(8,128)S(1)} collective-permute-done((f32[96,512]{1,0:T(8,128)S(1)}, f32[96,512]{1,0:T(8,128)S(1)}, u32[]{:S(2)}, u32[]{:S(2)}) %collective-permute-start.14) | collective-permute-done | bytes 196640 | tf_op jit(solution)/shard_map/ppermute | solution.py:420
  26.2 0.1 collective-permute-start.15
  26.2 1.3 collective-permute-done.18
  27.5 3.8 %collective-permute-start.19 = (f32[96,512]{1,0:T(8,128)S(1)}, f32[96,512]{1,0:T(8,128)S(1)}, u32[]{:S(2)}, u32[]{:S(2)}) collective-permute-start(f32[96,512]{1,0:T(8,128)S(1)} %add.106), channel_id=1, source_target_pairs={{0,7},{1,0},{2,1},{3,2},{4,3},{5,4},{6,5},{7,6},{8,15},{9,8},{10,9... | collective-permute-start | bytes 589832 | tf_op jit(solution)/shard_map/ppermute | solution.py:420
  31.4 3.8 %collective-permute-start.5 = (f32[96,512]{1,0:T(8,128)S(1)}, f32[96,512]{1,0:T(8,128)S(1)}, u32[]{:S(2)}, u32[]{:S(2)}) collective-permute-start(f32[96,512]{1,0:T(8,128)S(1)} %add.99), channel_id=1, source_target_pairs={{0,7},{1,0},{2,1},{3,2},{4,3},{5,4},{6,5},{7,6},{8,15},{9,8},{10,9... | collective-permute-start | bytes 589832 | tf_op jit(solution)/shard_map/ppermute | solution.py:420
  35.2 0.1 collective-permute-start.2
  35.3 0.2 collective-permute-done.15
  35.5 0.1 collective-permute-start.16
  35.6 0.8 collective-permute-done.19
  36.4 3.8 %collective-permute-start.20 = (f32[96,512]{1,0:T(8,128)S(1)}, f32[96,512]{1,0:T(8,128)S(1)}, u32[]{:S(2)}, u32[]{:S(2)}) collective-permute-start(f32[96,512]{1,0:T(8,128)S(1)} %add.107), channel_id=1, source_target_pairs={{0,7},{1,0},{2,1},{3,2},{4,3},{5,4},{6,5},{7,6},{8,15},{9,8},{10,9... | collective-permute-start | bytes 589832 | tf_op jit(solution)/shard_map/ppermute | solution.py:420
  40.2 3.5 %collective-permute-start.6 = (f32[96,512]{1,0:T(8,128)S(1)}, f32[96,512]{1,0:T(8,128)S(1)}, u32[]{:S(2)}, u32[]{:S(2)}) collective-permute-start(f32[96,512]{1,0:T(8,128)S(1)} %add.100), channel_id=1, source_target_pairs={{0,7},{1,0},{2,1},{3,2},{4,3},{5,4},{6,5},{7,6},{8,15},{9,8},{10,9... | collective-permute-start | bytes 589832 | tf_op jit(solution)/shard_map/ppermute | solution.py:420
  43.8 0.1 collective-permute-start.3
  43.9 0.5 collective-permute-done.16
  44.4 0.7 collective-permute-done.20
  45.1 3.9 %collective-permute-start.21 = (f32[96,512]{1,0:T(8,128)S(1)}, f32[96,512]{1,0:T(8,128)S(1)}, u32[]{:S(2)}, u32[]{:S(2)}) collective-permute-start(f32[96,512]{1,0:T(8,128)S(1)} %add_add_fusion.refs_5_.refs_1_), channel_id=1, source_target_pairs={{0,7},{1,0},{2,1},{3,2},{4,3},{5,4},{6,5},{7,6},{8,15},{9,8},{10,9... | collective-permute-start | bytes 589832 | tf_op jit(solution)/shard_map/ppermute | solution.py:420
  49.1 2.3 %collective-permute-done.3 = f32[96,512]{1,0:T(8,128)S(1)} collective-permute-done((f32[96,512]{1,0:T(8,128)S(1)}, f32[96,512]{1,0:T(8,128)S(1)}, u32[]{:S(2)}, u32[]{:S(2)}) %collective-permute-start.3) | collective-permute-done | bytes 196640 | tf_op jit(solution)/shard_map/ppermute | solution.py:420
  51.4 0.1 collective-permute-start.10
  51.5 0.1 collective-permute-start.25
  51.6 3.2 %collective-permute-start.7 = (f32[96,512]{1,0:T(8,128)S(1)}, f32[96,512]{1,0:T(8,128)S(1)}, u32[]{:S(2)}, u32[]{:S(2)}) collective-permute-start(f32[96,512]{1,0:T(8,128)S(1)} %add_add_fusion.1.refs_0_), channel_id=1, source_target_pairs={{0,7},{1,0},{2,1},{3,2},{4,3},{5,4},{6,5},{7,6},{8,15},{9,8},{10,9... | collective-permute-start | bytes 589832 | tf_op jit(solution)/shard_map/ppermute | solution.py:420
  54.8 3.2 %collective-permute-start.22 = (f32[96,512]{1,0:T(8,128)S(1)}, f32[96,512]{1,0:T(8,128)S(1)}, u32[]{:S(2)}, u32[]{:S(2)}) collective-permute-start(f32[96,512]{1,0:T(8,128)S(1)} %collective-permute-done.21.refs_6_), channel_id=1, source_target_pairs={{0,7},{1,0},{2,1},{3,2},{4,3},{5,4},{6,5},{7,6},{8,15},{9,8},{10,9... | collective-permute-start | bytes 589832 | tf_op jit(solution)/shard_map/ppermute | solution.py:420
  58.1 2.2 %collective-permute-done.10.refs_4_ = f32[96,512]{1,0:T(8,128)S(1)} collective-permute-done((f32[96,512]{1,0:T(8,128)S(1)}, f32[96,512]{1,0:T(8,128)S(1)}, u32[]{:S(2)}, u32[]{:S(2)}) %collective-permute-start.10) | collective-permute-done | bytes 196640 | tf_op jit(solution)/shard_map/ppermute | solution.py:420
  60.3 4.2 %collective-permute-done.25.refs_9_ = f32[96,512]{1,0:T(8,128)S(1)} collective-permute-done((f32[96,512]{1,0:T(8,128)S(1)}, f32[96,512]{1,0:T(8,128)S(1)}, u32[]{:S(2)}, u32[]{:S(2)}) %collective-permute-start.25) | collective-permute-done | bytes 196640 | tf_op jit(solution)/shard_map/ppermute | solution.py:420
  64.5 3.2 %collective-permute-start.8 = (f32[96,512]{1,0:T(8,128)S(1)}, f32[96,512]{1,0:T(8,128)S(1)}, u32[]{:S(2)}, u32[]{:S(2)}) collective-permute-start(f32[96,512]{1,0:T(8,128)S(1)} %collective-permute-done.7.refs_1_), channel_id=1, source_target_pairs={{0,7},{1,0},{2,1},{3,2},{4,3},{5,4},{6,5},{7,6},{8,15},{9,8},{10,9... | collective-permute-start | bytes 589832 | tf_op jit(solution)/shard_map/ppermute | solution.py:420
  67.8 0.1 collective-permute-start.23
  67.8 1.4 %collective-permute-done.11.refs_3_ = f32[96,512]{1,0:T(8,128)S(1)} collective-permute-done((f32[96,512]{1,0:T(8,128)S(1)}, f32[96,512]{1,0:T(8,128)S(1)}, u32[]{:S(2)}, u32[]{:S(2)}) %collective-permute-start.11) | collective-permute-done | bytes 196640 | tf_op jit(solution)/shard_map/ppermute | solution.py:420
  69.3 0.5 collective-permute-start.12
  69.8 3.7 %collective-permute-done.26.refs_8_ = f32[96,512]{1,0:T(8,128)S(1)} collective-permute-done((f32[96,512]{1,0:T(8,128)S(1)}, f32[96,512]{1,0:T(8,128)S(1)}, u32[]{:S(2)}, u32[]{:S(2)}) %collective-permute-start.26) | collective-permute-done | bytes 196640 | tf_op jit(solution)/shard_map/ppermute | solution.py:420
  73.5 3.2 %collective-permute-start.9 = (f32[96,512]{1,0:T(8,128)S(1)}, f32[96,512]{1,0:T(8,128)S(1)}, u32[]{:S(2)}, u32[]{:S(2)}) collective-permute-start(f32[96,512]{1,0:T(8,128)S(1)} %collective-permute-done.8.refs_2_), channel_id=1, source_target_pairs={{0,7},{1,0},{2,1},{3,2},{4,3},{5,4},{6,5},{7,6},{8,15},{9,8},{10,9... | collective-permute-start | bytes 589832 | tf_op jit(solution)/shard_map/ppermute | solution.py:420
  76.7 3.1 %collective-permute-start.24 = (f32[96,512]{1,0:T(8,128)S(1)}, f32[96,512]{1,0:T(8,128)S(1)}, u32[]{:S(2)}, u32[]{:S(2)}) collective-permute-start(f32[96,512]{1,0:T(8,128)S(1)} %collective-permute-done.23.refs_3_), channel_id=1, source_target_pairs={{0,7},{1,0},{2,1},{3,2},{4,3},{5,4},{6,5},{7,6},{8,15},{9,8},{10,9... | collective-permute-start | bytes 589832 | tf_op jit(solution)/shard_map/ppermute | solution.py:420
  79.8 1.9 %lists.1 = (s32[96]{0:T(128)S(1)}, s32[96]{0:T(128)S(1)}, s32[2]{0:T(128)S(1)}) custom-call(s32[2,96]{1,0:T(2,128)S(1)} %bitcast.21, s32[1]{0:T(128)S(6)} %copy.5.live_ref, s32[1]{0:T(128)} %bitcast.1.index_ref), custom_call_target="tpu_custom_call" | custom-call | tf_op jit(solution)/shard_map/lists/pallas_call | solution.py:125
  81.7 2.9 %split_near.1 = (bf16[10,384,256]{2,1,0:T(8,128)(2,1)S(1)}, f32[192,192]{1,0:T(8,128)S(1)}) custom-call(f32[96,512]{1,0:T(8,128)S(1)} %add_add_fusion.1.refs_0_, f32[96,512]{1,0:T(8,128)S(1)} %collective-permute-done.7.refs_1_, f32[96,512]{1,0:T(8,128)S(1)} %collective-permute-done.8.refs_2_, f32[96,512]{1,0:T(8,128)S(1)} %collective-permute-done.11.refs_3_, ...), custom_call_target="tpu_custom_call" | custom-call | tf_op jit(solution)/shard_map/split_near/pallas_call | solution.py:208
  84.6 6.1 %adjoint_near.1.refs_0_ = f32[16,192,256]{2,1,0:T(8,128)S(1)} custom-call(s32[96]{0:T(128)S(1)} %get-tuple-element.50.list_ref, s32[2,96]{1,0:T(2,128)S(1)} %bitcast.22, s32[2]{0:T(128)S(1)} %get-tuple-element.47.count_ref, s32[1]{0:T(128)} %bitcast.1.index_ref, bf16[96,256,256]{2,1,0:T(8,128)(2,1)S(1)} %get-tuple-element.48.buf_ref, ...), custom_call_target="tpu_custom_call" | custom-call | tf_op jit(solution)/shard_map/adjoint_near/pallas_call | solution.py:283
  90.8 1.9 %split_far.1 = (bf16[6,384,256]{2,1,0:T(8,128)(2,1)S(1)}, f32[192,128]{1,0:T(8,128)S(1)}) custom-call(f32[96,512]{1,0:T(8,128)S(1)} %collective-permute-done.9.refs_0_, f32[96,512]{1,0:T(8,128)S(1)} %collective-permute-done.13.refs_1_, f32[96,512]{1,0:T(8,128)S(1)} %collective-permute-done.12.refs_2_, f32[96,512]{1,0:T(8,128)S(1)} %collective-permute-done.23.refs_3_, ...), custom_call_target="tpu_custom_call" | custom-call | tf_op jit(solution)/shard_map/split_far/pallas_call | solution.py:208
  92.7 4.6 %adjoint_far.1 = (f32[16,192,128]{2,1,0:T(8,128)S(1)}, f32[16,192,128]{2,1,0:T(8,128)S(1)}) custom-call(s32[96]{0:T(128)S(1)} %get-tuple-element.46.list_ref, s32[2,96]{1,0:T(2,128)S(1)} %bitcast.23, s32[2]{0:T(128)S(1)} %get-tuple-element.47.count_ref, s32[1]{0:T(128)} %bitcast.1.index_ref, bf16[96,256,256]{2,1,0:T(8,128)(2,1)S(1)} %get-tuple-element.48.buf_ref, ...), custom_call_target="tpu_custom_call" | custom-call | tf_op jit(solution)/shard_map/adjoint_far/pallas_call | solution.py:283
  97.3 0.1 collective-permute-start.35
  97.4 0.5 collective-permute-start.28
  97.9 3.0 %collective-permute-done.28 = f32[192,128]{1,0:T(8,128)S(1)} collective-permute-done((f32[192,128]{1,0:T(8,128)S(1)}, f32[192,128]{1,0:T(8,128)S(1)}, u32[]{:S(2)}, u32[]{:S(2)}) %collective-permute-start.28) | collective-permute-done | bytes 98336 | tf_op jit(solution)/shard_map/ppermute | solution.py:420
  101.0 4.6 %collective-permute-start.29 = (f32[192,128]{1,0:T(8,128)S(1)}, f32[192,128]{1,0:T(8,128)S(1)}, u32[]{:S(2)}, u32[]{:S(2)}) collective-permute-start(f32[192,128]{1,0:T(8,128)S(1)} %add.110), channel_id=1, source_target_pairs={{0,128},{8,40},{16,144},{24,56},{32,160},{40,8},{48,176},{56,24},{... | collective-permute-start | bytes 294920 | tf_op jit(solution)/shard_map/ppermute | solution.py:463
  105.5 0.2 add.117
  105.7 0.1 fusion.5
  105.8 0.1 collective-permute-start.36
  105.9 0.1 collective-permute-start.37
  106.0 2.0 %collective-permute-start.38 = (f32[4,192,128]{2,1,0:T(8,128)S(1)}, f32[4,192,128]{2,1,0:T(8,128)S(1)}, u32[]{:S(2)}, u32[]{:S(2)}) collective-permute-start(f32[4,192,128]{2,1,0:T(8,128)S(1)} %get-tuple-element.55), channel_id=1, source_target_pairs={{0,192},{8,56},{16,208},{24,8},{32,224},{40,24},{48,240},{56,40},{... | collective-permute-start | bytes 1179656 | tf_op jit(solution)/shard_map/ppermute | solution.py:463
  108.0 2.0 %collective-permute-start.30 = (f32[192,128]{1,0:T(8,128)S(1)}, f32[192,128]{1,0:T(8,128)S(1)}, u32[]{:S(2)}, u32[]{:S(2)}) collective-permute-start(f32[192,128]{1,0:T(8,128)S(1)} %add.110), channel_id=1, source_target_pairs={{0,64},{8,24},{16,80},{24,40},{32,96},{40,56},{48,112},{56,8},{64,... | collective-permute-start | bytes 294920 | tf_op jit(solution)/shard_map/ppermute | solution.py:463
  110.0 0.6 collective-permute-start.31
  110.6 7.1 %collective-permute-done.30 = f32[192,128]{1,0:T(8,128)S(1)} collective-permute-done((f32[192,128]{1,0:T(8,128)S(1)}, f32[192,128]{1,0:T(8,128)S(1)}, u32[]{:S(2)}, u32[]{:S(2)}) %collective-permute-start.30) | collective-permute-done | bytes 98336 | tf_op jit(solution)/shard_map/ppermute | solution.py:463
  117.7 2.7 %collective-permute-done.31 = f32[192,128]{1,0:T(8,128)S(1)} collective-permute-done((f32[192,128]{1,0:T(8,128)S(1)}, f32[192,128]{1,0:T(8,128)S(1)}, u32[]{:S(2)}, u32[]{:S(2)}) %collective-permute-start.31) | collective-permute-done | bytes 98336 | tf_op jit(solution)/shard_map/ppermute | solution.py:463
  120.5 2.7 %collective-permute-start.32 = (f32[192,128]{1,0:T(8,128)S(1)}, f32[192,128]{1,0:T(8,128)S(1)}, u32[]{:S(2)}, u32[]{:S(2)}) collective-permute-start(f32[192,128]{1,0:T(8,128)S(1)} %add_add_fusion.3), channel_id=1, source_target_pairs={{0,32},{8,136},{16,48},{24,152},{32,0},{40,168},{48,16},{56,184},{... | collective-permute-start | bytes 294920 | tf_op jit(solution)/shard_map/ppermute | solution.py:463
  123.1 3.2 %collective-permute-start.34 = (f32[192,128]{1,0:T(8,128)S(1)}, f32[192,128]{1,0:T(8,128)S(1)}, u32[]{:S(2)}, u32[]{:S(2)}) collective-permute-start(f32[192,128]{1,0:T(8,128)S(1)} %add_add_fusion.3), channel_id=1, source_target_pairs={{0,48},{8,200},{16,0},{24,216},{32,16},{40,232},{48,32},{56,248},{... | collective-permute-start | bytes 294920 | tf_op jit(solution)/shard_map/ppermute | solution.py:463
  126.4 0.1 fusion.1
  126.5 0.1 collective-permute-start.39
  126.6 0.9 collective-permute-start.40
  127.4 2.5 %collective-permute-start.41 = (f32[192,128]{1,0:T(8,128)S(1)}, f32[192,128]{1,0:T(8,128)S(1)}, u32[]{:S(2)}, u32[]{:S(2)}) collective-permute-start(f32[192,128]{1,0:T(8,128)S(1)} %get-tuple-element.58), channel_id=1, source_target_pairs={{0,48},{8,200},{16,0},{24,216},{32,16},{40,232},{48,32},{56,248},{... | collective-permute-start | bytes 294920 | tf_op jit(solution)/shard_map/ppermute | solution.py:463
  129.9 8.6 %factor.1.factor_ref = f32[192,192]{1,0:T(8,128)S(1)} custom-call(f32[192,128]{1,0:T(8,128)S(1)} %add_add_fusion.2.packed_ref), custom_call_target="tpu_custom_call" | custom-call | tf_op jit(solution)/shard_map/factor/pallas_call | solution.py:388
  138.5 1.2 shard_map.50
  139.8 1.0 shard_map.51
  (53 shorter events, 0.6 us)
Async XLA Ops:
  1.3 0.7 copy-start
  10.4 8.1 %collective-permute-start.17 = (f32[96,512]{1,0:T(8,128)S(1)}, f32[96,512]{1,0:T(8,128)S(1)}, u32[]{:S(2)}, u32[]{:S(2)}) collective-permute-start(f32[96,512]{1,0:T(8,128)S(1)} %get-tuple-element.39), channel_id=1, source_target_pairs={{0,7},{1,0},{2,1},{3,2},{4,3},{5,4},{6,5},{7,6},{8,15},{9,8},{10,9... | collective-permute-start | bytes 589832 | tf_op jit(solution)/shard_map/ppermute | solution.py:420
  15.2 8.8 %collective-permute-start = (f32[96,512]{1,0:T(8,128)S(1)}, f32[96,512]{1,0:T(8,128)S(1)}, u32[]{:S(2)}, u32[]{:S(2)}) collective-permute-start(f32[96,512]{1,0:T(8,128)S(1)} %get-tuple-element.28), channel_id=1, source_target_pairs={{0,1},{1,2},{2,3},{3,4},{4,5},{5,6},{6,7},{7,0},{8,9},{9,10},{10,1... | collective-permute-start | bytes 589832 | tf_op jit(solution)/shard_map/ppermute | solution.py:420
  15.2 10.9 %collective-permute-start.14 = (f32[96,512]{1,0:T(8,128)S(1)}, f32[96,512]{1,0:T(8,128)S(1)}, u32[]{:S(2)}, u32[]{:S(2)}) collective-permute-start(f32[96,512]{1,0:T(8,128)S(1)} %get-tuple-element.36), channel_id=1, source_target_pairs={{0,1},{1,2},{2,3},{3,4},{4,5},{5,6},{6,7},{7,0},{8,9},{9,10},{10,1... | collective-permute-start | bytes 589832 | tf_op jit(solution)/shard_map/ppermute | solution.py:420
  18.4 9.1 %collective-permute-start.18 = (f32[96,512]{1,0:T(8,128)S(1)}, f32[96,512]{1,0:T(8,128)S(1)}, u32[]{:S(2)}, u32[]{:S(2)}) collective-permute-start(f32[96,512]{1,0:T(8,128)S(1)} %add.105), channel_id=1, source_target_pairs={{0,7},{1,0},{2,1},{3,2},{4,3},{5,4},{6,5},{7,6},{8,15},{9,8},{10,9... | collective-permute-start | bytes 589832 | tf_op jit(solution)/shard_map/ppermute | solution.py:420
  22.2 9.1 %collective-permute-start.4 = (f32[96,512]{1,0:T(8,128)S(1)}, f32[96,512]{1,0:T(8,128)S(1)}, u32[]{:S(2)}, u32[]{:S(2)}) collective-permute-start(f32[96,512]{1,0:T(8,128)S(1)} %get-tuple-element.32), channel_id=1, source_target_pairs={{0,7},{1,0},{2,1},{3,2},{4,3},{5,4},{6,5},{7,6},{8,15},{9,8},{10,9... | collective-permute-start | bytes 589832 | tf_op jit(solution)/shard_map/ppermute | solution.py:420
  24.1 11.1 %collective-permute-start.1 = (f32[96,512]{1,0:T(8,128)S(1)}, f32[96,512]{1,0:T(8,128)S(1)}, u32[]{:S(2)}, u32[]{:S(2)}) collective-permute-start(f32[96,512]{1,0:T(8,128)S(1)} %add.96), channel_id=1, source_target_pairs={{0,1},{1,2},{2,3},{3,4},{4,5},{5,6},{6,7},{7,0},{8,9},{9,10},{10,1... | collective-permute-start | bytes 589832 | tf_op jit(solution)/shard_map/ppermute | solution.py:420
  26.2 9.3 %collective-permute-start.15 = (f32[96,512]{1,0:T(8,128)S(1)}, f32[96,512]{1,0:T(8,128)S(1)}, u32[]{:S(2)}, u32[]{:S(2)}) collective-permute-start(f32[96,512]{1,0:T(8,128)S(1)} %add.103), channel_id=1, source_target_pairs={{0,1},{1,2},{2,3},{3,4},{4,5},{5,6},{6,7},{7,0},{8,9},{9,10},{10,1... | collective-permute-start | bytes 589832 | tf_op jit(solution)/shard_map/ppermute | solution.py:420
  27.5 8.9 %collective-permute-start.19 = (f32[96,512]{1,0:T(8,128)S(1)}, f32[96,512]{1,0:T(8,128)S(1)}, u32[]{:S(2)}, u32[]{:S(2)}) collective-permute-start(f32[96,512]{1,0:T(8,128)S(1)} %add.106), channel_id=1, source_target_pairs={{0,7},{1,0},{2,1},{3,2},{4,3},{5,4},{6,5},{7,6},{8,15},{9,8},{10,9... | collective-permute-start | bytes 589832 | tf_op jit(solution)/shard_map/ppermute | solution.py:420
  31.4 8.8 %collective-permute-start.5 = (f32[96,512]{1,0:T(8,128)S(1)}, f32[96,512]{1,0:T(8,128)S(1)}, u32[]{:S(2)}, u32[]{:S(2)}) collective-permute-start(f32[96,512]{1,0:T(8,128)S(1)} %add.99), channel_id=1, source_target_pairs={{0,7},{1,0},{2,1},{3,2},{4,3},{5,4},{6,5},{7,6},{8,15},{9,8},{10,9... | collective-permute-start | bytes 589832 | tf_op jit(solution)/shard_map/ppermute | solution.py:420
  35.2 8.6 %collective-permute-start.2 = (f32[96,512]{1,0:T(8,128)S(1)}, f32[96,512]{1,0:T(8,128)S(1)}, u32[]{:S(2)}, u32[]{:S(2)}) collective-permute-start(f32[96,512]{1,0:T(8,128)S(1)} %add.97), channel_id=1, source_target_pairs={{0,1},{1,2},{2,3},{3,4},{4,5},{5,6},{6,7},{7,0},{8,9},{9,10},{10,1... | collective-permute-start | bytes 589832 | tf_op jit(solution)/shard_map/ppermute | solution.py:420
  35.5 8.8 %collective-permute-start.16 = (f32[96,512]{1,0:T(8,128)S(1)}, f32[96,512]{1,0:T(8,128)S(1)}, u32[]{:S(2)}, u32[]{:S(2)}) collective-permute-start(f32[96,512]{1,0:T(8,128)S(1)} %add.104), channel_id=1, source_target_pairs={{0,1},{1,2},{2,3},{3,4},{4,5},{5,6},{6,7},{7,0},{8,9},{9,10},{10,1... | collective-permute-start | bytes 589832 | tf_op jit(solution)/shard_map/ppermute | solution.py:420
  36.4 43.4 %copy-start.1 = (s32[96,2]{0,1:T(2,128)S(1)}, s32[96,2]{0,1:T(2,128)}, u32[]{:S(2)}) copy-start(s32[96,2]{0,1:T(2,128)} %param.4) | copy-start | bytes 2308
  36.4 8.7 %collective-permute-start.20 = (f32[96,512]{1,0:T(8,128)S(1)}, f32[96,512]{1,0:T(8,128)S(1)}, u32[]{:S(2)}, u32[]{:S(2)}) collective-permute-start(f32[96,512]{1,0:T(8,128)S(1)} %add.107), channel_id=1, source_target_pairs={{0,7},{1,0},{2,1},{3,2},{4,3},{5,4},{6,5},{7,6},{8,15},{9,8},{10,9... | collective-permute-start | bytes 589832 | tf_op jit(solution)/shard_map/ppermute | solution.py:420
  40.2 8.9 %collective-permute-start.6 = (f32[96,512]{1,0:T(8,128)S(1)}, f32[96,512]{1,0:T(8,128)S(1)}, u32[]{:S(2)}, u32[]{:S(2)}) collective-permute-start(f32[96,512]{1,0:T(8,128)S(1)} %add.100), channel_id=1, source_target_pairs={{0,7},{1,0},{2,1},{3,2},{4,3},{5,4},{6,5},{7,6},{8,15},{9,8},{10,9... | collective-permute-start | bytes 589832 | tf_op jit(solution)/shard_map/ppermute | solution.py:420
  43.8 7.6 %collective-permute-start.3 = (f32[96,512]{1,0:T(8,128)S(1)}, f32[96,512]{1,0:T(8,128)S(1)}, u32[]{:S(2)}, u32[]{:S(2)}) collective-permute-start(f32[96,512]{1,0:T(8,128)S(1)} %add.98), channel_id=1, source_target_pairs={{0,1},{1,2},{2,3},{3,4},{4,5},{5,6},{6,7},{7,0},{8,9},{9,10},{10,1... | collective-permute-start | bytes 589832 | tf_op jit(solution)/shard_map/ppermute | solution.py:420
  45.1 9.7 %collective-permute-start.21 = (f32[96,512]{1,0:T(8,128)S(1)}, f32[96,512]{1,0:T(8,128)S(1)}, u32[]{:S(2)}, u32[]{:S(2)}) collective-permute-start(f32[96,512]{1,0:T(8,128)S(1)} %add_add_fusion.refs_5_.refs_1_), channel_id=1, source_target_pairs={{0,7},{1,0},{2,1},{3,2},{4,3},{5,4},{6,5},{7,6},{8,15},{9,8},{10,9... | collective-permute-start | bytes 589832 | tf_op jit(solution)/shard_map/ppermute | solution.py:420
  51.4 8.9 %collective-permute-start.10 = (f32[96,512]{1,0:T(8,128)S(1)}, f32[96,512]{1,0:T(8,128)S(1)}, u32[]{:S(2)}, u32[]{:S(2)}) collective-permute-start(f32[96,512]{1,0:T(8,128)S(1)} %add_add_fusion.1.refs_0_), channel_id=1, source_target_pairs={{0,1},{1,2},{2,3},{3,4},{4,5},{5,6},{6,7},{7,0},{8,9},{9,10},{10,1... | collective-permute-start | bytes 589832 | tf_op jit(solution)/shard_map/ppermute | solution.py:420
  51.5 13.0 %collective-permute-start.25 = (f32[96,512]{1,0:T(8,128)S(1)}, f32[96,512]{1,0:T(8,128)S(1)}, u32[]{:S(2)}, u32[]{:S(2)}) collective-permute-start(f32[96,512]{1,0:T(8,128)S(1)} %add_add_fusion.refs_5_.refs_1_), channel_id=1, source_target_pairs={{0,1},{1,2},{2,3},{3,4},{4,5},{5,6},{6,7},{7,0},{8,9},{9,10},{10,1... | collective-permute-start | bytes 589832 | tf_op jit(solution)/shard_map/ppermute | solution.py:420
  51.6 12.9 %collective-permute-start.7 = (f32[96,512]{1,0:T(8,128)S(1)}, f32[96,512]{1,0:T(8,128)S(1)}, u32[]{:S(2)}, u32[]{:S(2)}) collective-permute-start(f32[96,512]{1,0:T(8,128)S(1)} %add_add_fusion.1.refs_0_), channel_id=1, source_target_pairs={{0,7},{1,0},{2,1},{3,2},{4,3},{5,4},{6,5},{7,6},{8,15},{9,8},{10,9... | collective-permute-start | bytes 589832 | tf_op jit(solution)/shard_map/ppermute | solution.py:420
  54.8 12.9 %collective-permute-start.22 = (f32[96,512]{1,0:T(8,128)S(1)}, f32[96,512]{1,0:T(8,128)S(1)}, u32[]{:S(2)}, u32[]{:S(2)}) collective-permute-start(f32[96,512]{1,0:T(8,128)S(1)} %collective-permute-done.21.refs_6_), channel_id=1, source_target_pairs={{0,7},{1,0},{2,1},{3,2},{4,3},{5,4},{6,5},{7,6},{8,15},{9,8},{10,9... | collective-permute-start | bytes 589832 | tf_op jit(solution)/shard_map/ppermute | solution.py:420
  60.3 9.0 %collective-permute-start.11 = (f32[96,512]{1,0:T(8,128)S(1)}, f32[96,512]{1,0:T(8,128)S(1)}, u32[]{:S(2)}, u32[]{:S(2)}) collective-permute-start(f32[96,512]{1,0:T(8,128)S(1)} %collective-permute-done.10.refs_4_), channel_id=1, source_target_pairs={{0,1},{1,2},{2,3},{3,4},{4,5},{5,6},{6,7},{7,0},{8,9},{9,10},{10,1... | collective-permute-start | bytes 589832 | tf_op jit(solution)/shard_map/ppermute | solution.py:420
  64.5 9.0 %collective-permute-start.26 = (f32[96,512]{1,0:T(8,128)S(1)}, f32[96,512]{1,0:T(8,128)S(1)}, u32[]{:S(2)}, u32[]{:S(2)}) collective-permute-start(f32[96,512]{1,0:T(8,128)S(1)} %collective-permute-done.25.refs_9_), channel_id=1, source_target_pairs={{0,1},{1,2},{2,3},{3,4},{4,5},{5,6},{6,7},{7,0},{8,9},{9,10},{10,1... | collective-permute-start | bytes 589832 | tf_op jit(solution)/shard_map/ppermute | solution.py:420
  64.5 9.0 %collective-permute-start.8 = (f32[96,512]{1,0:T(8,128)S(1)}, f32[96,512]{1,0:T(8,128)S(1)}, u32[]{:S(2)}, u32[]{:S(2)}) collective-permute-start(f32[96,512]{1,0:T(8,128)S(1)} %collective-permute-done.7.refs_1_), channel_id=1, source_target_pairs={{0,7},{1,0},{2,1},{3,2},{4,3},{5,4},{6,5},{7,6},{8,15},{9,8},{10,9... | collective-permute-start | bytes 589832 | tf_op jit(solution)/shard_map/ppermute | solution.py:420
  67.8 9.0 %collective-permute-start.23 = (f32[96,512]{1,0:T(8,128)S(1)}, f32[96,512]{1,0:T(8,128)S(1)}, u32[]{:S(2)}, u32[]{:S(2)}) collective-permute-start(f32[96,512]{1,0:T(8,128)S(1)} %collective-permute-done.22.refs_7_), channel_id=1, source_target_pairs={{0,7},{1,0},{2,1},{3,2},{4,3},{5,4},{6,5},{7,6},{8,15},{9,8},{10,9... | collective-permute-start | bytes 589832 | tf_op jit(solution)/shard_map/ppermute | solution.py:420
  69.3 10.5 %collective-permute-start.12 = (f32[96,512]{1,0:T(8,128)S(1)}, f32[96,512]{1,0:T(8,128)S(1)}, u32[]{:S(2)}, u32[]{:S(2)}) collective-permute-start(f32[96,512]{1,0:T(8,128)S(1)} %collective-permute-done.11.refs_3_), channel_id=1, source_target_pairs={{0,1},{1,2},{2,3},{3,4},{4,5},{5,6},{6,7},{7,0},{8,9},{9,10},{10,1... | collective-permute-start | bytes 589832 | tf_op jit(solution)/shard_map/ppermute | solution.py:420
  73.5 17.3 %collective-permute-start.27 = (f32[96,512]{1,0:T(8,128)S(1)}, f32[96,512]{1,0:T(8,128)S(1)}, u32[]{:S(2)}, u32[]{:S(2)}) collective-permute-start(f32[96,512]{1,0:T(8,128)S(1)} %collective-permute-done.26.refs_8_), channel_id=1, source_target_pairs={{0,1},{1,2},{2,3},{3,4},{4,5},{5,6},{6,7},{7,0},{8,9},{9,10},{10,1... | collective-permute-start | bytes 589832 | tf_op jit(solution)/shard_map/ppermute | solution.py:420
  73.5 17.3 %collective-permute-start.9 = (f32[96,512]{1,0:T(8,128)S(1)}, f32[96,512]{1,0:T(8,128)S(1)}, u32[]{:S(2)}, u32[]{:S(2)}) collective-permute-start(f32[96,512]{1,0:T(8,128)S(1)} %collective-permute-done.8.refs_2_), channel_id=1, source_target_pairs={{0,7},{1,0},{2,1},{3,2},{4,3},{5,4},{6,5},{7,6},{8,15},{9,8},{10,9... | collective-permute-start | bytes 589832 | tf_op jit(solution)/shard_map/ppermute | solution.py:420
  76.7 14.0 %collective-permute-start.24 = (f32[96,512]{1,0:T(8,128)S(1)}, f32[96,512]{1,0:T(8,128)S(1)}, u32[]{:S(2)}, u32[]{:S(2)}) collective-permute-start(f32[96,512]{1,0:T(8,128)S(1)} %collective-permute-done.23.refs_3_), channel_id=1, source_target_pairs={{0,7},{1,0},{2,1},{3,2},{4,3},{5,4},{6,5},{7,6},{8,15},{9,8},{10,9... | collective-permute-start | bytes 589832 | tf_op jit(solution)/shard_map/ppermute | solution.py:420
  79.8 11.0 %collective-permute-start.13 = (f32[96,512]{1,0:T(8,128)S(1)}, f32[96,512]{1,0:T(8,128)S(1)}, u32[]{:S(2)}, u32[]{:S(2)}) collective-permute-start(f32[96,512]{1,0:T(8,128)S(1)} %collective-permute-done.12.refs_2_), channel_id=1, source_target_pairs={{0,1},{1,2},{2,3},{3,4},{4,5},{5,6},{6,7},{7,0},{8,9},{9,10},{10,1... | collective-permute-start | bytes 589832 | tf_op jit(solution)/shard_map/ppermute | solution.py:420
  97.3 8.2 %collective-permute-start.35 = (f32[16,192,128]{2,1,0:T(8,128)S(1)}, f32[16,192,128]{2,1,0:T(8,128)S(1)}, u32[]{:S(2)}, u32[]{:S(2)}) collective-permute-start(f32[16,192,128]{2,1,0:T(8,128)S(1)} %get-tuple-element.53), channel_id=1, source_target_pairs={{0,8},{8,0},{1,9},{9,1},{2,10},{10,2},{3,11},{11,3},{4,12},{12,4},... | collective-permute-start | bytes 4718600 | tf_op jit(solution)/shard_map/ppermute | solution.py:420
  97.4 3.5 %collective-permute-start.28 = (f32[192,128]{1,0:T(8,128)S(1)}, f32[192,128]{1,0:T(8,128)S(1)}, u32[]{:S(2)}, u32[]{:S(2)}) collective-permute-start(f32[192,128]{1,0:T(8,128)S(1)} %get-tuple-element.45), channel_id=1, source_target_pairs={{0,8},{8,0},{1,9},{9,1},{2,10},{10,2},{3,11},{11,3},{4,12},{12,4},... | collective-permute-start | bytes 294920 | tf_op jit(solution)/shard_map/ppermute | solution.py:420
  101.0 9.0 %collective-permute-start.29 = (f32[192,128]{1,0:T(8,128)S(1)}, f32[192,128]{1,0:T(8,128)S(1)}, u32[]{:S(2)}, u32[]{:S(2)}) collective-permute-start(f32[192,128]{1,0:T(8,128)S(1)} %add.110), channel_id=1, source_target_pairs={{0,128},{8,40},{16,144},{24,56},{32,160},{40,8},{48,176},{56,24},{... | collective-permute-start | bytes 294920 | tf_op jit(solution)/shard_map/ppermute | solution.py:463
  105.8 17.3 %collective-permute-start.36 = (f32[4,192,128]{2,1,0:T(8,128)S(1)}, f32[4,192,128]{2,1,0:T(8,128)S(1)}, u32[]{:S(2)}, u32[]{:S(2)}) collective-permute-start(f32[4,192,128]{2,1,0:T(8,128)S(1)} %get-tuple-element.54), channel_id=1, source_target_pairs={{0,128},{8,40},{16,144},{24,56},{32,160},{40,8},{48,176},{56,24},{... | collective-permute-start | bytes 1179656 | tf_op jit(solution)/shard_map/ppermute | solution.py:463
  105.9 20.5 %collective-permute-start.37 = (f32[4,192,128]{2,1,0:T(8,128)S(1)}, f32[4,192,128]{2,1,0:T(8,128)S(1)}, u32[]{:S(2)}, u32[]{:S(2)}) collective-permute-start(f32[4,192,128]{2,1,0:T(8,128)S(1)} %get-tuple-element.56), channel_id=1, source_target_pairs={{0,64},{8,24},{16,80},{24,40},{32,96},{40,56},{48,112},{56,8},{64,... | collective-permute-start | bytes 1179656 | tf_op jit(solution)/shard_map/ppermute | solution.py:463
  106.0 20.4 %collective-permute-start.38 = (f32[4,192,128]{2,1,0:T(8,128)S(1)}, f32[4,192,128]{2,1,0:T(8,128)S(1)}, u32[]{:S(2)}, u32[]{:S(2)}) collective-permute-start(f32[4,192,128]{2,1,0:T(8,128)S(1)} %get-tuple-element.55), channel_id=1, source_target_pairs={{0,192},{8,56},{16,208},{24,8},{32,224},{40,24},{48,240},{56,40},{... | collective-permute-start | bytes 1179656 | tf_op jit(solution)/shard_map/ppermute | solution.py:463
  108.0 9.7 %collective-permute-start.30 = (f32[192,128]{1,0:T(8,128)S(1)}, f32[192,128]{1,0:T(8,128)S(1)}, u32[]{:S(2)}, u32[]{:S(2)}) collective-permute-start(f32[192,128]{1,0:T(8,128)S(1)} %add.110), channel_id=1, source_target_pairs={{0,64},{8,24},{16,80},{24,40},{32,96},{40,56},{48,112},{56,8},{64,... | collective-permute-start | bytes 294920 | tf_op jit(solution)/shard_map/ppermute | solution.py:463
  110.0 10.4 %collective-permute-start.31 = (f32[192,128]{1,0:T(8,128)S(1)}, f32[192,128]{1,0:T(8,128)S(1)}, u32[]{:S(2)}, u32[]{:S(2)}) collective-permute-start(f32[192,128]{1,0:T(8,128)S(1)} %add.110), channel_id=1, source_target_pairs={{0,192},{8,56},{16,208},{24,8},{32,224},{40,24},{48,240},{56,40},{... | collective-permute-start | bytes 294920 | tf_op jit(solution)/shard_map/ppermute | solution.py:463
  120.5 7.0 %collective-permute-start.32 = (f32[192,128]{1,0:T(8,128)S(1)}, f32[192,128]{1,0:T(8,128)S(1)}, u32[]{:S(2)}, u32[]{:S(2)}) collective-permute-start(f32[192,128]{1,0:T(8,128)S(1)} %add_add_fusion.3), channel_id=1, source_target_pairs={{0,32},{8,136},{16,48},{24,152},{32,0},{40,168},{48,16},{56,184},{... | collective-permute-start | bytes 294920 | tf_op jit(solution)/shard_map/ppermute | solution.py:463
  123.1 6.8 %collective-permute-start.33 = (f32[192,128]{1,0:T(8,128)S(1)}, f32[192,128]{1,0:T(8,128)S(1)}, u32[]{:S(2)}, u32[]{:S(2)}) collective-permute-start(f32[192,128]{1,0:T(8,128)S(1)} %add_add_fusion.3), channel_id=1, source_target_pairs={{0,16},{8,72},{16,32},{24,88},{32,48},{40,104},{48,0},{56,120},{64... | collective-permute-start | bytes 294920 | tf_op jit(solution)/shard_map/ppermute | solution.py:463
  123.1 6.8 %collective-permute-start.34 = (f32[192,128]{1,0:T(8,128)S(1)}, f32[192,128]{1,0:T(8,128)S(1)}, u32[]{:S(2)}, u32[]{:S(2)}) collective-permute-start(f32[192,128]{1,0:T(8,128)S(1)} %add_add_fusion.3), channel_id=1, source_target_pairs={{0,48},{8,200},{16,0},{24,216},{32,16},{40,232},{48,32},{56,248},{... | collective-permute-start | bytes 294920 | tf_op jit(solution)/shard_map/ppermute | solution.py:463
  126.5 13.3 %collective-permute-start.39 = (f32[192,128]{1,0:T(8,128)S(1)}, f32[192,128]{1,0:T(8,128)S(1)}, u32[]{:S(2)}, u32[]{:S(2)}) collective-permute-start(f32[192,128]{1,0:T(8,128)S(1)} %get-tuple-element.57), channel_id=1, source_target_pairs={{0,32},{8,136},{16,48},{24,152},{32,0},{40,168},{48,16},{56,184},{... | collective-permute-start | bytes 294920 | tf_op jit(solution)/shard_map/ppermute | solution.py:463
  126.6 13.2 %collective-permute-start.40 = (f32[192,128]{1,0:T(8,128)S(1)}, f32[192,128]{1,0:T(8,128)S(1)}, u32[]{:S(2)}, u32[]{:S(2)}) collective-permute-start(f32[192,128]{1,0:T(8,128)S(1)} %get-tuple-element.59), channel_id=1, source_target_pairs={{0,16},{8,72},{16,32},{24,88},{32,48},{40,104},{48,0},{56,120},{64... | collective-permute-start | bytes 294920 | tf_op jit(solution)/shard_map/ppermute | solution.py:463
  127.4 12.3 %collective-permute-start.41 = (f32[192,128]{1,0:T(8,128)S(1)}, f32[192,128]{1,0:T(8,128)S(1)}, u32[]{:S(2)}, u32[]{:S(2)}) collective-permute-start(f32[192,128]{1,0:T(8,128)S(1)} %get-tuple-element.58), channel_id=1, source_target_pairs={{0,48},{8,200},{16,0},{24,216},{32,16},{40,232},{48,32},{56,248},{... | collective-permute-start | bytes 294920 | tf_op jit(solution)/shard_map/ppermute | solution.py:463

commit v5 on v4

--- a/solution.py
+++ b/solution.py
@@ -18,7 +18,7 @@
 KH = K // 2
 CH = RT * TB // NZ
 SLOTS = 8
-UNROLL = 4
+UNROLL = 8
 NEAR = (0, 1, 2, 6, 7)
 FAR = (3, 4, 5)
 STEPS = NT // SLOTS
@@ -74,15 +74,14 @@
     lax.fori_loop(0, batches, fetch, 0)
     k_ids = lax.broadcasted_iota(jnp.int32, (K, TB), 0)
     g_ids = lax.broadcasted_iota(jnp.int32, (K, TB), 1)
-    base = g_ids * K + k_ids
+    base = (g_ids * K + k_ids) * 747796405
 
     def fill(j, carry):
-        h = base + (z * CT + j) * (TB * K)
-        h = h * 747796405 + 1442695040
+        h = base + ((z * CT + j) * (TB * K) * 747796405 + 1442695040)
         h = h ^ (h >> 15)
         h = h * 1103515245 + 12345
         h = h ^ (h >> 13)
-        omega_ref[j] = (1 - 2 * ((h >> 9) & 1)).astype(jnp.float32).astype(jnp.bfloat16)
+        omega_ref[j] = jnp.where((h & 512) == 0, 1.0, -1.0).astype(jnp.bfloat16)
         acc_ref[j] = jnp.zeros((K, TB), jnp.float32)
         return carry
 
@@ -228,7 +227,7 @@
         acc_out = refs[0]
     acc_ref = refs[-1]
     total = count_ref[1] if last else count_ref[0]
-    steps = (total + UNROLL - 1) >> 2
+    steps = (total + UNROLL - 1) >> 3
     x, y, core, z = place_on_mesh(index_ref)
 
     def clear(j, carry):
@@ -472,7 +471,7 @@
 
 def per_device(tiles, tile_coords, live_counts):
     index = lax.axis_index(("x", "y", "core", "z")).astype(jnp.int32).reshape(1)
-    coords = tile_coords.T
+    coords = pltpu.with_memory_space_constraint(tile_coords.T, pltpu.HBM)
     tiles = pltpu.with_memory_space_constraint(tiles, pltpu.HBM)
     parts, held = sketch_call(coords, live_counts, index, tiles)
     near_slots, far_slots, count = lists_call(coords, live_counts, index)

time: 143 us -> 142 us (level)
  no operation moved by 1% of the time
where the time goes in v5:
time: 142 us; the launch traced here: 139 us
  starting transfers between devices  64.5 us (45%)
  waiting for transfers between devices  36.5 us (26%)
  Pallas kernels  35.7 us (25%)
  between operations  1.57 us (1%)
    ppermute x30, starting transfers between devices, shift(): return lax.ppermute(x, axis, [(i, (i + by) % size) for i in range(size)])  46.5 us
    ppermute x30, waiting for transfers between devices, shift(): return lax.ppermute(x, axis, [(i, (i + by) % size) for i in range(size)])  26.6 us
    ppermute x12, starting transfers between devices, shift_xy(): return lax.ppermute(x, ('x', 'y', 'core'), pairs)  18 us
    ppermute x12, waiting for transfers between devices, shift_xy(): return lax.ppermute(x, ('x', 'y', 'core'), pairs)  9.86 us
    pallas_call x2, Pallas kernels, adjoint_call(): pl.pallas_call(functools.partial(adjoint_body, dists=dists, last=last), n...  9.84 us
    pallas_call x1, Pallas kernels, factor_call(): pl.pallas_call(functools.partial(factor_body, scale=scale), name='factor'...  8.55 us
    pallas_call x1, Pallas kernels, sketch_call(): pl.pallas_call(sketch_body, name='sketch', in_specs=[SMEM_SPEC] * 3 + [HB...  8.3 us
    pallas_call x2, Pallas kernels, split_call(): pl.pallas_call(functools.partial(split_body, n=n, last=bool(carried)), na...  4.73 us
  transfers between devices with their start and end apart: 42, of which 16 were waited for; matrix products, arithmetic and copies ran while one was open for 1% of the time, Pallas kernels for 15%

profile of v5, /device:TPU:2, one launch (start us, length us, event | category | flops | bytes accessed | tf_op | source)
XLA Modules:
  0.0 139.0 jit_solution(13811726274575538331)
XLA Ops:
  1.3 8.3 %sketch.1 = (f32[96,512]{1,0:T(8,128)S(1)}, f32[96,512]{1,0:T(8,128)S(1)}, f32[96,512]{1,0:T(8,128)S(1)}, f32[96,512]{1,0:T(8,128)S(1)}, f32[96,512]{1,0:T(8,128...) custom-call(s32[2,96]{1,0:T(2,128)} %bitcast.22, ...), custom_call_target="tpu_custom_call" | custom-call | tf_op jit(solution)/shard_map/sketch/pallas_call | solution.py:139
  9.6 4.9 %collective-permute-start.17 = (f32[96,512]{1,0:T(8,128)S(1)}, f32[96,512]{1,0:T(8,128)S(1)}, u32[]{:S(2)}, u32[]{:S(2)}) collective-permute-start(f32[96,512]{1,0:T(8,128)S(1)} %get-tuple-element.39), channel_id=1, source_target_pairs={{0,7},{1,0},{2,1},{3,2},{4,3},{5,4},{6,5},{7,6},{8,15},{9,8},{10,9... | collective-permute-start | bytes 589832 | tf_op jit(solution)/shard_map/ppermute | solution.py:419
  14.5 3.2 %collective-permute-done.17 = f32[96,512]{1,0:T(8,128)S(1)} collective-permute-done((f32[96,512]{1,0:T(8,128)S(1)}, f32[96,512]{1,0:T(8,128)S(1)}, u32[]{:S(2)}, u32[]{:S(2)}) %collective-permute-start.17) | collective-permute-done | bytes 196640 | tf_op jit(solution)/shard_map/ppermute | solution.py:419
  17.7 3.8 %collective-permute-start.18 = (f32[96,512]{1,0:T(8,128)S(1)}, f32[96,512]{1,0:T(8,128)S(1)}, u32[]{:S(2)}, u32[]{:S(2)}) collective-permute-start(f32[96,512]{1,0:T(8,128)S(1)} %add.105), channel_id=1, source_target_pairs={{0,7},{1,0},{2,1},{3,2},{4,3},{5,4},{6,5},{7,6},{8,15},{9,8},{10,9... | collective-permute-start | bytes 589832 | tf_op jit(solution)/shard_map/ppermute | solution.py:419
  21.5 0.9 collective-permute-start.4
  22.3 0.9 collective-permute-done
  23.3 0.3 collective-permute-start.1
  23.6 1.8 %collective-permute-done.14 = f32[96,512]{1,0:T(8,128)S(1)} collective-permute-done((f32[96,512]{1,0:T(8,128)S(1)}, f32[96,512]{1,0:T(8,128)S(1)}, u32[]{:S(2)}, u32[]{:S(2)}) %collective-permute-start.14) | collective-permute-done | bytes 196640 | tf_op jit(solution)/shard_map/ppermute | solution.py:419
  25.4 0.1 collective-permute-start.15
  25.5 1.3 collective-permute-done.18
  26.8 3.8 %collective-permute-start.19 = (f32[96,512]{1,0:T(8,128)S(1)}, f32[96,512]{1,0:T(8,128)S(1)}, u32[]{:S(2)}, u32[]{:S(2)}) collective-permute-start(f32[96,512]{1,0:T(8,128)S(1)} %add.106), channel_id=1, source_target_pairs={{0,7},{1,0},{2,1},{3,2},{4,3},{5,4},{6,5},{7,6},{8,15},{9,8},{10,9... | collective-permute-start | bytes 589832 | tf_op jit(solution)/shard_map/ppermute | solution.py:419
  30.6 0.0 collective-permute-done.4
  30.6 3.8 %collective-permute-start.5 = (f32[96,512]{1,0:T(8,128)S(1)}, f32[96,512]{1,0:T(8,128)S(1)}, u32[]{:S(2)}, u32[]{:S(2)}) collective-permute-start(f32[96,512]{1,0:T(8,128)S(1)} %add.99), channel_id=1, source_target_pairs={{0,7},{1,0},{2,1},{3,2},{4,3},{5,4},{6,5},{7,6},{8,15},{9,8},{10,9... | collective-permute-start | bytes 589832 | tf_op jit(solution)/shard_map/ppermute | solution.py:419
  34.4 0.1 collective-permute-start.2
  34.5 0.2 collective-permute-done.15
  34.7 0.1 collective-permute-start.16
  34.8 0.8 collective-permute-done.19
  35.7 3.8 %collective-permute-start.20 = (f32[96,512]{1,0:T(8,128)S(1)}, f32[96,512]{1,0:T(8,128)S(1)}, u32[]{:S(2)}, u32[]{:S(2)}) collective-permute-start(f32[96,512]{1,0:T(8,128)S(1)} %add.107), channel_id=1, source_target_pairs={{0,7},{1,0},{2,1},{3,2},{4,3},{5,4},{6,5},{7,6},{8,15},{9,8},{10,9... | collective-permute-start | bytes 589832 | tf_op jit(solution)/shard_map/ppermute | solution.py:419
  39.5 3.6 %collective-permute-start.6 = (f32[96,512]{1,0:T(8,128)S(1)}, f32[96,512]{1,0:T(8,128)S(1)}, u32[]{:S(2)}, u32[]{:S(2)}) collective-permute-start(f32[96,512]{1,0:T(8,128)S(1)} %add.100), channel_id=1, source_target_pairs={{0,7},{1,0},{2,1},{3,2},{4,3},{5,4},{6,5},{7,6},{8,15},{9,8},{10,9... | collective-permute-start | bytes 589832 | tf_op jit(solution)/shard_map/ppermute | solution.py:419
  43.1 0.1 collective-permute-start.3
  43.2 0.4 collective-permute-done.16
  43.6 0.8 collective-permute-done.20
  44.4 3.9 %collective-permute-start.21 = (f32[96,512]{1,0:T(8,128)S(1)}, f32[96,512]{1,0:T(8,128)S(1)}, u32[]{:S(2)}, u32[]{:S(2)}) collective-permute-start(f32[96,512]{1,0:T(8,128)S(1)} %add_add_fusion.refs_5_.refs_1_), channel_id=1, source_target_pairs={{0,7},{1,0},{2,1},{3,2},{4,3},{5,4},{6,5},{7,6},{8,15},{9,8},{10,9... | collective-permute-start | bytes 589832 | tf_op jit(solution)/shard_map/ppermute | solution.py:419
  48.4 2.4 %collective-permute-done.3 = f32[96,512]{1,0:T(8,128)S(1)} collective-permute-done((f32[96,512]{1,0:T(8,128)S(1)}, f32[96,512]{1,0:T(8,128)S(1)}, u32[]{:S(2)}, u32[]{:S(2)}) %collective-permute-start.3) | collective-permute-done | bytes 196640 | tf_op jit(solution)/shard_map/ppermute | solution.py:419
  50.8 0.1 collective-permute-start.10
  50.9 0.1 collective-permute-start.25
  51.0 3.2 %collective-permute-start.7 = (f32[96,512]{1,0:T(8,128)S(1)}, f32[96,512]{1,0:T(8,128)S(1)}, u32[]{:S(2)}, u32[]{:S(2)}) collective-permute-start(f32[96,512]{1,0:T(8,128)S(1)} %add_add_fusion.1.refs_0_), channel_id=1, source_target_pairs={{0,7},{1,0},{2,1},{3,2},{4,3},{5,4},{6,5},{7,6},{8,15},{9,8},{10,9... | collective-permute-start | bytes 589832 | tf_op jit(solution)/shard_map/ppermute | solution.py:419
  54.2 3.1 %collective-permute-start.22 = (f32[96,512]{1,0:T(8,128)S(1)}, f32[96,512]{1,0:T(8,128)S(1)}, u32[]{:S(2)}, u32[]{:S(2)}) collective-permute-start(f32[96,512]{1,0:T(8,128)S(1)} %collective-permute-done.21.refs_6_), channel_id=1, source_target_pairs={{0,7},{1,0},{2,1},{3,2},{4,3},{5,4},{6,5},{7,6},{8,15},{9,8},{10,9... | collective-permute-start | bytes 589832 | tf_op jit(solution)/shard_map/ppermute | solution.py:419
  57.3 2.4 %collective-permute-done.10.refs_4_ = f32[96,512]{1,0:T(8,128)S(1)} collective-permute-done((f32[96,512]{1,0:T(8,128)S(1)}, f32[96,512]{1,0:T(8,128)S(1)}, u32[]{:S(2)}, u32[]{:S(2)}) %collective-permute-start.10) | collective-permute-done | bytes 196640 | tf_op jit(solution)/shard_map/ppermute | solution.py:419
  59.8 4.2 %collective-permute-done.25.refs_9_ = f32[96,512]{1,0:T(8,128)S(1)} collective-permute-done((f32[96,512]{1,0:T(8,128)S(1)}, f32[96,512]{1,0:T(8,128)S(1)}, u32[]{:S(2)}, u32[]{:S(2)}) %collective-permute-start.25) | collective-permute-done | bytes 196640 | tf_op jit(solution)/shard_map/ppermute | solution.py:419
  64.0 3.2 %collective-permute-start.8 = (f32[96,512]{1,0:T(8,128)S(1)}, f32[96,512]{1,0:T(8,128)S(1)}, u32[]{:S(2)}, u32[]{:S(2)}) collective-permute-start(f32[96,512]{1,0:T(8,128)S(1)} %collective-permute-done.7.refs_1_), channel_id=1, source_target_pairs={{0,7},{1,0},{2,1},{3,2},{4,3},{5,4},{6,5},{7,6},{8,15},{9,8},{10,9... | collective-permute-start | bytes 589832 | tf_op jit(solution)/shard_map/ppermute | solution.py:419
  67.2 0.1 collective-permute-start.23
  67.3 1.4 %collective-permute-done.11.refs_3_ = f32[96,512]{1,0:T(8,128)S(1)} collective-permute-done((f32[96,512]{1,0:T(8,128)S(1)}, f32[96,512]{1,0:T(8,128)S(1)}, u32[]{:S(2)}, u32[]{:S(2)}) %collective-permute-start.11) | collective-permute-done | bytes 196640 | tf_op jit(solution)/shard_map/ppermute | solution.py:419
  68.7 0.5 collective-permute-start.12
  69.3 3.7 %collective-permute-done.26.refs_8_ = f32[96,512]{1,0:T(8,128)S(1)} collective-permute-done((f32[96,512]{1,0:T(8,128)S(1)}, f32[96,512]{1,0:T(8,128)S(1)}, u32[]{:S(2)}, u32[]{:S(2)}) %collective-permute-start.26) | collective-permute-done | bytes 196640 | tf_op jit(solution)/shard_map/ppermute | solution.py:419
  73.0 3.2 %collective-permute-start.9 = (f32[96,512]{1,0:T(8,128)S(1)}, f32[96,512]{1,0:T(8,128)S(1)}, u32[]{:S(2)}, u32[]{:S(2)}) collective-permute-start(f32[96,512]{1,0:T(8,128)S(1)} %collective-permute-done.8.refs_2_), channel_id=1, source_target_pairs={{0,7},{1,0},{2,1},{3,2},{4,3},{5,4},{6,5},{7,6},{8,15},{9,8},{10,9... | collective-permute-start | bytes 589832 | tf_op jit(solution)/shard_map/ppermute | solution.py:419
  76.2 3.1 %collective-permute-start.24 = (f32[96,512]{1,0:T(8,128)S(1)}, f32[96,512]{1,0:T(8,128)S(1)}, u32[]{:S(2)}, u32[]{:S(2)}) collective-permute-start(f32[96,512]{1,0:T(8,128)S(1)} %collective-permute-done.23.refs_3_), channel_id=1, source_target_pairs={{0,7},{1,0},{2,1},{3,2},{4,3},{5,4},{6,5},{7,6},{8,15},{9,8},{10,9... | collective-permute-start | bytes 589832 | tf_op jit(solution)/shard_map/ppermute | solution.py:419
  79.3 2.0 %lists.1 = (s32[96]{0:T(128)S(1)}, s32[96]{0:T(128)S(1)}, s32[2]{0:T(128)S(1)}) custom-call(s32[2,96]{1,0:T(2,128)} %bitcast.23, s32[1]{0:T(128)S(6)} %copy.5.live_ref, s32[1]{0:T(128)} %bitcast.1.index_ref), custom_call_target="tpu_custom_call" | custom-call | tf_op jit(solution)/shard_map/lists/pallas_call | solution.py:124
  81.3 2.9 %split_near.1 = (bf16[10,384,256]{2,1,0:T(8,128)(2,1)S(1)}, f32[192,192]{1,0:T(8,128)S(1)}) custom-call(f32[96,512]{1,0:T(8,128)S(1)} %add_add_fusion.1.refs_0_, f32[96,512]{1,0:T(8,128)S(1)} %collective-permute-done.7.refs_1_, f32[96,512]{1,0:T(8,128)S(1)} %collective-permute-done.8.refs_2_, f32[96,512]{1,0:T(8,128)S(1)} %collective-permute-done.11.refs_3_, ...), custom_call_target="tpu_custom_call" | custom-call | tf_op jit(solution)/shard_map/split_near/pallas_call | solution.py:207
  84.2 5.5 %adjoint_near.1.refs_0_ = f32[16,192,256]{2,1,0:T(8,128)S(1)} custom-call(s32[96]{0:T(128)S(1)} %get-tuple-element.50.list_ref, s32[2,96]{1,0:T(2,128)} %bitcast.24, s32[2]{0:T(128)S(1)} %get-tuple-element.47.count_ref, s32[1]{0:T(128)} %bitcast.1.index_ref, bf16[96,256,256]{2,1,0:T(8,128)(2,1)S(1)} %get-tuple-element.48.buf_ref, ...), custom_call_target="tpu_custom_call" | custom-call | tf_op jit(solution)/shard_map/adjoint_near/pallas_call | solution.py:282
  89.7 1.9 %split_far.1 = (bf16[6,384,256]{2,1,0:T(8,128)(2,1)S(1)}, f32[192,128]{1,0:T(8,128)S(1)}) custom-call(f32[96,512]{1,0:T(8,128)S(1)} %collective-permute-done.9.refs_0_, f32[96,512]{1,0:T(8,128)S(1)} %collective-permute-done.13.refs_1_, f32[96,512]{1,0:T(8,128)S(1)} %collective-permute-done.12.refs_2_, f32[96,512]{1,0:T(8,128)S(1)} %collective-permute-done.23.refs_3_, ...), custom_call_target="tpu_custom_call" | custom-call | tf_op jit(solution)/shard_map/split_far/pallas_call | solution.py:207
  91.6 4.4 %adjoint_far.1 = (f32[16,192,128]{2,1,0:T(8,128)S(1)}, f32[16,192,128]{2,1,0:T(8,128)S(1)}) custom-call(s32[96]{0:T(128)S(1)} %get-tuple-element.46.list_ref, s32[2,96]{1,0:T(2,128)} %bitcast.25, s32[2]{0:T(128)S(1)} %get-tuple-element.47.count_ref, s32[1]{0:T(128)} %bitcast.1.index_ref, bf16[96,256,256]{2,1,0:T(8,128)(2,1)S(1)} %get-tuple-element.48.buf_ref, ...), custom_call_target="tpu_custom_call" | custom-call | tf_op jit(solution)/shard_map/adjoint_far/pallas_call | solution.py:282
  96.0 0.3 collective-permute-start.35
  96.3 0.5 collective-permute-start.28
  96.8 3.0 %collective-permute-done.28 = f32[192,128]{1,0:T(8,128)S(1)} collective-permute-done((f32[192,128]{1,0:T(8,128)S(1)}, f32[192,128]{1,0:T(8,128)S(1)}, u32[]{:S(2)}, u32[]{:S(2)}) %collective-permute-start.28) | collective-permute-done | bytes 98336 | tf_op jit(solution)/shard_map/ppermute | solution.py:419
  99.9 3.6 %collective-permute-start.29 = (f32[192,128]{1,0:T(8,128)S(1)}, f32[192,128]{1,0:T(8,128)S(1)}, u32[]{:S(2)}, u32[]{:S(2)}) collective-permute-start(f32[192,128]{1,0:T(8,128)S(1)} %add.110), channel_id=1, source_target_pairs={{0,128},{8,40},{16,144},{24,56},{32,160},{40,8},{48,176},{56,24},{... | collective-permute-start | bytes 294920 | tf_op jit(solution)/shard_map/ppermute | solution.py:462
  103.5 0.2 add.117
  103.7 0.1 fusion.5
  103.7 0.1 collective-permute-start.36
  103.8 0.1 collective-permute-start.37
  103.9 2.0 %collective-permute-start.38 = (f32[4,192,128]{2,1,0:T(8,128)S(1)}, f32[4,192,128]{2,1,0:T(8,128)S(1)}, u32[]{:S(2)}, u32[]{:S(2)}) collective-permute-start(f32[4,192,128]{2,1,0:T(8,128)S(1)} %get-tuple-element.55), channel_id=1, source_target_pairs={{0,192},{8,56},{16,208},{24,8},{32,224},{40,24},{48,240},{56,40},{... | collective-permute-start | bytes 1179656 | tf_op jit(solution)/shard_map/ppermute | solution.py:462
  105.9 2.0 %collective-permute-start.30 = (f32[192,128]{1,0:T(8,128)S(1)}, f32[192,128]{1,0:T(8,128)S(1)}, u32[]{:S(2)}, u32[]{:S(2)}) collective-permute-start(f32[192,128]{1,0:T(8,128)S(1)} %add.110), channel_id=1, source_target_pairs={{0,64},{8,24},{16,80},{24,40},{32,96},{40,56},{48,112},{56,8},{64,... | collective-permute-start | bytes 294920 | tf_op jit(solution)/shard_map/ppermute | solution.py:462
  107.9 0.6 collective-permute-start.31
  108.5 7.6 %collective-permute-done.30 = f32[192,128]{1,0:T(8,128)S(1)} collective-permute-done((f32[192,128]{1,0:T(8,128)S(1)}, f32[192,128]{1,0:T(8,128)S(1)}, u32[]{:S(2)}, u32[]{:S(2)}) %collective-permute-start.30) | collective-permute-done | bytes 98336 | tf_op jit(solution)/shard_map/ppermute | solution.py:462
  116.2 2.2 %collective-permute-done.31 = f32[192,128]{1,0:T(8,128)S(1)} collective-permute-done((f32[192,128]{1,0:T(8,128)S(1)}, f32[192,128]{1,0:T(8,128)S(1)}, u32[]{:S(2)}, u32[]{:S(2)}) %collective-permute-start.31) | collective-permute-done | bytes 98336 | tf_op jit(solution)/shard_map/ppermute | solution.py:462
  118.4 3.0 %collective-permute-start.32 = (f32[192,128]{1,0:T(8,128)S(1)}, f32[192,128]{1,0:T(8,128)S(1)}, u32[]{:S(2)}, u32[]{:S(2)}) collective-permute-start(f32[192,128]{1,0:T(8,128)S(1)} %add_add_fusion.3), channel_id=1, source_target_pairs={{0,32},{8,136},{16,48},{24,152},{32,0},{40,168},{48,16},{56,184},{... | collective-permute-start | bytes 294920 | tf_op jit(solution)/shard_map/ppermute | solution.py:462
  121.4 3.2 %collective-permute-start.34 = (f32[192,128]{1,0:T(8,128)S(1)}, f32[192,128]{1,0:T(8,128)S(1)}, u32[]{:S(2)}, u32[]{:S(2)}) collective-permute-start(f32[192,128]{1,0:T(8,128)S(1)} %add_add_fusion.3), channel_id=1, source_target_pairs={{0,48},{8,200},{16,0},{24,216},{32,16},{40,232},{48,32},{56,248},{... | collective-permute-start | bytes 294920 | tf_op jit(solution)/shard_map/ppermute | solution.py:462
  124.6 0.1 fusion.1
  124.7 0.1 collective-permute-start.39
  124.8 0.9 collective-permute-start.40
  125.7 2.5 %collective-permute-start.41 = (f32[192,128]{1,0:T(8,128)S(1)}, f32[192,128]{1,0:T(8,128)S(1)}, u32[]{:S(2)}, u32[]{:S(2)}) collective-permute-start(f32[192,128]{1,0:T(8,128)S(1)} %get-tuple-element.58), channel_id=1, source_target_pairs={{0,48},{8,200},{16,0},{24,216},{32,16},{40,232},{48,32},{56,248},{... | collective-permute-start | bytes 294920 | tf_op jit(solution)/shard_map/ppermute | solution.py:462
  128.2 8.6 %factor.1.factor_ref = f32[192,192]{1,0:T(8,128)S(1)} custom-call(f32[192,128]{1,0:T(8,128)S(1)} %add_add_fusion.2.packed_ref), custom_call_target="tpu_custom_call" | custom-call | tf_op jit(solution)/shard_map/factor/pallas_call | solution.py:387
  136.8 1.2 shard_map.50
  138.0 1.0 shard_map.51
  (49 shorter events, 0.5 us)
Async XLA Ops:
  9.6 8.1 %collective-permute-start.17 = (f32[96,512]{1,0:T(8,128)S(1)}, f32[96,512]{1,0:T(8,128)S(1)}, u32[]{:S(2)}, u32[]{:S(2)}) collective-permute-start(f32[96,512]{1,0:T(8,128)S(1)} %get-tuple-element.39), channel_id=1, source_target_pairs={{0,7},{1,0},{2,1},{3,2},{4,3},{5,4},{6,5},{7,6},{8,15},{9,8},{10,9... | collective-permute-start | bytes 589832 | tf_op jit(solution)/shard_map/ppermute | solution.py:419
  14.5 8.8 %collective-permute-start = (f32[96,512]{1,0:T(8,128)S(1)}, f32[96,512]{1,0:T(8,128)S(1)}, u32[]{:S(2)}, u32[]{:S(2)}) collective-permute-start(f32[96,512]{1,0:T(8,128)S(1)} %get-tuple-element.28), channel_id=1, source_target_pairs={{0,1},{1,2},{2,3},{3,4},{4,5},{5,6},{6,7},{7,0},{8,9},{9,10},{10,1... | collective-permute-start | bytes 589832 | tf_op jit(solution)/shard_map/ppermute | solution.py:419
  14.5 10.9 %collective-permute-start.14 = (f32[96,512]{1,0:T(8,128)S(1)}, f32[96,512]{1,0:T(8,128)S(1)}, u32[]{:S(2)}, u32[]{:S(2)}) collective-permute-start(f32[96,512]{1,0:T(8,128)S(1)} %get-tuple-element.36), channel_id=1, source_target_pairs={{0,1},{1,2},{2,3},{3,4},{4,5},{5,6},{6,7},{7,0},{8,9},{9,10},{10,1... | collective-permute-start | bytes 589832 | tf_op jit(solution)/shard_map/ppermute | solution.py:419
  17.7 9.1 %collective-permute-start.18 = (f32[96,512]{1,0:T(8,128)S(1)}, f32[96,512]{1,0:T(8,128)S(1)}, u32[]{:S(2)}, u32[]{:S(2)}) collective-permute-start(f32[96,512]{1,0:T(8,128)S(1)} %add.105), channel_id=1, source_target_pairs={{0,7},{1,0},{2,1},{3,2},{4,3},{5,4},{6,5},{7,6},{8,15},{9,8},{10,9... | collective-permute-start | bytes 589832 | tf_op jit(solution)/shard_map/ppermute | solution.py:419
  21.5 9.1 %collective-permute-start.4 = (f32[96,512]{1,0:T(8,128)S(1)}, f32[96,512]{1,0:T(8,128)S(1)}, u32[]{:S(2)}, u32[]{:S(2)}) collective-permute-start(f32[96,512]{1,0:T(8,128)S(1)} %get-tuple-element.32), channel_id=1, source_target_pairs={{0,7},{1,0},{2,1},{3,2},{4,3},{5,4},{6,5},{7,6},{8,15},{9,8},{10,9... | collective-permute-start | bytes 589832 | tf_op jit(solution)/shard_map/ppermute | solution.py:419
  23.3 11.1 %collective-permute-start.1 = (f32[96,512]{1,0:T(8,128)S(1)}, f32[96,512]{1,0:T(8,128)S(1)}, u32[]{:S(2)}, u32[]{:S(2)}) collective-permute-start(f32[96,512]{1,0:T(8,128)S(1)} %add.96), channel_id=1, source_target_pairs={{0,1},{1,2},{2,3},{3,4},{4,5},{5,6},{6,7},{7,0},{8,9},{9,10},{10,1... | collective-permute-start | bytes 589832 | tf_op jit(solution)/shard_map/ppermute | solution.py:419
  25.4 9.3 %collective-permute-start.15 = (f32[96,512]{1,0:T(8,128)S(1)}, f32[96,512]{1,0:T(8,128)S(1)}, u32[]{:S(2)}, u32[]{:S(2)}) collective-permute-start(f32[96,512]{1,0:T(8,128)S(1)} %add.103), channel_id=1, source_target_pairs={{0,1},{1,2},{2,3},{3,4},{4,5},{5,6},{6,7},{7,0},{8,9},{9,10},{10,1... | collective-permute-start | bytes 589832 | tf_op jit(solution)/shard_map/ppermute | solution.py:419
  26.8 8.9 %collective-permute-start.19 = (f32[96,512]{1,0:T(8,128)S(1)}, f32[96,512]{1,0:T(8,128)S(1)}, u32[]{:S(2)}, u32[]{:S(2)}) collective-permute-start(f32[96,512]{1,0:T(8,128)S(1)} %add.106), channel_id=1, source_target_pairs={{0,7},{1,0},{2,1},{3,2},{4,3},{5,4},{6,5},{7,6},{8,15},{9,8},{10,9... | collective-permute-start | bytes 589832 | tf_op jit(solution)/shard_map/ppermute | solution.py:419
  30.6 8.8 %collective-permute-start.5 = (f32[96,512]{1,0:T(8,128)S(1)}, f32[96,512]{1,0:T(8,128)S(1)}, u32[]{:S(2)}, u32[]{:S(2)}) collective-permute-start(f32[96,512]{1,0:T(8,128)S(1)} %add.99), channel_id=1, source_target_pairs={{0,7},{1,0},{2,1},{3,2},{4,3},{5,4},{6,5},{7,6},{8,15},{9,8},{10,9... | collective-permute-start | bytes 589832 | tf_op jit(solution)/shard_map/ppermute | solution.py:419
  34.4 8.7 %collective-permute-start.2 = (f32[96,512]{1,0:T(8,128)S(1)}, f32[96,512]{1,0:T(8,128)S(1)}, u32[]{:S(2)}, u32[]{:S(2)}) collective-permute-start(f32[96,512]{1,0:T(8,128)S(1)} %add.97), channel_id=1, source_target_pairs={{0,1},{1,2},{2,3},{3,4},{4,5},{5,6},{6,7},{7,0},{8,9},{9,10},{10,1... | collective-permute-start | bytes 589832 | tf_op jit(solution)/shard_map/ppermute | solution.py:419
  34.7 8.8 %collective-permute-start.16 = (f32[96,512]{1,0:T(8,128)S(1)}, f32[96,512]{1,0:T(8,128)S(1)}, u32[]{:S(2)}, u32[]{:S(2)}) collective-permute-start(f32[96,512]{1,0:T(8,128)S(1)} %add.104), channel_id=1, source_target_pairs={{0,1},{1,2},{2,3},{3,4},{4,5},{5,6},{6,7},{7,0},{8,9},{9,10},{10,1... | collective-permute-start | bytes 589832 | tf_op jit(solution)/shard_map/ppermute | solution.py:419
  35.7 8.7 %collective-permute-start.20 = (f32[96,512]{1,0:T(8,128)S(1)}, f32[96,512]{1,0:T(8,128)S(1)}, u32[]{:S(2)}, u32[]{:S(2)}) collective-permute-start(f32[96,512]{1,0:T(8,128)S(1)} %add.107), channel_id=1, source_target_pairs={{0,7},{1,0},{2,1},{3,2},{4,3},{5,4},{6,5},{7,6},{8,15},{9,8},{10,9... | collective-permute-start | bytes 589832 | tf_op jit(solution)/shard_map/ppermute | solution.py:419
  39.5 8.9 %collective-permute-start.6 = (f32[96,512]{1,0:T(8,128)S(1)}, f32[96,512]{1,0:T(8,128)S(1)}, u32[]{:S(2)}, u32[]{:S(2)}) collective-permute-start(f32[96,512]{1,0:T(8,128)S(1)} %add.100), channel_id=1, source_target_pairs={{0,7},{1,0},{2,1},{3,2},{4,3},{5,4},{6,5},{7,6},{8,15},{9,8},{10,9... | collective-permute-start | bytes 589832 | tf_op jit(solution)/shard_map/ppermute | solution.py:419
  43.1 7.7 %collective-permute-start.3 = (f32[96,512]{1,0:T(8,128)S(1)}, f32[96,512]{1,0:T(8,128)S(1)}, u32[]{:S(2)}, u32[]{:S(2)}) collective-permute-start(f32[96,512]{1,0:T(8,128)S(1)} %add.98), channel_id=1, source_target_pairs={{0,1},{1,2},{2,3},{3,4},{4,5},{5,6},{6,7},{7,0},{8,9},{9,10},{10,1... | collective-permute-start | bytes 589832 | tf_op jit(solution)/shard_map/ppermute | solution.py:419
  44.4 9.8 %collective-permute-start.21 = (f32[96,512]{1,0:T(8,128)S(1)}, f32[96,512]{1,0:T(8,128)S(1)}, u32[]{:S(2)}, u32[]{:S(2)}) collective-permute-start(f32[96,512]{1,0:T(8,128)S(1)} %add_add_fusion.refs_5_.refs_1_), channel_id=1, source_target_pairs={{0,7},{1,0},{2,1},{3,2},{4,3},{5,4},{6,5},{7,6},{8,15},{9,8},{10,9... | collective-permute-start | bytes 589832 | tf_op jit(solution)/shard_map/ppermute | solution.py:419
  50.8 8.9 %collective-permute-start.10 = (f32[96,512]{1,0:T(8,128)S(1)}, f32[96,512]{1,0:T(8,128)S(1)}, u32[]{:S(2)}, u32[]{:S(2)}) collective-permute-start(f32[96,512]{1,0:T(8,128)S(1)} %add_add_fusion.1.refs_0_), channel_id=1, source_target_pairs={{0,1},{1,2},{2,3},{3,4},{4,5},{5,6},{6,7},{7,0},{8,9},{9,10},{10,1... | collective-permute-start | bytes 589832 | tf_op jit(solution)/shard_map/ppermute | solution.py:419
  50.9 13.1 %collective-permute-start.25 = (f32[96,512]{1,0:T(8,128)S(1)}, f32[96,512]{1,0:T(8,128)S(1)}, u32[]{:S(2)}, u32[]{:S(2)}) collective-permute-start(f32[96,512]{1,0:T(8,128)S(1)} %add_add_fusion.refs_5_.refs_1_), channel_id=1, source_target_pairs={{0,1},{1,2},{2,3},{3,4},{4,5},{5,6},{6,7},{7,0},{8,9},{9,10},{10,1... | collective-permute-start | bytes 589832 | tf_op jit(solution)/shard_map/ppermute | solution.py:419
  51.0 13.0 %collective-permute-start.7 = (f32[96,512]{1,0:T(8,128)S(1)}, f32[96,512]{1,0:T(8,128)S(1)}, u32[]{:S(2)}, u32[]{:S(2)}) collective-permute-start(f32[96,512]{1,0:T(8,128)S(1)} %add_add_fusion.1.refs_0_), channel_id=1, source_target_pairs={{0,7},{1,0},{2,1},{3,2},{4,3},{5,4},{6,5},{7,6},{8,15},{9,8},{10,9... | collective-permute-start | bytes 589832 | tf_op jit(solution)/shard_map/ppermute | solution.py:419
  54.2 13.0 %collective-permute-start.22 = (f32[96,512]{1,0:T(8,128)S(1)}, f32[96,512]{1,0:T(8,128)S(1)}, u32[]{:S(2)}, u32[]{:S(2)}) collective-permute-start(f32[96,512]{1,0:T(8,128)S(1)} %collective-permute-done.21.refs_6_), channel_id=1, source_target_pairs={{0,7},{1,0},{2,1},{3,2},{4,3},{5,4},{6,5},{7,6},{8,15},{9,8},{10,9... | collective-permute-start | bytes 589832 | tf_op jit(solution)/shard_map/ppermute | solution.py:419
  59.8 8.9 %collective-permute-start.11 = (f32[96,512]{1,0:T(8,128)S(1)}, f32[96,512]{1,0:T(8,128)S(1)}, u32[]{:S(2)}, u32[]{:S(2)}) collective-permute-start(f32[96,512]{1,0:T(8,128)S(1)} %collective-permute-done.10.refs_4_), channel_id=1, source_target_pairs={{0,1},{1,2},{2,3},{3,4},{4,5},{5,6},{6,7},{7,0},{8,9},{9,10},{10,1... | collective-permute-start | bytes 589832 | tf_op jit(solution)/shard_map/ppermute | solution.py:419
  64.0 9.0 %collective-permute-start.26 = (f32[96,512]{1,0:T(8,128)S(1)}, f32[96,512]{1,0:T(8,128)S(1)}, u32[]{:S(2)}, u32[]{:S(2)}) collective-permute-start(f32[96,512]{1,0:T(8,128)S(1)} %collective-permute-done.25.refs_9_), channel_id=1, source_target_pairs={{0,1},{1,2},{2,3},{3,4},{4,5},{5,6},{6,7},{7,0},{8,9},{9,10},{10,1... | collective-permute-start | bytes 589832 | tf_op jit(solution)/shard_map/ppermute | solution.py:419
  64.0 9.0 %collective-permute-start.8 = (f32[96,512]{1,0:T(8,128)S(1)}, f32[96,512]{1,0:T(8,128)S(1)}, u32[]{:S(2)}, u32[]{:S(2)}) collective-permute-start(f32[96,512]{1,0:T(8,128)S(1)} %collective-permute-done.7.refs_1_), channel_id=1, source_target_pairs={{0,7},{1,0},{2,1},{3,2},{4,3},{5,4},{6,5},{7,6},{8,15},{9,8},{10,9... | collective-permute-start | bytes 589832 | tf_op jit(solution)/shard_map/ppermute | solution.py:419
  67.2 9.0 %collective-permute-start.23 = (f32[96,512]{1,0:T(8,128)S(1)}, f32[96,512]{1,0:T(8,128)S(1)}, u32[]{:S(2)}, u32[]{:S(2)}) collective-permute-start(f32[96,512]{1,0:T(8,128)S(1)} %collective-permute-done.22.refs_7_), channel_id=1, source_target_pairs={{0,7},{1,0},{2,1},{3,2},{4,3},{5,4},{6,5},{7,6},{8,15},{9,8},{10,9... | collective-permute-start | bytes 589832 | tf_op jit(solution)/shard_map/ppermute | solution.py:419
  68.7 10.6 %collective-permute-start.12 = (f32[96,512]{1,0:T(8,128)S(1)}, f32[96,512]{1,0:T(8,128)S(1)}, u32[]{:S(2)}, u32[]{:S(2)}) collective-permute-start(f32[96,512]{1,0:T(8,128)S(1)} %collective-permute-done.11.refs_3_), channel_id=1, source_target_pairs={{0,1},{1,2},{2,3},{3,4},{4,5},{5,6},{6,7},{7,0},{8,9},{9,10},{10,1... | collective-permute-start | bytes 589832 | tf_op jit(solution)/shard_map/ppermute | solution.py:419
  73.0 16.7 %collective-permute-start.27 = (f32[96,512]{1,0:T(8,128)S(1)}, f32[96,512]{1,0:T(8,128)S(1)}, u32[]{:S(2)}, u32[]{:S(2)}) collective-permute-start(f32[96,512]{1,0:T(8,128)S(1)} %collective-permute-done.26.refs_8_), channel_id=1, source_target_pairs={{0,1},{1,2},{2,3},{3,4},{4,5},{5,6},{6,7},{7,0},{8,9},{9,10},{10,1... | collective-permute-start | bytes 589832 | tf_op jit(solution)/shard_map/ppermute | solution.py:419
  73.0 16.7 %collective-permute-start.9 = (f32[96,512]{1,0:T(8,128)S(1)}, f32[96,512]{1,0:T(8,128)S(1)}, u32[]{:S(2)}, u32[]{:S(2)}) collective-permute-start(f32[96,512]{1,0:T(8,128)S(1)} %collective-permute-done.8.refs_2_), channel_id=1, source_target_pairs={{0,7},{1,0},{2,1},{3,2},{4,3},{5,4},{6,5},{7,6},{8,15},{9,8},{10,9... | collective-permute-start | bytes 589832 | tf_op jit(solution)/shard_map/ppermute | solution.py:419
  76.2 13.5 %collective-permute-start.24 = (f32[96,512]{1,0:T(8,128)S(1)}, f32[96,512]{1,0:T(8,128)S(1)}, u32[]{:S(2)}, u32[]{:S(2)}) collective-permute-start(f32[96,512]{1,0:T(8,128)S(1)} %collective-permute-done.23.refs_3_), channel_id=1, source_target_pairs={{0,7},{1,0},{2,1},{3,2},{4,3},{5,4},{6,5},{7,6},{8,15},{9,8},{10,9... | collective-permute-start | bytes 589832 | tf_op jit(solution)/shard_map/ppermute | solution.py:419
  79.3 10.4 %collective-permute-start.13 = (f32[96,512]{1,0:T(8,128)S(1)}, f32[96,512]{1,0:T(8,128)S(1)}, u32[]{:S(2)}, u32[]{:S(2)}) collective-permute-start(f32[96,512]{1,0:T(8,128)S(1)} %collective-permute-done.12.refs_2_), channel_id=1, source_target_pairs={{0,1},{1,2},{2,3},{3,4},{4,5},{5,6},{6,7},{7,0},{8,9},{9,10},{10,1... | collective-permute-start | bytes 589832 | tf_op jit(solution)/shard_map/ppermute | solution.py:419
  96.0 7.5 %collective-permute-start.35 = (f32[16,192,128]{2,1,0:T(8,128)S(1)}, f32[16,192,128]{2,1,0:T(8,128)S(1)}, u32[]{:S(2)}, u32[]{:S(2)}) collective-permute-start(f32[16,192,128]{2,1,0:T(8,128)S(1)} %get-tuple-element.53), channel_id=1, source_target_pairs={{0,8},{8,0},{1,9},{9,1},{2,10},{10,2},{3,11},{11,3},{4,12},{12,4},... | collective-permute-start | bytes 4718600 | tf_op jit(solution)/shard_map/ppermute | solution.py:419
  96.3 3.5 %collective-permute-start.28 = (f32[192,128]{1,0:T(8,128)S(1)}, f32[192,128]{1,0:T(8,128)S(1)}, u32[]{:S(2)}, u32[]{:S(2)}) collective-permute-start(f32[192,128]{1,0:T(8,128)S(1)} %get-tuple-element.45), channel_id=1, source_target_pairs={{0,8},{8,0},{1,9},{9,1},{2,10},{10,2},{3,11},{11,3},{4,12},{12,4},... | collective-permute-start | bytes 294920 | tf_op jit(solution)/shard_map/ppermute | solution.py:419
  99.9 8.1 %collective-permute-start.29 = (f32[192,128]{1,0:T(8,128)S(1)}, f32[192,128]{1,0:T(8,128)S(1)}, u32[]{:S(2)}, u32[]{:S(2)}) collective-permute-start(f32[192,128]{1,0:T(8,128)S(1)} %add.110), channel_id=1, source_target_pairs={{0,128},{8,40},{16,144},{24,56},{32,160},{40,8},{48,176},{56,24},{... | collective-permute-start | bytes 294920 | tf_op jit(solution)/shard_map/ppermute | solution.py:462
  103.7 17.7 %collective-permute-start.36 = (f32[4,192,128]{2,1,0:T(8,128)S(1)}, f32[4,192,128]{2,1,0:T(8,128)S(1)}, u32[]{:S(2)}, u32[]{:S(2)}) collective-permute-start(f32[4,192,128]{2,1,0:T(8,128)S(1)} %get-tuple-element.54), channel_id=1, source_target_pairs={{0,128},{8,40},{16,144},{24,56},{32,160},{40,8},{48,176},{56,24},{... | collective-permute-start | bytes 1179656 | tf_op jit(solution)/shard_map/ppermute | solution.py:462
  103.8 20.8 %collective-permute-start.37 = (f32[4,192,128]{2,1,0:T(8,128)S(1)}, f32[4,192,128]{2,1,0:T(8,128)S(1)}, u32[]{:S(2)}, u32[]{:S(2)}) collective-permute-start(f32[4,192,128]{2,1,0:T(8,128)S(1)} %get-tuple-element.56), channel_id=1, source_target_pairs={{0,64},{8,24},{16,80},{24,40},{32,96},{40,56},{48,112},{56,8},{64,... | collective-permute-start | bytes 1179656 | tf_op jit(solution)/shard_map/ppermute | solution.py:462
  103.9 20.7 %collective-permute-start.38 = (f32[4,192,128]{2,1,0:T(8,128)S(1)}, f32[4,192,128]{2,1,0:T(8,128)S(1)}, u32[]{:S(2)}, u32[]{:S(2)}) collective-permute-start(f32[4,192,128]{2,1,0:T(8,128)S(1)} %get-tuple-element.55), channel_id=1, source_target_pairs={{0,192},{8,56},{16,208},{24,8},{32,224},{40,24},{48,240},{56,40},{... | collective-permute-start | bytes 1179656 | tf_op jit(solution)/shard_map/ppermute | solution.py:462
  105.9 10.2 %collective-permute-start.30 = (f32[192,128]{1,0:T(8,128)S(1)}, f32[192,128]{1,0:T(8,128)S(1)}, u32[]{:S(2)}, u32[]{:S(2)}) collective-permute-start(f32[192,128]{1,0:T(8,128)S(1)} %add.110), channel_id=1, source_target_pairs={{0,64},{8,24},{16,80},{24,40},{32,96},{40,56},{48,112},{56,8},{64,... | collective-permute-start | bytes 294920 | tf_op jit(solution)/shard_map/ppermute | solution.py:462
  107.9 10.4 %collective-permute-start.31 = (f32[192,128]{1,0:T(8,128)S(1)}, f32[192,128]{1,0:T(8,128)S(1)}, u32[]{:S(2)}, u32[]{:S(2)}) collective-permute-start(f32[192,128]{1,0:T(8,128)S(1)} %add.110), channel_id=1, source_target_pairs={{0,192},{8,56},{16,208},{24,8},{32,224},{40,24},{48,240},{56,40},{... | collective-permute-start | bytes 294920 | tf_op jit(solution)/shard_map/ppermute | solution.py:462
  118.4 7.3 %collective-permute-start.32 = (f32[192,128]{1,0:T(8,128)S(1)}, f32[192,128]{1,0:T(8,128)S(1)}, u32[]{:S(2)}, u32[]{:S(2)}) collective-permute-start(f32[192,128]{1,0:T(8,128)S(1)} %add_add_fusion.3), channel_id=1, source_target_pairs={{0,32},{8,136},{16,48},{24,152},{32,0},{40,168},{48,16},{56,184},{... | collective-permute-start | bytes 294920 | tf_op jit(solution)/shard_map/ppermute | solution.py:462
  121.4 6.8 %collective-permute-start.33 = (f32[192,128]{1,0:T(8,128)S(1)}, f32[192,128]{1,0:T(8,128)S(1)}, u32[]{:S(2)}, u32[]{:S(2)}) collective-permute-start(f32[192,128]{1,0:T(8,128)S(1)} %add_add_fusion.3), channel_id=1, source_target_pairs={{0,16},{8,72},{16,32},{24,88},{32,48},{40,104},{48,0},{56,120},{64... | collective-permute-start | bytes 294920 | tf_op jit(solution)/shard_map/ppermute | solution.py:462
  121.4 6.8 %collective-permute-start.34 = (f32[192,128]{1,0:T(8,128)S(1)}, f32[192,128]{1,0:T(8,128)S(1)}, u32[]{:S(2)}, u32[]{:S(2)}) collective-permute-start(f32[192,128]{1,0:T(8,128)S(1)} %add_add_fusion.3), channel_id=1, source_target_pairs={{0,48},{8,200},{16,0},{24,216},{32,16},{40,232},{48,32},{56,248},{... | collective-permute-start | bytes 294920 | tf_op jit(solution)/shard_map/ppermute | solution.py:462
  124.7 13.3 %collective-permute-start.39 = (f32[192,128]{1,0:T(8,128)S(1)}, f32[192,128]{1,0:T(8,128)S(1)}, u32[]{:S(2)}, u32[]{:S(2)}) collective-permute-start(f32[192,128]{1,0:T(8,128)S(1)} %get-tuple-element.57), channel_id=1, source_target_pairs={{0,32},{8,136},{16,48},{24,152},{32,0},{40,168},{48,16},{56,184},{... | collective-permute-start | bytes 294920 | tf_op jit(solution)/shard_map/ppermute | solution.py:462
  124.8 13.2 %collective-permute-start.40 = (f32[192,128]{1,0:T(8,128)S(1)}, f32[192,128]{1,0:T(8,128)S(1)}, u32[]{:S(2)}, u32[]{:S(2)}) collective-permute-start(f32[192,128]{1,0:T(8,128)S(1)} %get-tuple-element.59), channel_id=1, source_target_pairs={{0,16},{8,72},{16,32},{24,88},{32,48},{40,104},{48,0},{56,120},{64... | collective-permute-start | bytes 294920 | tf_op jit(solution)/shard_map/ppermute | solution.py:462
  125.7 12.3 %collective-permute-start.41 = (f32[192,128]{1,0:T(8,128)S(1)}, f32[192,128]{1,0:T(8,128)S(1)}, u32[]{:S(2)}, u32[]{:S(2)}) collective-permute-start(f32[192,128]{1,0:T(8,128)S(1)} %get-tuple-element.58), channel_id=1, source_target_pairs={{0,48},{8,200},{16,0},{24,216},{32,16},{40,232},{48,32},{56,248},{... | collective-permute-start | bytes 294920 | tf_op jit(solution)/shard_map/ppermute | solution.py:462
